TPU v7x, 32 devices: a whole 2x2x4 slice. The times are simulated.
32 devices in a mesh: group: 2 (over y), sky: 4 (over z), visit: 2 (over x), band: 2 (over core).
Axes of the slice: x: 2, y: 2, z: 4, core: 2. Of those that a mesh axis runs over, the one named last changes fastest.
Arguments:
- raw_tiles: bfloat16 [16, 32, 128, 128], P(('group', 'visit', 'band'), 'sky'), parts along dimension 0, may hold values from -6 to 6
- pixel_offsets: int32 [16, 32, 2], P(('group', 'visit', 'band'), 'sky'), parts along dimension 0, may hold values from -1 to 1
- shift_entry_index: int32 [16, 32], P(('group', 'visit', 'band'), 'sky'), parts along dimension 0, may hold values from 0 to 15
- shift_table: float32 [16, 2], replicated, may hold values from 0 to 1
- tile_routes: int32 [16, 32], P(('group', 'visit', 'band'), 'sky'), parts along dimension 0, may hold values from 0 to 31, as said below
- bad_pixels: int32 [16, 32, 32], P('group', 'sky'), parts along dimension 0, may hold values from 0 to 16383, as said below
- basis_kernels: bfloat16 [4, 33, 33], replicated, may hold values from -0.5 to 0.5
- basis_choice: int32 [16, 32], P(('group', 'visit', 'band'), 'sky'), parts along dimension 0, may hold values from 0 to 15
- coef_table: float32 [16, 4], replicated, may hold values from -4 to 4
Outputs:
- difference: bfloat16 [16, 512, 1024], P(('group', 'visit', 'band'), 'sky'), parts along dimension 0
There are 2 independent parts, one for each index of `group`. A program takes and returns all parts, laid end to end along the dimension named above; an argument that names none is the same for every part. Nothing has to cross between parts.
Inputs may be any that keep to these rules, and one draw needn't show every extreme that they name: `tile_routes`: for every visit, each of the 32 slab tiles is named by exactly one source tile. Within each aligned block of 2 visits, the source tiles i with one value of i // 8 name at most 5 slab tiles t with one value of t // 8, and exactly 5 for some value. `bad_pixels`: an entry names the pixel at row r and column c of the slab tile as r * 128 + c. For one slab tile, the entries of all visits together are distinct.
All inputs are finite; a program needn't handle non-finite values.
Results may differ from a plain program's by a relative error of at most 0.018.
Values may be sent and summed in bfloat16 or wider, within the bound.
No kernel may reach another device: no remote copies, remote signals or barrier semaphores. Data moves between devices by JAX's collectives and lax.ppermute only.
A program may use at most 128 MiB of HBM per device.

v0:
```python
import functools
import itertools
import math

import jax
import jax.numpy as jnp
from jax import lax
from jax.experimental import pallas as pl
from jax.experimental.pallas import tpu as pltpu
from jax.sharding import PartitionSpec as P


BF = jnp.bfloat16
F32 = jnp.float32
I32 = jnp.int32
VMEM = pl.BlockSpec(memory_space=pltpu.VMEM)
SMEM = pl.BlockSpec(memory_space=pltpu.SMEM)
HBM = pl.BlockSpec(memory_space=pltpu.HBM)
LABELS = 8


def kernel_call(body, outs, in_specs, scratch=(), flops=0, data=0, out_specs=None):
    def call(*args):
        held = [*args, *jax.tree.leaves(outs), *(s for s in scratch if len(s.shape) > 1)]
        places = out_specs or jax.tree.map(lambda _: VMEM, outs)
        room = sum(math.prod(a.shape) * jnp.dtype(a.dtype).itemsize for a in held)
        return pl.pallas_call(
            body,
            out_shape=outs,
            in_specs=in_specs,
            out_specs=places,
            scratch_shapes=list(scratch),
            cost_estimate=pl.CostEstimate(flops=flops, bytes_accessed=data, transcendentals=0),
            compiler_params=pltpu.CompilerParams(vmem_limit_bytes=room + room // 4 + (4 << 20)),
        )(*args)

    return call


def sinc(x):
    angle = x * jnp.float32(jnp.pi)
    safe = jnp.where(x == 0.0, 1.0, angle)
    return jnp.where(x == 0.0, 1.0, jnp.sin(safe) / safe)


def iota(shape, dim):
    return lax.broadcasted_iota(I32, shape, dim)


def warp_body(patches, visits, cap, *refs):
    sources, parcels, held = refs[:5], refs[5:-9], refs[-9:]
    routes, offsets, entries, table, raw, small, large, seats, labels = held[:9]
    copies = [
        pltpu.make_async_copy(source, target, small.at[n])
        for n, (source, target) in enumerate(zip(sources[:4], held[:4]))
    ]
    groups = large.shape[0]
    per_group = raw.shape[1] // groups
    loads = [
        pltpu.make_async_copy(
            sources[4].at[:, g * per_group : (g + 1) * per_group],
            raw.at[:, g * per_group : (g + 1) * per_group],
            large.at[g],
        )
        for g in range(groups)
    ]
    for copy in copies + loads:
        copy.start()
    visit_count, tile_cols, side, _ = raw.shape
    tiles = visit_count * tile_cols
    part = side // visits
    sky, visit = lax.axis_index("sky"), lax.axis_index("visit")
    for copy in copies:
        copy.wait()
    row = iota((2 * tiles, side), 0)
    shift = jnp.zeros((2 * tiles, side), F32)
    for n in range(tiles):
        v, i = divmod(n, tile_cols)
        entry = entries[v, i]
        for axis in range(2):
            amount = offsets[v, axis, i].astype(F32) + table[axis, entry]
            shift = jnp.where(row == 2 * n + axis, amount, shift)
    lane = iota((2 * tiles, side), 1)
    step = jnp.where(lane < side // 2, lane, lane - side)
    x = jnp.where(row % 2 == 0, -step, step).astype(F32) - shift
    taps = jnp.where(jnp.abs(x) < 3.0, sinc(x) * sinc(x / 3.0), 0.0)
    near = jnp.abs(iota((side, side), 1) - iota((side, side), 0)) < side // 2

    def spread(index):
        rows = jnp.broadcast_to(taps[index : index + 1, :], (side, side))
        rolled = pltpu.roll(rows, 0, 1, stride=1, stride_axis=0)
        return jnp.where(near, rolled, 0.0).astype(BF)

    for k in range(patches):
        labels[k] = jnp.full((LABELS, side), -1.0, F32)
    count = [jnp.int32(0)] * patches
    for i, v in itertools.product(range(tile_cols), range(visit_count)):
        n = v * tile_cols + i
        if v == 0 and i % per_group == 0:
            loads[i // per_group].wait()
        halfway = jnp.dot(spread(2 * n), raw[v, i], preferred_element_type=F32).astype(BF)
        warped = jnp.dot(halfway, spread(2 * n + 1), preferred_element_type=F32).astype(BF)
        route = routes[v, i]
        owner = lax.div(route, tile_cols)
        slot = route - owner * tile_cols
        relative = lax.rem(owner - sky + patches, patches)
        seat = sum(jnp.where(relative == k, count[k], 0) for k in range(patches))
        count = [count[k] + (relative == k).astype(I32) for k in range(patches)]
        seats[relative * cap + seat] = warped
        labels[relative, pl.ds(seat, 1), :] = jnp.full(
            (1, side), ((visit * visit_count + v) * tile_cols + slot).astype(F32), F32
        )
    for k in range(patches):
        for r in range(visits):
            parcel = parcels[k * visits + r]
            target = lax.rem(visit + r, visits)
            rows = pl.ds(pl.multiple_of(target * part, part), part)
            for seat in range(cap):
                parcel[seat * part : (seat + 1) * part, :] = seats[k * cap + seat, rows, :]
            parcel[cap * part :, :] = labels[k].astype(BF)


def warp_tiles(patches, visits, cap, raw, offsets, entries, table, routes):
    visit_count, tile_cols, side, _ = raw.shape
    parcel = jax.ShapeDtypeStruct((cap * (side // visits) + LABELS, side), BF)
    small = [routes, jnp.transpose(offsets, (0, 2, 1)), entries, table.T]
    return kernel_call(
        functools.partial(warp_body, patches, visits, cap),
        [parcel] * (patches * visits),
        [HBM] * 5,
        [pltpu.SMEM(a.shape, a.dtype) for a in small]
        + [
            pltpu.VMEM(raw.shape, BF),
            pltpu.SemaphoreType.DMA((len(small),)),
            pltpu.SemaphoreType.DMA((math.gcd(4, tile_cols),)),
            pltpu.VMEM((patches * cap, side, side), BF),
            pltpu.VMEM((patches, LABELS, side), F32),
        ],
        flops=4 * visit_count * tile_cols * side**3,
        data=4 * raw.size,
    )(*(pltpu.with_memory_space_constraint(a, pltpu.HBM) for a in (*small, raw)))


def tables_body(side, block, choice, coefs, listed, taps, plane, bands, mixes):
    for j, t, b in itertools.product(*map(range, (*choice.shape, coefs.shape[0]))):
        row = (j * choice.shape[1] + t) * coefs.shape[0] + b
        mixes[row : row + 1, :] = jnp.full((1, side), coefs[b, choice[j, t]], F32)
    visit_total, tile_cols, per = listed.shape
    width = visit_total * per
    bad = jnp.concatenate([listed[v] for v in range(visit_total)], axis=1)
    bad_row = lax.div(bad, side)
    bad_col = bad - bad_row * side
    place = iota((side, width), 0)
    weight = (lax.div(iota((side, width), 1), per) + 1).astype(F32)
    for t in range(tile_cols):
        rows = jnp.where(bad_row[t : t + 1, :] == place, 1.0, 0.0).astype(BF)
        cols = jnp.where(bad_col[t : t + 1, :] == place, weight, 0.0).astype(BF)
        plane[:, t * side : (t + 1) * side] = lax.dot_general(
            rows, cols, (((1,), (1,)), ((), ())), preferred_element_type=F32
        )
    bases, pairs, lanes = taps.shape
    for b in range(bases):
        for j in range(pairs):
            rows = jnp.broadcast_to(taps[b, j : j + 1, :], (block, lanes))
            bands[b * block : (b + 1) * block, j * lanes : (j + 1) * lanes] = pltpu.roll(
                rows, 0, 1, stride=1, stride_axis=0
            ).astype(BF)


def make_tables(choice, coefs, listed, kernels, side, block):
    visit_total, tile_cols, per = listed.shape
    bases, taps, _ = kernels.shape
    window = block + taps - 1
    group = max(1, 128 // window)
    padded = -(-taps // group) * group
    columns = jnp.pad(
        jnp.transpose(kernels, (0, 2, 1)).astype(F32), ((0, 0), (0, padded - taps), (0, window - taps))
    ).reshape(bases, padded // group, group * window)
    return kernel_call(
        functools.partial(tables_body, side, block),
        [
            jax.ShapeDtypeStruct((side, tile_cols * side), F32),
            jax.ShapeDtypeStruct((bases * block, padded * window), BF),
            jax.ShapeDtypeStruct((choice.size * bases, side), F32),
        ],
        [SMEM] * 2 + [VMEM] * 2,
        flops=2 * tile_cols * side * side * visit_total * per,
        data=4 * side * side * tile_cols,
    )(choice, coefs.T, listed, columns)


def land_body(visits, bands, visit_count, cap, plane, *refs):
    count = len(refs) - 2 - visits
    parcels, slabs, partial, image = refs[:count], refs[count:-2], refs[-2], refs[-1]
    side = parcels[0].shape[1]
    part = (parcels[0].shape[0] - LABELS) // cap
    tile_cols = image.shape[2] // side
    held = visits * visit_count
    visit, band = lax.axis_index("visit"), lax.axis_index("band")
    for parcel in parcels:
        labels = parcel[cap * part :, :].astype(F32)
        for seat in range(cap):
            label = labels[seat, 0].astype(I32)
            label = jnp.where(label < 0, held * tile_cols, label)
            which = lax.div(label, tile_cols)
            column = (label - which * tile_cols) * side
            image[which, :, pl.ds(pl.multiple_of(column, side), side)] = parcel[
                seat * part : (seat + 1) * part, :
            ]
    mine = plane[pl.ds(pl.multiple_of(visit * part, part), part), :]
    total = jnp.zeros(mine.shape, F32)
    high = jnp.full(mine.shape, -jnp.inf, F32)
    low = jnp.full(mine.shape, jnp.inf, F32)
    for n in range(held):
        own, local = divmod(n, visit_count)
        number = ((own * bands + band) * visit_count + local + 1).astype(F32)
        value = image[n].astype(F32)
        bad = mine == number
        total = total + jnp.where(bad, 0.0, value)
        high = jnp.maximum(high, jnp.where(bad, -jnp.inf, value))
        low = jnp.minimum(low, jnp.where(bad, jnp.inf, value))
    partial[0] = total.astype(BF)
    partial[1] = high.astype(BF)
    partial[2] = low.astype(BF)
    for r in range(visits):
        base = lax.rem(visit + r, visits) * visit_count
        for j in range(visit_count):
            slabs[r][j] = image[base + j]


def land_tiles(visits, bands, visit_count, cap, tile_cols, plane, parcels):
    side = parcels[0].shape[1]
    part = (parcels[0].shape[0] - LABELS) // cap
    width = tile_cols * side
    out = kernel_call(
        functools.partial(land_body, visits, bands, visit_count, cap),
        [jax.ShapeDtypeStruct((visit_count, part, width), BF)] * visits
        + [jax.ShapeDtypeStruct((3, part, width), BF)],
        [VMEM] * (1 + len(parcels)),
        [pltpu.VMEM((visits * visit_count + 1, part, width), BF)],
        flops=10 * visits * visit_count * part * width,
        data=4 * visits * visit_count * part * width,
    )(plane, *parcels)
    return out[:-1], out[-1]


def coadd_body(visit_total, margin, plane, *refs):
    partials, (coadd, edge) = refs[:-2], refs[-2:]
    part = coadd.shape[0]
    visit = lax.axis_index("visit")
    mine = plane[pl.ds(pl.multiple_of(visit * part, part), part), :]
    total, high, low = (partials[0][n].astype(F32) for n in range(3))
    for other in partials[1:]:
        total = total + other[0].astype(F32)
        high = jnp.maximum(high, other[1].astype(F32))
        low = jnp.minimum(low, other[2].astype(F32))
    scale = jnp.where(mine > 0.0, 1.0 / (visit_total - 3.0), 1.0 / (visit_total - 2.0))
    coadd[...] = ((total - high - low) * scale).astype(BF)
    start = pl.multiple_of(jnp.where(visit == 0, 0, part - margin), margin)
    edge[...] = coadd[pl.ds(start, margin), :]


def filter_body(visits, margin, bands, *refs):
    pieces, halos = refs[:visits], refs[visits : visits + 2]
    out, image, moved = refs[visits + 2 :]
    sky, visit, band = (lax.axis_index(name) for name in ("sky", "visit", "band"))
    patches = lax.axis_size("sky")
    part, width = pieces[0].shape
    taps = moved.shape[0]
    mine = lax.rem(visit, 2) == band
    below = jnp.where(mine, halos[0][...], halos[1][...])
    above = jnp.where(mine, halos[1][...], halos[0][...])
    below = jnp.where(sky == patches - 1, jnp.zeros_like(below), below)
    above = jnp.where(sky == 0, jnp.zeros_like(above), above)
    image[:margin, :] = above
    image[margin + visits * part :, :] = below
    for r in range(visits):
        start = pl.multiple_of(lax.rem(visit + r, visits) * part + margin, margin)
        image[pl.ds(start, part), :] = pieces[r][...]
    column = iota((image.shape[0], width), 1)
    zero = jnp.zeros((), BF)
    for dx in range(taps):
        rolled = pltpu.roll(image[...], (margin - dx) % width, 1)
        if dx < margin:
            rolled = jnp.where(column >= margin - dx, rolled, zero)
        elif dx > margin:
            rolled = jnp.where(column < width + margin - dx, rolled, zero)
        moved[dx] = rolled
    blocks = out.shape[0]
    block = visits * part // blocks
    window = block + 2 * margin
    step = min(256, width)
    left = bands[:, : taps * window]
    for n in range(blocks):
        for c in range(0, width, step):
            right = moved[:, n * block : n * block + window, c : c + step].reshape(taps * window, step)
            out[n, :, c : c + step] = jnp.dot(left, right, preferred_element_type=F32).astype(BF)


def finish_body(visits, bands, tile_cols, mixes, filtered, plane, *refs):
    slabs, (out, image, result, sems) = refs[:visits], refs[visits:]
    visit, band = lax.axis_index("visit"), lax.axis_index("band")
    visit_count, part, width = slabs[0].shape
    blocks = filtered.shape[0]
    bases = mixes.shape[0] // (visit_count * tile_cols)
    block = filtered.shape[1] // bases
    side = width // tile_cols
    for r in range(visits):
        start = pl.multiple_of(lax.rem(visit + r, visits) * part, part)
        image[:, pl.ds(start, part), :] = slabs[r][...]
    numbers = [
        ((visit * bands + band) * visit_count + j + 1).astype(F32) for j in range(visit_count)
    ]
    copies = []
    for n in range(blocks):
        rows = slice(n * block, (n + 1) * block)
        for t in range(tile_cols):
            cols = slice(t * side, (t + 1) * side)
            planes = [
                filtered[n, b * block : (b + 1) * block, cols].astype(F32) for b in range(bases)
            ]
            bad = plane[rows, cols]
            for j in range(visit_count):
                row = (j * tile_cols + t) * bases
                template = sum(mixes[row + b : row + b + 1, :] * planes[b] for b in range(bases))
                value = image[j, rows, cols].astype(F32) - template
                result[j, rows, cols] = jnp.where(bad == numbers[j], 0.0, value).astype(BF)
        copies.append(pltpu.make_async_copy(result.at[:, rows], out.at[:, rows], sems.at[n]))
        copies[-1].start()
    for copy in copies:
        copy.wait()


def on_device(
    raw_tiles,
    pixel_offsets,
    shift_entry_index,
    shift_table,
    tile_routes,
    bad_pixels,
    basis_kernels,
    basis_choice,
    coef_table,
):
    visit_count, tile_cols, side = raw_tiles.shape[:3]
    patches, visits, bands = (lax.axis_size(name) for name in ("sky", "visit", "band"))
    cap = (visit_count * tile_cols + patches - 1) // patches + 1
    part, width = side // visits, tile_cols * side
    visit_total = bad_pixels.shape[0]
    bases, taps = basis_kernels.shape[:2]
    margin = taps // 2
    block = 2 * margin

    parcels = warp_tiles(
        patches, visits, cap, raw_tiles, pixel_offsets, shift_entry_index, shift_table, tile_routes
    )
    far = sorted(range(patches), key=lambda k: (-min(k, patches - k), -k))
    order = [k * visits + r for k in far for r in reversed(range(visits)) if k + r > 0]
    arrived = [parcels[0]]
    for n in order:
        k, r = divmod(n, visits)
        pairs = [
            (s * visits + v, (s + k) % patches * visits + (v + r) % visits)
            for s in range(patches)
            for v in range(visits)
        ]
        arrived.append(lax.ppermute(parcels[n], ("sky", "visit"), pairs))
    plane, toeplitz, mixes = make_tables(
        basis_choice, coef_table, bad_pixels, basis_kernels, side, block
    )
    slabs, partial = land_tiles(visits, bands, visit_count, cap, tile_cols, plane, arrived)

    partials = [partial] + [
        lax.ppermute(partial, "band", [(b, (b + q) % bands) for b in range(bands)])
        for q in range(1, bands)
    ]
    coadd, edge = kernel_call(
        functools.partial(coadd_body, visit_total, margin),
        [jax.ShapeDtypeStruct((part, width), BF), jax.ShapeDtypeStruct((margin, width), BF)],
        [VMEM] * (1 + bands),
        flops=8 * part * width,
        data=8 * part * width,
    )(plane, *partials)

    def turn(r):
        return [(v, (v - r) % visits) for v in range(visits)]

    pieces = [coadd] + [lax.ppermute(coadd, "visit", turn(r)) for r in range(1, visits)]
    halos = []
    for first in range(0, visits, bands):
        pairs = []
        for s, b in itertools.product(range(patches), range(bands)):
            r = first + b
            top = ((s - 1) % patches, r)
            bottom = ((s + 1) % patches, visits - 1 - r)
            for v, (to_s, to_v) in ((0, top), (visits - 1, bottom)):
                pairs.append(((s * visits + v) * bands + b, (to_s * visits + to_v) * bands + b))
        halos.append(lax.ppermute(edge, ("sky", "visit", "band"), pairs))
    halo = functools.reduce(jnp.add, halos)
    halos = [halo, lax.ppermute(halo, "band", [(b, (b + 1) % bands) for b in range(bands)])]
    own = [slabs[0]] + [
        lax.ppermute(slabs[r], "visit", [(v, (v + r) % visits) for v in range(visits)])
        for r in range(1, visits)
    ]
    own = [own[0]] + [own[visits - r] for r in range(1, visits)]
    filtered = kernel_call(
        functools.partial(filter_body, visits, margin),
        jax.ShapeDtypeStruct((side // block, bases * block, width), BF),
        [VMEM] * (3 + visits),
        [
            pltpu.VMEM((side + 2 * margin, width), BF),
            pltpu.VMEM((taps, side + 2 * margin, width), BF),
        ],
        flops=2 * bases * side * width * taps * (block + taps - 1),
        data=2 * bases * side * width,
    )(toeplitz, *pieces, *halos)
    return kernel_call(
        functools.partial(finish_body, visits, bands, tile_cols),
        jax.ShapeDtypeStruct((visit_count, side, width), BF),
        [VMEM] * (3 + visits),
        [
            pltpu.VMEM((visit_count, side, width), BF),
            pltpu.VMEM((visit_count, side, width), BF),
            pltpu.SemaphoreType.DMA((side // block,)),
        ],
        flops=20 * visit_count * side * width,
        data=4 * visit_count * side * width,
        out_specs=HBM,
    )(mixes, filtered, plane, *own)


def solution(mesh):
    return jax.shard_map(
        on_device,
        mesh=mesh,
        in_specs=(
            P(("group", "visit", "band"), "sky", None, None),
            P(("group", "visit", "band"), "sky", None),
            P(("group", "visit", "band"), "sky"),
            P(),
            P(("group", "visit", "band"), "sky"),
            P("group", "sky", None),
            P(),
            P(("group", "visit", "band"), "sky"),
            P(),
        ),
        out_specs=P(("group", "visit", "band"), "sky", None),
        check_vma=False,
    )
```

profile of v0, /device:TPU:0, one launch (start us, length us, event | category | flops | bytes accessed | tf_op | source)
XLA Modules:
  0.0 40.7 jit_solution(16277834444006535453)
XLA Ops:
  0.0 0.0 copy-start.3
  0.0 2.7 %shard_map.92 = (bf16[328,128]{1,0:T(8,128)(2,1)S(1)}, bf16[328,128]{1,0:T(8,128)(2,1)S(1)}, bf16[328,128]{1,0:T(8,128)(2,1)S(1)}, bf16[328,128]{1,0:T(8,128)(2,...) custom-call(s32[2,8]{1,0:T(2,128)} %refs_0_.1, ...), custom_call_target="tpu_custom_call" | custom-call | flops 134217728 | bytes 1048576 | tf_op jit(solution)/shard_map/pallas_call | solution.py:27
  2.7 5.1 %collective-permute-start = (bf16[328,128]{1,0:T(8,128)(2,1)S(1)}, bf16[328,128]{1,0:T(8,128)(2,1)S(1)}, u32[]{:S(2)}, u32[]{:S(2)}) collective-permute-start(bf16[328,128]{1,0:T(8,128)(2,1)S(1)} %get-tuple-element.25), channel_id=1, source_target_pairs={{0,10},{2,8},{4,14},{6,12},{8,2},{10,0},{12,6},{14,4},{1,11},{3,9}... | collective-permute-start | bytes 251912 | tf_op jit(solution)/shard_map/ppermute | solution.py:367
  7.7 0.3 collective-permute-start.1
  8.1 3.6 %collective-permute-start.2 = (bf16[328,128]{1,0:T(8,128)(2,1)S(1)}, bf16[328,128]{1,0:T(8,128)(2,1)S(1)}, u32[]{:S(2)}, u32[]{:S(2)}) collective-permute-start(bf16[328,128]{1,0:T(8,128)(2,1)S(1)} %get-tuple-element.27), channel_id=1, source_target_pairs={{0,14},{2,12},{4,2},{6,0},{8,6},{10,4},{12,10},{14,8},{1,15},{3,13... | collective-permute-start | bytes 251912 | tf_op jit(solution)/shard_map/ppermute | solution.py:367
  11.6 0.4 %collective-permute-start.3 = (bf16[328,128]{1,0:T(8,128)(2,1)S(1)}, bf16[328,128]{1,0:T(8,128)(2,1)S(1)}, u32[]{:S(2)}, u32[]{:S(2)}) collective-permute-start(bf16[328,128]{1,0:T(8,128)(2,1)S(1)} %get-tuple-element.28), channel_id=1, source_target_pairs={{0,12},{2,14},{4,0},{6,2},{8,4},{10,6},{12,8},{14,10},{1,13},{3,15... | collective-permute-start | bytes 251912 | tf_op jit(solution)/shard_map/ppermute | solution.py:367
  12.1 2.5 %collective-permute-start.4 = (bf16[328,128]{1,0:T(8,128)(2,1)S(1)}, bf16[328,128]{1,0:T(8,128)(2,1)S(1)}, u32[]{:S(2)}, u32[]{:S(2)}) collective-permute-start(bf16[328,128]{1,0:T(8,128)(2,1)S(1)} %get-tuple-element.29), channel_id=1, source_target_pairs={{0,6},{2,4},{4,10},{6,8},{8,14},{10,12},{12,2},{14,0},{1,7},{3,5},... | collective-permute-start | bytes 251912 | tf_op jit(solution)/shard_map/ppermute | solution.py:367
  14.6 0.0 copy-done.3
  14.6 0.1 copy.12
  14.7 0.0 collective-permute-done.refs_1_
  14.7 3.5 %collective-permute-start.5 = (bf16[328,128]{1,0:T(8,128)(2,1)S(1)}, bf16[328,128]{1,0:T(8,128)(2,1)S(1)}, u32[]{:S(2)}, u32[]{:S(2)}) collective-permute-start(bf16[328,128]{1,0:T(8,128)(2,1)S(1)} %get-tuple-element.30), channel_id=1, source_target_pairs={{0,4},{2,6},{4,8},{6,10},{8,12},{10,14},{12,0},{14,2},{1,5},{3,7},... | collective-permute-start | bytes 251912 | tf_op jit(solution)/shard_map/ppermute | solution.py:367
  18.3 0.0 collective-permute-done.1.refs_2_
  18.3 0.0 collective-permute-start.6
  18.3 0.0 copy-start
  18.3 0.0 copy-start.1
  18.4 0.1 reshape.8.taps
  18.4 0.0 copy-start.2
  18.4 0.7 %copy-done = s32[8,8,32]{2,1,0:T(8,128)S(1)} copy-done((s32[8,8,32]{2,1,0:T(8,128)S(1)}, s32[8,8,32]{2,1,0:T(8,128)}, u32[]{:S(2)}) %copy-start) | copy-done | bytes 8216
  19.1 0.0 copy-done.1
  19.1 0.0 copy-done.2
  19.1 1.0 %shard_map.91 = (f32[128,1024]{1,0:T(8,128)S(1)}, bf16[128,2176]{1,0:T(8,128)(2,1)S(1)}, f32[64,128]{1,0:T(8,128)S(1)}) custom-call(s32[2,8]{1,0:T(2,128)S(1)} %copy-done.2, f32[4,16]{1,0:T(4,128)S(1)} %bitcast.4, s32[8,8,32]{2,1,0:T(8,128)S(1)} %copy-done, f32[4,17,128]{2,1,0:T(8,128)S(1)} %reshape.8.taps), custom_call_target="tpu_custom_call" | custom-call | flops 67108864 | bytes 524288 | tf_op jit(solution)/shard_map/pallas_call | solution.py:27
  20.1 0.0 collective-permute-done.2.refs_3_
  20.1 0.0 collective-permute-done.3.refs_4_
  20.1 0.0 collective-permute-done.4.refs_5_
  20.1 3.5 %collective-permute-done.5.refs_6_ = bf16[328,128]{1,0:T(8,128)(2,1)S(1)} collective-permute-done((bf16[328,128]{1,0:T(8,128)(2,1)S(1)}, bf16[328,128]{1,0:T(8,128)(2,1)S(1)}, u32[]{:S(2)}, u32[]{:S(2)}) %collective-permute-start.5) | collective-permute-done | bytes 84000 | tf_op jit(solution)/shard_map/ppermute | solution.py:367
  23.6 0.0 collective-permute-done.6.refs_7_
  23.6 0.8 %shard_map.93 = (bf16[2,64,1024]{2,1,0:T(8,128)(2,1)S(1)}, bf16[2,64,1024]{2,1,0:T(8,128)(2,1)S(1)}, bf16[3,64,1024]{2,1,0:T(8,128)(2,1)S(1)}) custom-call(f32[128,1024]{1,0:T(8,128)S(1)} %get-tuple-element.23.plane, bf16[328,128]{1,0:T(8,128)(2,1)S(1)} %get-tuple-element.24.refs_0_, bf16[328,128]{1,0:T(8,128)(2,1)S(1)} %collective-permute-done.refs_1_, ...), custom_call_target="tpu_custom_call" | custom-call | flops 2621440 | bytes 1048576 | tf_op jit(solution)/shard_map/pallas_call | solution.py:27
  24.5 0.1 collective-permute-start.7
  24.6 1.7 %collective-permute-done.7.refs_1_ = bf16[3,64,1024]{2,1,0:T(8,128)(2,1)S(1)} collective-permute-done((bf16[3,64,1024]{2,1,0:T(8,128)(2,1)S(1)}, bf16[3,64,1024]{2,1,0:T(8,128)(2,1)S(1)}, u32[]{:S(2)}, u32[]{:S(2)}) %collective-permute-start.7) | collective-permute-done | bytes 393248 | tf_op jit(solution)/shard_map/ppermute | solution.py:374
  26.3 0.2 shard_map.94
  26.5 1.6 %collective-permute-start.8 = (bf16[64,1024]{1,0:T(8,128)(2,1)S(1)}, bf16[64,1024]{1,0:T(8,128)(2,1)S(1)}, u32[]{:S(2)}, u32[]{:S(2)}) collective-permute-start(bf16[64,1024]{1,0:T(8,128)(2,1)S(1)} %get-tuple-element.33.refs_0_), channel_id=1, source_target_pairs={{0,2},{2,0},{1,3},{3,1},{4,6},{6,4},{5,7},{7,5},{8,10},{10,8},{9,1... | collective-permute-start | bytes 393224 | tf_op jit(solution)/shard_map/ppermute | solution.py:388
  28.1 2.8 %collective-permute-start.9 = (bf16[16,1024]{1,0:T(8,128)(2,1)S(1)}, bf16[16,1024]{1,0:T(8,128)(2,1)S(1)}, u32[]{:S(2)}, u32[]{:S(2)}) collective-permute-start(bf16[16,1024]{1,0:T(8,128)(2,1)S(1)} %get-tuple-element.34), channel_id=1, source_target_pairs={{0,12},{2,6},{1,15},{3,5},{4,0},{6,10},{5,3},{7,9},{8,4},{10,14},{... | collective-permute-start | bytes 98312 | tf_op jit(solution)/shard_map/ppermute | solution.py:398
  30.8 0.0 collective-permute-start.11
  30.8 1.6 %collective-permute-done.9.refs_2_ = bf16[16,1024]{1,0:T(8,128)(2,1)S(1)} collective-permute-done((bf16[16,1024]{1,0:T(8,128)(2,1)S(1)}, bf16[16,1024]{1,0:T(8,128)(2,1)S(1)}, u32[]{:S(2)}, u32[]{:S(2)}) %collective-permute-start.9) | collective-permute-done | bytes 32800 | tf_op jit(solution)/shard_map/ppermute | solution.py:398
  32.4 1.1 %collective-permute-start.10 = (bf16[16,1024]{1,0:T(8,128)(2,1)S(1)}, bf16[16,1024]{1,0:T(8,128)(2,1)S(1)}, u32[]{:S(2)}, u32[]{:S(2)}) collective-permute-start(bf16[16,1024]{1,0:T(8,128)(2,1)S(1)} %collective-permute-done.9.refs_2_), channel_id=1, source_target_pairs={{0,1},{1,0},{2,3},{3,2},{4,5},{5,4},{6,7},{7,6},{8,9},{9,8},{10,11... | collective-permute-start | bytes 98312 | tf_op jit(solution)/shard_map/ppermute | solution.py:400
  33.5 0.9 %collective-permute-done.10.refs_3_ = bf16[16,1024]{1,0:T(8,128)(2,1)S(1)} collective-permute-done((bf16[16,1024]{1,0:T(8,128)(2,1)S(1)}, bf16[16,1024]{1,0:T(8,128)(2,1)S(1)}, u32[]{:S(2)}, u32[]{:S(2)}) %collective-permute-start.10) | collective-permute-done | bytes 32800 | tf_op jit(solution)/shard_map/ppermute | solution.py:400
  34.4 0.0 collective-permute-done.8.refs_1_
  34.4 3.7 %shard_map.95.filtered = bf16[4,128,1024]{2,1,0:T(8,128)(2,1)S(1)} custom-call(bf16[128,2176]{1,0:T(8,128)(2,1)S(1)} %get-tuple-element.22.bands, bf16[64,1024]{1,0:T(8,128)(2,1)S(1)} %get-tuple-element.33.refs_0_, bf16[64,1024]{1,0:T(8,128)(2,1)S(1)} %collective-permute-done.8.refs_1_, bf16[16,1024]{1,0:T(8,128)(2,1)S(1)} %collective-permute-done.9.refs_2_, ...), custom_call_target="tpu_custom_call" | custom-call | flops 2214592512 | bytes 1048576 | tf_op jit(solution)/shard_map/pallas_call | solution.py:27
  38.1 1.4 %collective-permute-done.11.refs_1_ = bf16[2,64,1024]{2,1,0:T(8,128)(2,1)S(1)} collective-permute-done((bf16[2,64,1024]{2,1,0:T(8,128)(2,1)S(1)}, bf16[2,64,1024]{2,1,0:T(8,128)(2,1)S(1)}, u32[]{:S(2)}, u32[]{:S(2)}) %collective-permute-start.11) | collective-permute-done | bytes 262176 | tf_op jit(solution)/shard_map/ppermute | solution.py:402
  39.5 1.2 %shard_map.96 = bf16[2,128,1024]{2,1,0:T(8,128)(2,1)} custom-call(f32[64,128]{1,0:T(8,128)S(1)} %get-tuple-element.21.mixes, bf16[4,128,1024]{2,1,0:T(8,128)(2,1)S(1)} %shard_map.95.filtered, f32[128,1024]{1,0:T(8,128)S(1)} %get-tuple-element.23.plane, bf16[2,64,1024]{2,1,0:T(8,128)(2,1)S(1)} %get-tuple-element.35.refs_0_, ...), custom_call_target="tpu_custom_call" | custom-call | flops 5242880 | bytes 1048576 | tf_op jit(solution)/shard_map/pallas_call | solution.py:27
  (2 shorter events, 0.0 us)
Async XLA Ops:
  0.0 14.6 %copy-start.3 = (bf16[4,33,33]{2,0,1:T(4,128)(2,1)S(1)}, bf16[4,33,33]{2,0,1:T(4,128)(2,1)}, u32[]{:S(2)}) copy-start(bf16[4,33,33]{2,0,1:T(4,128)(2,1)} %param.15) | copy-start | bytes 26140
  2.7 12.1 %collective-permute-start = (bf16[328,128]{1,0:T(8,128)(2,1)S(1)}, bf16[328,128]{1,0:T(8,128)(2,1)S(1)}, u32[]{:S(2)}, u32[]{:S(2)}) collective-permute-start(bf16[328,128]{1,0:T(8,128)(2,1)S(1)} %get-tuple-element.25), channel_id=1, source_target_pairs={{0,10},{2,8},{4,14},{6,12},{8,2},{10,0},{12,6},{14,4},{1,11},{3,9}... | collective-permute-start | bytes 251912 | tf_op jit(solution)/shard_map/ppermute | solution.py:367
  7.7 10.6 %collective-permute-start.1 = (bf16[328,128]{1,0:T(8,128)(2,1)S(1)}, bf16[328,128]{1,0:T(8,128)(2,1)S(1)}, u32[]{:S(2)}, u32[]{:S(2)}) collective-permute-start(bf16[328,128]{1,0:T(8,128)(2,1)S(1)} %get-tuple-element.26), channel_id=1, source_target_pairs={{0,8},{2,10},{4,12},{6,14},{8,0},{10,2},{12,4},{14,6},{1,9},{3,11}... | collective-permute-start | bytes 251912 | tf_op jit(solution)/shard_map/ppermute | solution.py:367
  8.1 12.0 %collective-permute-start.2 = (bf16[328,128]{1,0:T(8,128)(2,1)S(1)}, bf16[328,128]{1,0:T(8,128)(2,1)S(1)}, u32[]{:S(2)}, u32[]{:S(2)}) collective-permute-start(bf16[328,128]{1,0:T(8,128)(2,1)S(1)} %get-tuple-element.27), channel_id=1, source_target_pairs={{0,14},{2,12},{4,2},{6,0},{8,6},{10,4},{12,10},{14,8},{1,15},{3,13... | collective-permute-start | bytes 251912 | tf_op jit(solution)/shard_map/ppermute | solution.py:367
  11.6 8.5 %collective-permute-start.3 = (bf16[328,128]{1,0:T(8,128)(2,1)S(1)}, bf16[328,128]{1,0:T(8,128)(2,1)S(1)}, u32[]{:S(2)}, u32[]{:S(2)}) collective-permute-start(bf16[328,128]{1,0:T(8,128)(2,1)S(1)} %get-tuple-element.28), channel_id=1, source_target_pairs={{0,12},{2,14},{4,0},{6,2},{8,4},{10,6},{12,8},{14,10},{1,13},{3,15... | collective-permute-start | bytes 251912 | tf_op jit(solution)/shard_map/ppermute | solution.py:367
  12.1 8.0 %collective-permute-start.4 = (bf16[328,128]{1,0:T(8,128)(2,1)S(1)}, bf16[328,128]{1,0:T(8,128)(2,1)S(1)}, u32[]{:S(2)}, u32[]{:S(2)}) collective-permute-start(bf16[328,128]{1,0:T(8,128)(2,1)S(1)} %get-tuple-element.29), channel_id=1, source_target_pairs={{0,6},{2,4},{4,10},{6,8},{8,14},{10,12},{12,2},{14,0},{1,7},{3,5},... | collective-permute-start | bytes 251912 | tf_op jit(solution)/shard_map/ppermute | solution.py:367
  14.7 8.9 %collective-permute-start.5 = (bf16[328,128]{1,0:T(8,128)(2,1)S(1)}, bf16[328,128]{1,0:T(8,128)(2,1)S(1)}, u32[]{:S(2)}, u32[]{:S(2)}) collective-permute-start(bf16[328,128]{1,0:T(8,128)(2,1)S(1)} %get-tuple-element.30), channel_id=1, source_target_pairs={{0,4},{2,6},{4,8},{6,10},{8,12},{10,14},{12,0},{14,2},{1,5},{3,7},... | collective-permute-start | bytes 251912 | tf_op jit(solution)/shard_map/ppermute | solution.py:367
  18.3 5.4 %collective-permute-start.6 = (bf16[328,128]{1,0:T(8,128)(2,1)S(1)}, bf16[328,128]{1,0:T(8,128)(2,1)S(1)}, u32[]{:S(2)}, u32[]{:S(2)}) collective-permute-start(bf16[328,128]{1,0:T(8,128)(2,1)S(1)} %get-tuple-element.31), channel_id=1, source_target_pairs={{0,2},{2,0},{4,6},{6,4},{8,10},{10,8},{12,14},{14,12},{1,3},{3,1},... | collective-permute-start | bytes 251912 | tf_op jit(solution)/shard_map/ppermute | solution.py:367
  18.3 0.8 %copy-start = (s32[8,8,32]{2,1,0:T(8,128)S(1)}, s32[8,8,32]{2,1,0:T(8,128)}, u32[]{:S(2)}) copy-start(s32[8,8,32]{2,1,0:T(8,128)} %listed.1) | copy-start | bytes 24580
  18.3 0.8 %copy-start.1 = (f32[16,4]{0,1:T(4,128)S(1)}, f32[16,4]{0,1:T(4,128)}, u32[]{:S(2)}) copy-start(f32[16,4]{0,1:T(4,128)} %param.17) | copy-start | bytes 772
  18.4 0.7 %copy-start.2 = (s32[2,8]{1,0:T(2,128)S(1)}, s32[2,8]{1,0:T(2,128)}, u32[]{:S(2)}) copy-start(s32[2,8]{1,0:T(2,128)} %choice.1) | copy-start | bytes 196
  24.5 1.8 %collective-permute-start.7 = (bf16[3,64,1024]{2,1,0:T(8,128)(2,1)S(1)}, bf16[3,64,1024]{2,1,0:T(8,128)(2,1)S(1)}, u32[]{:S(2)}, u32[]{:S(2)}) collective-permute-start(bf16[3,64,1024]{2,1,0:T(8,128)(2,1)S(1)} %get-tuple-element.32.refs_0_), channel_id=1, source_target_pairs={{0,1},{1,0},{2,3},{3,2},{4,5},{5,4},{6,7},{7,6},{8,9},{9,8},{10,11... | collective-permute-start | bytes 1179656 | tf_op jit(solution)/shard_map/ppermute | solution.py:374
  26.5 7.9 %collective-permute-start.8 = (bf16[64,1024]{1,0:T(8,128)(2,1)S(1)}, bf16[64,1024]{1,0:T(8,128)(2,1)S(1)}, u32[]{:S(2)}, u32[]{:S(2)}) collective-permute-start(bf16[64,1024]{1,0:T(8,128)(2,1)S(1)} %get-tuple-element.33.refs_0_), channel_id=1, source_target_pairs={{0,2},{2,0},{1,3},{3,1},{4,6},{6,4},{5,7},{7,5},{8,10},{10,8},{9,1... | collective-permute-start | bytes 393224 | tf_op jit(solution)/shard_map/ppermute | solution.py:388
  28.1 4.4 %collective-permute-start.9 = (bf16[16,1024]{1,0:T(8,128)(2,1)S(1)}, bf16[16,1024]{1,0:T(8,128)(2,1)S(1)}, u32[]{:S(2)}, u32[]{:S(2)}) collective-permute-start(bf16[16,1024]{1,0:T(8,128)(2,1)S(1)} %get-tuple-element.34), channel_id=1, source_target_pairs={{0,12},{2,6},{1,15},{3,5},{4,0},{6,10},{5,3},{7,9},{8,4},{10,14},{... | collective-permute-start | bytes 98312 | tf_op jit(solution)/shard_map/ppermute | solution.py:398
  30.8 8.7 %collective-permute-start.11 = (bf16[2,64,1024]{2,1,0:T(8,128)(2,1)S(1)}, bf16[2,64,1024]{2,1,0:T(8,128)(2,1)S(1)}, u32[]{:S(2)}, u32[]{:S(2)}) collective-permute-start(bf16[2,64,1024]{2,1,0:T(8,128)(2,1)S(1)} %get-tuple-element.36), channel_id=1, source_target_pairs={{0,2},{2,0},{1,3},{3,1},{4,6},{6,4},{5,7},{7,5},{8,10},{10,8},{9,1... | collective-permute-start | bytes 786440 | tf_op jit(solution)/shard_map/ppermute | solution.py:402
  32.4 2.0 %collective-permute-start.10 = (bf16[16,1024]{1,0:T(8,128)(2,1)S(1)}, bf16[16,1024]{1,0:T(8,128)(2,1)S(1)}, u32[]{:S(2)}, u32[]{:S(2)}) collective-permute-start(bf16[16,1024]{1,0:T(8,128)(2,1)S(1)} %collective-permute-done.9.refs_2_), channel_id=1, source_target_pairs={{0,1},{1,0},{2,3},{3,2},{4,5},{5,4},{6,7},{7,6},{8,9},{9,8},{10,11... | collective-permute-start | bytes 98312 | tf_op jit(solution)/shard_map/ppermute | solution.py:400
where the time goes:
time: 40.9 us; the launch traced here: 40.7 us
  starting transfers between devices  21 us (51%)
  Pallas kernels  9.59 us (23%)
  waiting for transfers between devices  9.13 us (22%)
  local copies, waits for them, and re-layouts  0.92 us (2%)
    ppermute x7, starting transfers between devices, on_device(): arrived.append(lax.ppermute(parcels[n], ('sky', 'visit'), pairs))  15.5 us
    pallas_call x6, Pallas kernels, call(): pl.pallas_call(body, out_shape=outs, in_specs=in_specs, out_specs=places,...  9.59 us
    ppermute x7, waiting for transfers between devices, on_device(): arrived.append(lax.ppermute(parcels[n], ('sky', 'visit'), pairs))  3.51 us
    ppermute x1, starting transfers between devices, on_device(): halos.append(lax.ppermute(edge, ('sky', 'visit', 'band'), pairs))  2.76 us
    ppermute x1, waiting for transfers between devices, on_device(): lax.ppermute(partial, 'band', [(b, (b + q) % bands) for b in range(bands)])  1.71 us
    ppermute x1, waiting for transfers between devices, on_device(): halos.append(lax.ppermute(edge, ('sky', 'visit', 'band'), pairs))  1.6 us
    ppermute x1, starting transfers between devices, on_device(): lax.ppermute(coadd, 'visit', turn(r))  1.56 us
    ppermute x1, waiting for transfers between devices, on_device(): lax.ppermute(slabs[r], 'visit', [(v, (v + r) % visits) for v in range(vis...  1.45 us
  transfers between devices with their start and end apart: 12, of which 5 were waited for; matrix products, arithmetic and copies ran while one was open for 1% of the time, Pallas kernels for 11%

commit v1 on v0

--- a/solution.py
+++ b/solution.py
@@ -19,7 +19,7 @@
 LABELS = 8
 
 
-def kernel_call(body, outs, in_specs, scratch=(), flops=0, data=0, out_specs=None):
+def kernel_call(body, outs, in_specs, scratch=(), flops=0, data=0, out_specs=None, spare=4):
     def call(*args):
         held = [*args, *jax.tree.leaves(outs), *(s for s in scratch if len(s.shape) > 1)]
         places = out_specs or jax.tree.map(lambda _: VMEM, outs)
@@ -31,7 +31,7 @@
             out_specs=places,
             scratch_shapes=list(scratch),
             cost_estimate=pl.CostEstimate(flops=flops, bytes_accessed=data, transcendentals=0),
-            compiler_params=pltpu.CompilerParams(vmem_limit_bytes=room + room // 4 + (4 << 20)),
+            compiler_params=pltpu.CompilerParams(vmem_limit_bytes=room + room // 4 + (spare << 20)),
         )(*args)
 
     return call
@@ -48,8 +48,8 @@
 
 
 def warp_body(patches, visits, cap, *refs):
-    sources, parcels, held = refs[:5], refs[5:-9], refs[-9:]
-    routes, offsets, entries, table, raw, small, large, seats, labels = held[:9]
+    sources, parcels, held = refs[:5], refs[5:-10], refs[-10:]
+    routes, offsets, entries, table, raw, small, large, seats, labels, weights = held
     copies = [
         pltpu.make_async_copy(source, target, small.at[n])
         for n, (source, target) in enumerate(zip(sources[:4], held[:4]))
@@ -91,15 +91,17 @@
         rolled = pltpu.roll(rows, 0, 1, stride=1, stride_axis=0)
         return jnp.where(near, rolled, 0.0).astype(BF)
 
+    for n in range(2 * tiles):
+        weights[n] = spread(n)
     for k in range(patches):
         labels[k] = jnp.full((LABELS, side), -1.0, F32)
     count = [jnp.int32(0)] * patches
+    for load in loads:
+        load.wait()
     for i, v in itertools.product(range(tile_cols), range(visit_count)):
         n = v * tile_cols + i
-        if v == 0 and i % per_group == 0:
-            loads[i // per_group].wait()
-        halfway = jnp.dot(spread(2 * n), raw[v, i], preferred_element_type=F32).astype(BF)
-        warped = jnp.dot(halfway, spread(2 * n + 1), preferred_element_type=F32).astype(BF)
+        halfway = jnp.dot(weights[2 * n], raw[v, i], preferred_element_type=F32).astype(BF)
+        warped = jnp.dot(halfway, weights[2 * n + 1], preferred_element_type=F32).astype(BF)
         route = routes[v, i]
         owner = lax.div(route, tile_cols)
         slot = route - owner * tile_cols
@@ -135,13 +137,14 @@
             pltpu.SemaphoreType.DMA((math.gcd(4, tile_cols),)),
             pltpu.VMEM((patches * cap, side, side), BF),
             pltpu.VMEM((patches, LABELS, side), F32),
+            pltpu.VMEM((2 * visit_count * tile_cols, side, side), BF),
         ],
         flops=4 * visit_count * tile_cols * side**3,
         data=4 * raw.size,
     )(*(pltpu.with_memory_space_constraint(a, pltpu.HBM) for a in (*small, raw)))
 
 
-def tables_body(side, block, choice, coefs, listed, taps, plane, bands, mixes):
+def tables_body(side, block, choice, coefs, listed, taps, heads, tails, plane, bands, mixes, ends):
     for j, t, b in itertools.product(*map(range, (*choice.shape, coefs.shape[0]))):
         row = (j * choice.shape[1] + t) * coefs.shape[0] + b
         mixes[row : row + 1, :] = jnp.full((1, side), coefs[b, choice[j, t]], F32)
@@ -165,6 +168,17 @@
             bands[b * block : (b + 1) * block, j * lanes : (j + 1) * lanes] = pltpu.roll(
                 rows, 0, 1, stride=1, stride_axis=0
             ).astype(BF)
+    margin = block // 2
+    row, place = iota((block, lanes), 0), lax.rem(iota((block, lanes), 1), margin)
+    for n, (source, shift, fits) in enumerate(
+        ((heads, 0, place >= row), (tails, lanes - 2 * margin + 1, place <= row - margin))
+    ):
+        for b, j in itertools.product(range(bases), range(source.shape[1])):
+            rows = jnp.broadcast_to(source[b, j : j + 1, :], (block, lanes))
+            rolled = pltpu.roll(rows, shift, 1, stride=1, stride_axis=0)
+            ends[n, b * block : (b + 1) * block, j * lanes : (j + 1) * lanes] = jnp.where(
+                fits, rolled, 0.0
+            ).astype(BF)
 
 
 def make_tables(choice, coefs, listed, kernels, side, block):
@@ -173,40 +187,52 @@
     window = block + taps - 1
     group = max(1, 128 // window)
     padded = -(-taps // group) * group
-    columns = jnp.pad(
-        jnp.transpose(kernels, (0, 2, 1)).astype(F32), ((0, 0), (0, padded - taps), (0, window - taps))
-    ).reshape(bases, padded // group, group * window)
+    turned = jnp.transpose(kernels, (0, 2, 1)).astype(F32)
+    columns = jnp.pad(turned, ((0, 0), (0, padded - taps), (0, window - taps))).reshape(
+        bases, padded // group, group * window
+    )
+    margin, lanes = taps // 2, group * window
+    groups = -(-taps * margin // lanes)
+    fill = ((0, 0), (0, groups * lanes // margin - taps), (0, 0))
+    heads, tails = (
+        jnp.pad(part, fill).reshape(bases, groups, lanes)
+        for part in (turned[:, :, :margin], turned[:, :, margin + 1 :])
+    )
     return kernel_call(
         functools.partial(tables_body, side, block),
         [
             jax.ShapeDtypeStruct((side, tile_cols * side), F32),
             jax.ShapeDtypeStruct((bases * block, padded * window), BF),
             jax.ShapeDtypeStruct((choice.size * bases, side), F32),
+            jax.ShapeDtypeStruct((2, bases * block, groups * lanes), BF),
         ],
-        [SMEM] * 2 + [VMEM] * 2,
+        [SMEM] * 2 + [VMEM] * 4,
         flops=2 * tile_cols * side * side * visit_total * per,
         data=4 * side * side * tile_cols,
-    )(choice, coefs.T, listed, columns)
-
-
-def land_body(visits, bands, visit_count, cap, plane, *refs):
-    count = len(refs) - 2 - visits
-    parcels, slabs, partial, image = refs[:count], refs[count:-2], refs[-2], refs[-1]
+    )(choice, coefs.T, listed, columns, heads, tails)
+
+
+def place(parcels, cap, part, image, of):
     side = parcels[0].shape[1]
-    part = (parcels[0].shape[0] - LABELS) // cap
-    tile_cols = image.shape[2] // side
-    held = visits * visit_count
-    visit, band = lax.axis_index("visit"), lax.axis_index("band")
+    tile_cols, dummy = image.shape[2] // side, image.shape[0] - 1
     for parcel in parcels:
         labels = parcel[cap * part :, :].astype(F32)
         for seat in range(cap):
             label = labels[seat, 0].astype(I32)
-            label = jnp.where(label < 0, held * tile_cols, label)
-            which = lax.div(label, tile_cols)
-            column = (label - which * tile_cols) * side
+            number = lax.div(jnp.maximum(label, 0), tile_cols)
+            column = jnp.where(label < 0, 0, label - number * tile_cols) * side
+            which = jnp.where(label < 0, dummy, of(number))
             image[which, :, pl.ds(pl.multiple_of(column, side), side)] = parcel[
                 seat * part : (seat + 1) * part, :
             ]
+
+
+def land_body(visits, bands, visit_count, cap, plane, *refs):
+    parcels, (slab, partial, image) = refs[:-3], refs[-3:]
+    part = slab.shape[1]
+    held = visits * visit_count
+    visit, band = lax.axis_index("visit"), lax.axis_index("band")
+    place(parcels, cap, part, image, lambda number: number)
     mine = plane[pl.ds(pl.multiple_of(visit * part, part), part), :]
     total = jnp.zeros(mine.shape, F32)
     high = jnp.full(mine.shape, -jnp.inf, F32)
@@ -222,32 +248,31 @@
     partial[0] = total.astype(BF)
     partial[1] = high.astype(BF)
     partial[2] = low.astype(BF)
-    for r in range(visits):
-        base = lax.rem(visit + r, visits) * visit_count
-        for j in range(visit_count):
-            slabs[r][j] = image[base + j]
+    for j in range(visit_count):
+        slab[j] = image[visit * visit_count + j]
 
 
 def land_tiles(visits, bands, visit_count, cap, tile_cols, plane, parcels):
     side = parcels[0].shape[1]
     part = (parcels[0].shape[0] - LABELS) // cap
     width = tile_cols * side
-    out = kernel_call(
+    return kernel_call(
         functools.partial(land_body, visits, bands, visit_count, cap),
-        [jax.ShapeDtypeStruct((visit_count, part, width), BF)] * visits
-        + [jax.ShapeDtypeStruct((3, part, width), BF)],
+        [
+            jax.ShapeDtypeStruct((visit_count, part, width), BF),
+            jax.ShapeDtypeStruct((3, part, width), BF),
+        ],
         [VMEM] * (1 + len(parcels)),
         [pltpu.VMEM((visits * visit_count + 1, part, width), BF)],
         flops=10 * visits * visit_count * part * width,
         data=4 * visits * visit_count * part * width,
     )(plane, *parcels)
-    return out[:-1], out[-1]
 
 
 def coadd_body(visit_total, margin, plane, *refs):
-    partials, (coadd, edge) = refs[:-2], refs[-2:]
-    part = coadd.shape[0]
-    visit = lax.axis_index("visit")
+    partials, (coadd, share, edge) = refs[:-3], refs[-3:]
+    part, some = coadd.shape[0], share.shape[0]
+    visit, band = lax.axis_index("visit"), lax.axis_index("band")
     mine = plane[pl.ds(pl.multiple_of(visit * part, part), part), :]
     total, high, low = (partials[0][n].astype(F32) for n in range(3))
     for other in partials[1:]:
@@ -256,58 +281,193 @@
         low = jnp.minimum(low, other[2].astype(F32))
     scale = jnp.where(mine > 0.0, 1.0 / (visit_total - 3.0), 1.0 / (visit_total - 2.0))
     coadd[...] = ((total - high - low) * scale).astype(BF)
+    share[...] = coadd[pl.ds(pl.multiple_of(band * some, some), some), :]
     start = pl.multiple_of(jnp.where(visit == 0, 0, part - margin), margin)
     edge[...] = coadd[pl.ds(start, margin), :]
 
 
-def filter_body(visits, margin, bands, *refs):
-    pieces, halos = refs[:visits], refs[visits : visits + 2]
-    out, image, moved = refs[visits + 2 :]
+def shifted(image, margin, taps, side, first, until):
+    rows, width = image.shape
+    lane = iota((rows, side), 1)
+    blank = jnp.zeros((rows, side), BF)
+    shifts = []
+    for dx in range(taps):
+        shift = dx - margin
+        low, high = (first - 1, until) if shift < 0 else (first, until + 1)
+        turned = {
+            t: pltpu.roll(image[:, t * side : (t + 1) * side], -shift % side, 1)
+            if 0 <= t < width // side
+            else blank
+            for t in range(low, high)
+        } if shift else {}
+        tiles = []
+        for t in range(first, until):
+            if shift < 0:
+                tiles.append(jnp.where(lane < -shift, turned[t - 1], turned[t]))
+            elif shift > 0:
+                tiles.append(jnp.where(lane < side - shift, turned[t], turned[t + 1]))
+            else:
+                tiles.append(image[:, t * side : (t + 1) * side])
+        shifts.append(jnp.concatenate(tiles, axis=1))
+    return shifts
+
+
+def apply_rows(left, shifts, pick):
+    right = jnp.concatenate([pick(each) for each in shifts], axis=0)
+    return jnp.dot(left, right, preferred_element_type=F32)
+
+
+def collect_body(visits, visit_count, cap, *refs):
+    count = len(refs) - (visits - 1)
+    parcels, others = refs[:count], refs[count:]
+    each = count // (visits - 1)
+    part = others[0].shape[1]
+    for r, other in enumerate(others):
+        place(
+            parcels[r * each : (r + 1) * each],
+            cap,
+            part,
+            other,
+            lambda number: lax.rem(number, visit_count),
+        )
+
+
+def filter_ahead_body(margin, taps, side, per, bands, own, sums, image):
+    part, width = own.shape
+    block = 2 * margin
+    window = block + taps - 1
+    image[:margin] = jnp.zeros((margin, width), BF)
+    image[margin + part :] = jnp.zeros((margin, width), BF)
+    image[margin : margin + part] = own[...]
+    left = bands[:, : taps * window]
+    for t in range(0, width // side, per):
+        shifts = shifted(image, margin, taps, side, t, t + per)
+        for n in range(part // block):
+            rows = slice(n * block, n * block + window)
+            sums[n, :, t * side : (t + per) * side] = apply_rows(left, shifts, lambda x: x[rows])
+
+
+def joined(pieces, halos, place_piece):
     sky, visit, band = (lax.axis_index(name) for name in ("sky", "visit", "band"))
-    patches = lax.axis_size("sky")
-    part, width = pieces[0].shape
-    taps = moved.shape[0]
+    patches, visits = lax.axis_size("sky"), lax.axis_size("visit")
+    for n, piece in enumerate(pieces):
+        some = piece.shape[0]
+        place_piece(lax.rem(visit + 1 + n // 2, visits), lax.rem(band + n, 2) * some, piece[...])
     mine = lax.rem(visit, 2) == band
     below = jnp.where(mine, halos[0][...], halos[1][...])
     above = jnp.where(mine, halos[1][...], halos[0][...])
     below = jnp.where(sky == patches - 1, jnp.zeros_like(below), below)
     above = jnp.where(sky == 0, jnp.zeros_like(above), above)
-    image[:margin, :] = above
-    image[margin + visits * part :, :] = below
-    for r in range(visits):
-        start = pl.multiple_of(lax.rem(visit + r, visits) * part + margin, margin)
-        image[pl.ds(start, part), :] = pieces[r][...]
-    column = iota((image.shape[0], width), 1)
-    zero = jnp.zeros((), BF)
-    for dx in range(taps):
-        rolled = pltpu.roll(image[...], (margin - dx) % width, 1)
-        if dx < margin:
-            rolled = jnp.where(column >= margin - dx, rolled, zero)
-        elif dx > margin:
-            rolled = jnp.where(column < width + margin - dx, rolled, zero)
-        moved[dx] = rolled
-    blocks = out.shape[0]
-    block = visits * part // blocks
-    window = block + 2 * margin
-    step = min(256, width)
+    return above, below
+
+
+def render_body(
+    margin, taps, tile_cols, per, bands, ends, mixes, plane, sums, own, slab, others, *refs
+):
+    part, width = own.shape
+    pieces, halos, (out, result, sems, image) = refs[:-6], refs[-6:-4], refs[-4:]
+    block, step = 2 * margin, per * (width // tile_cols)
+    window, blocks = block + taps - 1, part // block
+    visit_count, side = result.shape[0], width // tile_cols
+    bases = bands.shape[0] // block
+    visit, band = lax.axis_index("visit"), lax.axis_index("band")
+    band_count = lax.axis_size("band")
+    first = visit == 0
+
+    def put(_, start, piece):
+        rows = pl.ds(pl.multiple_of(start + margin, margin), piece.shape[0])
+        image[rows, :] = piece
+
+    above, below = joined(pieces, halos, put)
+    image[:margin] = jnp.where(first, own[part - margin :, :], above)
+    image[margin + part : 2 * margin + part] = jnp.where(first, below, own[:margin, :])
+    image[2 * margin + part :] = jnp.where(first, above, below)
+    edge = slice(part + 2 * margin, part + 3 * margin)
+
+    def before(x):
+        return jnp.where(first, x[edge], x[part : part + margin])
+
+    def after(x):
+        return jnp.where(first, x[margin : 2 * margin], x[edge])
+
+    numbers = [
+        ((visit * band_count + band) * visit_count + j + 1).astype(F32)
+        for j in range(visit_count)
+    ]
     left = bands[:, : taps * window]
-    for n in range(blocks):
-        for c in range(0, width, step):
-            right = moved[:, n * block : n * block + window, c : c + step].reshape(taps * window, step)
-            out[n, :, c : c + step] = jnp.dot(left, right, preferred_element_type=F32).astype(BF)
+
+    def finish(start, n, c, source, value):
+        value = value.astype(BF).astype(F32)
+        rows = pl.ds(pl.multiple_of(start + n * block, block), block)
+        for t in range(c * step // side, (c + 1) * step // side):
+            cols = slice(t * side, (t + 1) * side)
+            inset = slice(t * side - c * step, (t + 1) * side - c * step)
+            planes = [value[b * block : (b + 1) * block, inset] for b in range(bases)]
+            bad = plane[rows, cols]
+            for j in range(visit_count):
+                row = (j * tile_cols + t) * bases
+                template = sum(mixes[row + b : row + b + 1, :] * planes[b] for b in range(bases))
+                pixels = source[j, n * block : (n + 1) * block, cols].astype(F32) - template
+                result[j, rows, cols] = jnp.where(bad == numbers[j], 0.0, pixels).astype(BF)
+
+    copies = []
+    for c in range(width // step):
+        cols = slice(c * step, (c + 1) * step)
+        shifts = shifted(image, margin, taps, side, c * per, (c + 1) * per)
+        for n in range(blocks):
+            rows = slice(n * block, n * block + window)
+            value = apply_rows(left, shifts, lambda x: x[rows])
+            finish((1 - visit) * part, n, c, others, value)
+        for n in range(blocks):
+            value = sums[n, :, cols]
+            if n == 0:
+                value += apply_rows(ends[0, :, : taps * margin], shifts, before)
+            if n == blocks - 1:
+                value += apply_rows(ends[1, :, : taps * margin], shifts, after)
+            finish(visit * part, n, c, slab, value)
+        copies.append(
+            pltpu.make_async_copy(result.at[:, :, cols], out.at[:, :, cols], sems.at[c])
+        )
+        copies[-1].start()
+    for copy in copies:
+        copy.wait()
+
+
+def filter_body(margin, taps, side, per, bands, own, *refs):
+    pieces, halos, (out, image) = refs[:-4], refs[-4:-2], refs[-2:]
+    part, width = own.shape
+    block = 2 * margin
+    window = block + taps - 1
+
+    def put(turn, start, piece):
+        start = pl.multiple_of(turn * part + start + margin, margin)
+        image[pl.ds(start, piece.shape[0])] = piece
+
+    above, below = joined(pieces, halos, put)
+    image[:margin] = above
+    image[image.shape[0] - margin :] = below
+    put(lax.axis_index("visit"), 0, own[...])
+    for t in range(0, width // side, per):
+        shifts = shifted(image, margin, taps, side, t, t + per)
+        for n in range(out.shape[0]):
+            rows = slice(n * block, n * block + window)
+            value = apply_rows(bands[:, : taps * window], shifts, lambda x: x[rows])
+            out[n, :, t * side : (t + per) * side] = value.astype(BF)
 
 
 def finish_body(visits, bands, tile_cols, mixes, filtered, plane, *refs):
-    slabs, (out, image, result, sems) = refs[:visits], refs[visits:]
+    slabs, (out, image, result, sems) = refs[:-4], refs[-4:]
     visit, band = lax.axis_index("visit"), lax.axis_index("band")
-    visit_count, part, width = slabs[0].shape
+    part, width = slabs[0].shape[1:]
+    visit_count = image.shape[0]
     blocks = filtered.shape[0]
     bases = mixes.shape[0] // (visit_count * tile_cols)
     block = filtered.shape[1] // bases
     side = width // tile_cols
     for r in range(visits):
         start = pl.multiple_of(lax.rem(visit + r, visits) * part, part)
-        image[:, pl.ds(start, part), :] = slabs[r][...]
+        for j in range(visit_count):
+            image[j, pl.ds(start, part), :] = slabs[r][j]
     numbers = [
         ((visit * bands + band) * visit_count + j + 1).astype(F32) for j in range(visit_count)
     ]
@@ -355,8 +515,8 @@
         patches, visits, cap, raw_tiles, pixel_offsets, shift_entry_index, shift_table, tile_routes
     )
     far = sorted(range(patches), key=lambda k: (-min(k, patches - k), -k))
-    order = [k * visits + r for k in far for r in reversed(range(visits)) if k + r > 0]
-    arrived = [parcels[0]]
+    order = [k * visits + r for r in reversed(range(visits)) for k in far if k + r > 0]
+    arrived = {0: parcels[0]}
     for n in order:
         k, r = divmod(n, visits)
         pairs = [
@@ -364,19 +524,30 @@
             for s in range(patches)
             for v in range(visits)
         ]
-        arrived.append(lax.ppermute(parcels[n], ("sky", "visit"), pairs))
-    plane, toeplitz, mixes = make_tables(
+        arrived[n] = lax.ppermute(parcels[n], ("sky", "visit"), pairs)
+    own_others = []
+    for r in range(1, visits):
+        own_others.append(parcels[r])
+        for k in (k for k in far if k > 0):
+            own_others.append(
+                lax.ppermute(
+                    arrived[k * visits + r], "visit", [(v, (v - r) % visits) for v in range(visits)]
+                )
+            )
+    plane, toeplitz, mixes, ends = make_tables(
         basis_choice, coef_table, bad_pixels, basis_kernels, side, block
     )
-    slabs, partial = land_tiles(visits, bands, visit_count, cap, tile_cols, plane, arrived)
+    slab, partial = land_tiles(
+        visits, bands, visit_count, cap, tile_cols, plane, list(arrived.values())
+    )
 
     partials = [partial] + [
         lax.ppermute(partial, "band", [(b, (b + q) % bands) for b in range(bands)])
         for q in range(1, bands)
     ]
-    coadd, edge = kernel_call(
+    coadd, share, edge = kernel_call(
         functools.partial(coadd_body, visit_total, margin),
-        [jax.ShapeDtypeStruct((part, width), BF), jax.ShapeDtypeStruct((margin, width), BF)],
+        [jax.ShapeDtypeStruct((rows, width), BF) for rows in (part, part // bands, margin)],
         [VMEM] * (1 + bands),
         flops=8 * part * width,
         data=8 * part * width,
@@ -385,7 +556,11 @@
     def turn(r):
         return [(v, (v - r) % visits) for v in range(visits)]
 
-    pieces = [coadd] + [lax.ppermute(coadd, "visit", turn(r)) for r in range(1, visits)]
+    swap = [(b, (b + 1) % bands) for b in range(bands)]
+    pieces = []
+    for r in range(1, visits):
+        pieces.append(lax.ppermute(share, "visit", turn(r)))
+        pieces.append(lax.ppermute(pieces[-1], "band", swap))
     halos = []
     for first in range(0, visits, bands):
         pairs = []
@@ -397,36 +572,63 @@
                 pairs.append(((s * visits + v) * bands + b, (to_s * visits + to_v) * bands + b))
         halos.append(lax.ppermute(edge, ("sky", "visit", "band"), pairs))
     halo = functools.reduce(jnp.add, halos)
-    halos = [halo, lax.ppermute(halo, "band", [(b, (b + 1) % bands) for b in range(bands)])]
-    own = [slabs[0]] + [
-        lax.ppermute(slabs[r], "visit", [(v, (v + r) % visits) for v in range(visits)])
-        for r in range(1, visits)
-    ]
-    own = [own[0]] + [own[visits - r] for r in range(1, visits)]
+    halos = [halo, lax.ppermute(halo, "band", swap)]
+    others = kernel_call(
+        functools.partial(collect_body, visits, visit_count, cap),
+        [jax.ShapeDtypeStruct((visit_count + 1, part, width), BF)] * (visits - 1),
+        [VMEM] * len(own_others),
+        flops=part * width,
+        data=4 * visit_count * side * width,
+    )(*own_others)
+    work = 2 * bases * side * width * taps * (block + taps - 1)
+    per = tile_cols
+    result = jax.ShapeDtypeStruct((visit_count, side, width), BF)
+    if visits == 2 and part % block == 0:
+        sums = kernel_call(
+            functools.partial(filter_ahead_body, margin, taps, side, per),
+            jax.ShapeDtypeStruct((part // block, bases * block, width), F32),
+            [VMEM] * 2,
+            [pltpu.VMEM((part + 2 * margin, width), BF)],
+            flops=work // 2,
+            data=4 * bases * part * width,
+            spare=24,
+        )(toeplitz, coadd)
+        return kernel_call(
+            functools.partial(render_body, margin, taps, tile_cols, per),
+            result,
+            [VMEM] * (8 + len(pieces) + 2),
+            [
+                pltpu.VMEM(result.shape, BF),
+                pltpu.SemaphoreType.DMA((tile_cols // per,)),
+                pltpu.VMEM((part + 3 * margin, width), BF),
+            ],
+            flops=work // 2,
+            data=2 * bases * side * width,
+            spare=24,
+            out_specs=HBM,
+        )(toeplitz, ends, mixes, plane, sums, coadd, slab, *others, *pieces, *halos)
     filtered = kernel_call(
-        functools.partial(filter_body, visits, margin),
+        functools.partial(filter_body, margin, taps, side, per),
         jax.ShapeDtypeStruct((side // block, bases * block, width), BF),
+        [VMEM] * (2 + len(pieces) + 2),
+        [pltpu.VMEM((side + 2 * margin, width), BF)],
+        flops=work,
+        data=2 * bases * side * width,
+        spare=24,
+    )(toeplitz, coadd, *pieces, *halos)
+    return kernel_call(
+        functools.partial(finish_body, visits, bands, tile_cols),
+        result,
         [VMEM] * (3 + visits),
         [
-            pltpu.VMEM((side + 2 * margin, width), BF),
-            pltpu.VMEM((taps, side + 2 * margin, width), BF),
-        ],
-        flops=2 * bases * side * width * taps * (block + taps - 1),
-        data=2 * bases * side * width,
-    )(toeplitz, *pieces, *halos)
-    return kernel_call(
-        functools.partial(finish_body, visits, bands, tile_cols),
-        jax.ShapeDtypeStruct((visit_count, side, width), BF),
-        [VMEM] * (3 + visits),
-        [
-            pltpu.VMEM((visit_count, side, width), BF),
-            pltpu.VMEM((visit_count, side, width), BF),
+            pltpu.VMEM(result.shape, BF),
+            pltpu.VMEM(result.shape, BF),
             pltpu.SemaphoreType.DMA((side // block,)),
         ],
         flops=20 * visit_count * side * width,
         data=4 * visit_count * side * width,
         out_specs=HBM,
-    )(mixes, filtered, plane, *own)
+    )(mixes, filtered, plane, slab, *others)
 
 
 def solution(mesh):

time: 40.9 us -> 39 us (0.954); the launches traced: 40.7 us -> 38.4 us
  waiting for transfers between devices: 9.13 us -> 5.31 us
  Pallas kernels: 9.59 us -> 10.4 us
    ppermute x1, waiting for transfers between devices: 1.71 us -> 0.01 us  [on_device(): lax.ppermute(partial, 'band', [(b, (b + q) % bands) for b in range(bands)])]
    ppermute x1, waiting for transfers between devices: 1.6 us -> 0.25 us  [on_device(): halos.append(lax.ppermute(edge, ('sky', 'visit', 'band'), pairs))]
    pallas_call x6 -> x7, Pallas kernels: 9.59 us -> 10.4 us  [call(): pl.pallas_call(body, out_shape=outs, in_specs=in_specs, out_specs=places,...]
    ppermute x10 -> x13, waiting for transfers between devices: 5.82 us -> 5.06 us  [the longest x7 3.1 us: on_device(): arrived[n] = lax.ppermute(parcels[n], ('sky', 'visit'), pairs)]
    ppermute x1, starting transfers between devices: 2.76 us -> 3.46 us  [on_device(): halos.append(lax.ppermute(edge, ('sky', 'visit', 'band'), pairs))]
    ppermute x10 -> x13, starting transfers between devices: 18.1 us -> 17.7 us  [the longest x7 13.5 us: on_device(): arrived[n] = lax.ppermute(parcels[n], ('sky', 'visit'), pairs)]
    unnamed x9 -> x11, local copies, waits for them, and re-layouts: 0.83 us -> 1.02 us
  transfers between devices with their start and end apart: 12 -> 15, of which waited for: 5 -> 4; matrix products, arithmetic and copies ran while one was open for 1% -> 2% of each run, Pallas kernels for 11% -> 10%
where the time goes in v1:
time: 39 us; the launch traced here: 38.4 us
  starting transfers between devices  21.2 us (54%)
  Pallas kernels  10.4 us (27%)
  waiting for transfers between devices  5.31 us (14%)
  local copies, waits for them, and re-layouts  1.31 us (3%)
    ppermute x7, starting transfers between devices, on_device(): arrived[n] = lax.ppermute(parcels[n], ('sky', 'visit'), pairs)  13.5 us
    pallas_call x7, Pallas kernels, call(): pl.pallas_call(body, out_shape=outs, in_specs=in_specs, out_specs=places,...  10.4 us
    ppermute x1, starting transfers between devices, on_device(): halos.append(lax.ppermute(edge, ('sky', 'visit', 'band'), pairs))  3.46 us
    ppermute x7, waiting for transfers between devices, on_device(): arrived[n] = lax.ppermute(parcels[n], ('sky', 'visit'), pairs)  3.1 us
    ppermute x3, starting transfers between devices, on_device(): lax.ppermute(arrived[k * visits + r], 'visit', [(v, (v - r) % visits) for...  3.05 us
    ppermute x3, waiting for transfers between devices, on_device(): lax.ppermute(arrived[k * visits + r], 'visit', [(v, (v - r) % visits) for...  1.18 us
    ppermute x1, starting transfers between devices, on_device(): pieces.append(lax.ppermute(share, 'visit', turn(r)))  1.13 us
    unnamed x11, local copies, waits for them, and re-layouts  1.02 us
  transfers between devices with their start and end apart: 15, of which 4 were waited for; matrix products, arithmetic and copies ran while one was open for 2% of the time, Pallas kernels for 10%

profile of v1, /device:TPU:0, one launch (start us, length us, event | category | flops | bytes accessed | tf_op | source)
XLA Modules:
  0.0 38.4 jit_solution(15114897982500846791)
XLA Ops:
  0.0 2.0 %shard_map.92 = (bf16[328,128]{1,0:T(8,128)(2,1)S(1)}, bf16[328,128]{1,0:T(8,128)(2,1)S(1)}, bf16[328,128]{1,0:T(8,128)(2,1)S(1)}, bf16[328,128]{1,0:T(8,128)(2,...) custom-call(s32[2,8]{1,0:T(2,128)} %refs_0_.1, ...), custom_call_target="tpu_custom_call" | custom-call | flops 134217728 | bytes 1048576 | tf_op jit(solution)/shard_map/pallas_call | solution.py:27
  2.0 5.1 %collective-permute-start = (bf16[328,128]{1,0:T(8,128)(2,1)S(1)}, bf16[328,128]{1,0:T(8,128)(2,1)S(1)}, u32[]{:S(2)}, u32[]{:S(2)}) collective-permute-start(bf16[328,128]{1,0:T(8,128)(2,1)S(1)} %get-tuple-element.27), channel_id=1, source_target_pairs={{0,10},{2,8},{4,14},{6,12},{8,2},{10,0},{12,6},{14,4},{1,11},{3,9}... | collective-permute-start | bytes 251912 | tf_op jit(solution)/shard_map/ppermute | solution.py:527
  7.0 1.3 %collective-permute-start.1 = (bf16[328,128]{1,0:T(8,128)(2,1)S(1)}, bf16[328,128]{1,0:T(8,128)(2,1)S(1)}, u32[]{:S(2)}, u32[]{:S(2)}) collective-permute-start(bf16[328,128]{1,0:T(8,128)(2,1)S(1)} %get-tuple-element.28), channel_id=1, source_target_pairs={{0,14},{2,12},{4,2},{6,0},{8,6},{10,4},{12,10},{14,8},{1,15},{3,13... | collective-permute-start | bytes 251912 | tf_op jit(solution)/shard_map/ppermute | solution.py:527
  8.4 1.6 %collective-permute-start.2 = (bf16[328,128]{1,0:T(8,128)(2,1)S(1)}, bf16[328,128]{1,0:T(8,128)(2,1)S(1)}, u32[]{:S(2)}, u32[]{:S(2)}) collective-permute-start(bf16[328,128]{1,0:T(8,128)(2,1)S(1)} %get-tuple-element.29), channel_id=1, source_target_pairs={{0,6},{2,4},{4,10},{6,8},{8,14},{10,12},{12,2},{14,0},{1,7},{3,5},... | collective-permute-start | bytes 251912 | tf_op jit(solution)/shard_map/ppermute | solution.py:527
  10.0 0.3 collective-permute-start.4
  10.3 3.6 %collective-permute-start.5 = (bf16[328,128]{1,0:T(8,128)(2,1)S(1)}, bf16[328,128]{1,0:T(8,128)(2,1)S(1)}, u32[]{:S(2)}, u32[]{:S(2)}) collective-permute-start(bf16[328,128]{1,0:T(8,128)(2,1)S(1)} %get-tuple-element.32), channel_id=1, source_target_pairs={{0,12},{2,14},{4,0},{6,2},{8,4},{10,6},{12,8},{14,10},{1,13},{3,15... | collective-permute-start | bytes 251912 | tf_op jit(solution)/shard_map/ppermute | solution.py:527
  13.9 0.0 collective-permute-done.refs_1_
  13.9 0.5 %collective-permute-start.6 = (bf16[328,128]{1,0:T(8,128)(2,1)S(1)}, bf16[328,128]{1,0:T(8,128)(2,1)S(1)}, u32[]{:S(2)}, u32[]{:S(2)}) collective-permute-start(bf16[328,128]{1,0:T(8,128)(2,1)S(1)} %get-tuple-element.33), channel_id=1, source_target_pairs={{0,4},{2,6},{4,8},{6,10},{8,12},{10,14},{12,0},{14,2},{1,5},{3,7},... | collective-permute-start | bytes 251912 | tf_op jit(solution)/shard_map/ppermute | solution.py:527
  14.5 0.0 collective-permute-done.1.refs_2_
  14.5 1.0 %collective-permute-start.3 = (bf16[328,128]{1,0:T(8,128)(2,1)S(1)}, bf16[328,128]{1,0:T(8,128)(2,1)S(1)}, u32[]{:S(2)}, u32[]{:S(2)}) collective-permute-start(bf16[328,128]{1,0:T(8,128)(2,1)S(1)} %get-tuple-element.30.refs_0_), channel_id=1, source_target_pairs={{0,2},{2,0},{4,6},{6,4},{8,10},{10,8},{12,14},{14,12},{1,3},{3,1},... | collective-permute-start | bytes 251912 | tf_op jit(solution)/shard_map/ppermute | solution.py:527
  15.5 0.1 copy.16
  15.6 0.1 reshape.9.taps
  15.7 0.1 copy.18
  15.8 0.1 reshape.11.tails
  15.9 0.1 copy.17
  16.1 0.0 copy-start
  16.1 0.0 copy-start.1
  16.1 0.1 reshape.10.heads
  16.2 0.0 copy-start.2
  16.2 0.6 %copy-done = s32[8,8,32]{2,1,0:T(8,128)S(1)} copy-done((s32[8,8,32]{2,1,0:T(8,128)S(1)}, s32[8,8,32]{2,1,0:T(8,128)}, u32[]{:S(2)}) %copy-start) | copy-done | bytes 8216
  16.8 0.0 copy-done.2
  16.9 1.1 %shard_map.91 = (f32[128,1024]{1,0:T(8,128)S(1)}, bf16[128,2176]{1,0:T(8,128)(2,1)S(1)}, f32[64,128]{1,0:T(8,128)S(1)}, bf16[2,128,640]{2,1,0:T(8,128)(2,1)S(1)}) custom-call(s32[2,8]{1,0:T(2,128)S(1)} %copy-done.2, f32[4,16]{1,0:T(4,128)S(1)} %bitcast.5, s32[8,8,32]{2,1,0:T(8,128)S(1)} %copy-done, f32[4,17,128]{2,1,0:T(8,128)S(1)} %reshape.9.taps, ...), custom_call_target="tpu_custom_call" | custom-call | flops 67108864 | bytes 524288 | tf_op jit(solution)/shard_map/pallas_call | solution.py:27
  17.9 0.0 collective-permute-done.2.refs_3_
  17.9 3.1 %collective-permute-done.4.refs_5_ = bf16[328,128]{1,0:T(8,128)(2,1)S(1)} collective-permute-done((bf16[328,128]{1,0:T(8,128)(2,1)S(1)}, bf16[328,128]{1,0:T(8,128)(2,1)S(1)}, u32[]{:S(2)}, u32[]{:S(2)}) %collective-permute-start.4) | collective-permute-done | bytes 84000 | tf_op jit(solution)/shard_map/ppermute | solution.py:527
  21.0 0.0 collective-permute-done.5.refs_6_
  21.0 0.0 collective-permute-done.6.refs_7_
  21.0 0.0 collective-permute-done.3.refs_4_
  21.0 0.8 %shard_map.93 = (bf16[2,64,1024]{2,1,0:T(8,128)(2,1)S(1)}, bf16[3,64,1024]{2,1,0:T(8,128)(2,1)S(1)}) custom-call(f32[128,1024]{1,0:T(8,128)S(1)} %get-tuple-element.25.plane, bf16[328,128]{1,0:T(8,128)(2,1)S(1)} %get-tuple-element.26.refs_0_, bf16[328,128]{1,0:T(8,128)(2,1)S(1)} %collective-permute-done.refs_1_, ...), custom_call_target="tpu_custom_call" | custom-call | flops 2621440 | bytes 1048576 | tf_op jit(solution)/shard_map/pallas_call | solution.py:27
  21.9 0.1 collective-permute-start.7
  21.9 1.0 %collective-permute-start.8 = (bf16[328,128]{1,0:T(8,128)(2,1)S(1)}, bf16[328,128]{1,0:T(8,128)(2,1)S(1)}, u32[]{:S(2)}, u32[]{:S(2)}) collective-permute-start(bf16[328,128]{1,0:T(8,128)(2,1)S(1)} %collective-permute-done.refs_1_), channel_id=1, source_target_pairs={{0,2},{2,0},{1,3},{3,1},{4,6},{6,4},{5,7},{7,5},{8,10},{10,8},{9,1... | collective-permute-start | bytes 251912 | tf_op jit(solution)/shard_map/ppermute | solution.py:533
  23.0 1.1 %collective-permute-start.9 = (bf16[328,128]{1,0:T(8,128)(2,1)S(1)}, bf16[328,128]{1,0:T(8,128)(2,1)S(1)}, u32[]{:S(2)}, u32[]{:S(2)}) collective-permute-start(bf16[328,128]{1,0:T(8,128)(2,1)S(1)} %collective-permute-done.1.refs_2_), channel_id=1, source_target_pairs={{0,2},{2,0},{1,3},{3,1},{4,6},{6,4},{5,7},{7,5},{8,10},{10,8},{9,1... | collective-permute-start | bytes 251912 | tf_op jit(solution)/shard_map/ppermute | solution.py:533
  24.0 1.0 %collective-permute-start.10 = (bf16[328,128]{1,0:T(8,128)(2,1)S(1)}, bf16[328,128]{1,0:T(8,128)(2,1)S(1)}, u32[]{:S(2)}, u32[]{:S(2)}) collective-permute-start(bf16[328,128]{1,0:T(8,128)(2,1)S(1)} %collective-permute-done.2.refs_3_), channel_id=1, source_target_pairs={{0,2},{2,0},{1,3},{3,1},{4,6},{6,4},{5,7},{7,5},{8,10},{10,8},{9,1... | collective-permute-start | bytes 251912 | tf_op jit(solution)/shard_map/ppermute | solution.py:533
  25.0 0.0 collective-permute-done.7.refs_1_
  25.0 0.2 shard_map.94
  25.2 1.1 %collective-permute-start.11 = (bf16[32,1024]{1,0:T(8,128)(2,1)S(1)}, bf16[32,1024]{1,0:T(8,128)(2,1)S(1)}, u32[]{:S(2)}, u32[]{:S(2)}) collective-permute-start(bf16[32,1024]{1,0:T(8,128)(2,1)S(1)} %get-tuple-element.37), channel_id=1, source_target_pairs={{0,2},{2,0},{1,3},{3,1},{4,6},{6,4},{5,7},{7,5},{8,10},{10,8},{9,1... | collective-permute-start | bytes 196616 | tf_op jit(solution)/shard_map/ppermute | solution.py:562
  26.3 3.5 %collective-permute-start.13 = (bf16[16,1024]{1,0:T(8,128)(2,1)S(1)}, bf16[16,1024]{1,0:T(8,128)(2,1)S(1)}, u32[]{:S(2)}, u32[]{:S(2)}) collective-permute-start(bf16[16,1024]{1,0:T(8,128)(2,1)S(1)} %get-tuple-element.38), channel_id=1, source_target_pairs={{0,12},{2,6},{1,15},{3,5},{4,0},{6,10},{5,3},{7,9},{8,4},{10,14},{... | collective-permute-start | bytes 98312 | tf_op jit(solution)/shard_map/ppermute | solution.py:573
  29.8 0.0 collective-permute-done.8.refs_1_
  29.8 0.0 collective-permute-done.9.refs_2_
  29.8 1.2 %collective-permute-done.10.refs_3_ = bf16[328,128]{1,0:T(8,128)(2,1)S(1)} collective-permute-done((bf16[328,128]{1,0:T(8,128)(2,1)S(1)}, bf16[328,128]{1,0:T(8,128)(2,1)S(1)}, u32[]{:S(2)}, u32[]{:S(2)}) %collective-permute-start.10) | collective-permute-done | bytes 84000 | tf_op jit(solution)/shard_map/ppermute | solution.py:533
  31.0 0.2 shard_map.96.others
  31.2 0.2 collective-permute-done.13.refs_2_
  31.4 0.0 collective-permute-start.14
  31.4 0.8 %collective-permute-done.11.refs_0_ = bf16[32,1024]{1,0:T(8,128)(2,1)S(1)} collective-permute-done((bf16[32,1024]{1,0:T(8,128)(2,1)S(1)}, bf16[32,1024]{1,0:T(8,128)(2,1)S(1)}, u32[]{:S(2)}, u32[]{:S(2)}) %collective-permute-start.11) | collective-permute-done | bytes 65568 | tf_op jit(solution)/shard_map/ppermute | solution.py:562
  32.2 0.0 collective-permute-start.12
  32.2 2.3 %shard_map.95.sums = f32[2,128,1024]{2,1,0:T(8,128)S(1)} custom-call(bf16[128,2176]{1,0:T(8,128)(2,1)S(1)} %get-tuple-element.22.bands, bf16[64,1024]{1,0:T(8,128)(2,1)S(1)} %get-tuple-element.35.own), custom_call_target="tpu_custom_call" | custom-call | flops 1107296256 | bytes 1048576 | tf_op jit(solution)/shard_map/pallas_call | solution.py:27
  34.5 0.0 collective-permute-done.14.refs_3_
  34.5 0.0 collective-permute-done.12.refs_1_
  34.5 3.9 %shard_map.97 = bf16[2,128,1024]{2,1,0:T(8,128)(2,1)} custom-call(bf16[128,2176]{1,0:T(8,128)(2,1)S(1)} %get-tuple-element.22.bands, bf16[2,128,640]{2,1,0:T(8,128)(2,1)S(1)} %get-tuple-element.23.ends, f32[64,128]{1,0:T(8,128)S(1)} %get-tuple-element.24.mixes, f32[128,1024]{1,0:T(8,128)S(1)} %get-tuple-element.25.plane, ...), custom_call_target="tpu_custom_call" | custom-call | flops 1107296256 | bytes 1048576 | tf_op jit(solution)/shard_map/pallas_call | solution.py:27
  (8 shorter events, 0.1 us)
Async XLA Ops:
  0.0 13.9 %copy-start.3 = (bf16[4,33,33]{2,0,1:T(4,128)(2,1)S(1)}, bf16[4,33,33]{2,0,1:T(4,128)(2,1)}, u32[]{:S(2)}) copy-start(bf16[4,33,33]{2,0,1:T(4,128)(2,1)} %param.15) | copy-start | bytes 26140
  2.0 11.9 %collective-permute-start = (bf16[328,128]{1,0:T(8,128)(2,1)S(1)}, bf16[328,128]{1,0:T(8,128)(2,1)S(1)}, u32[]{:S(2)}, u32[]{:S(2)}) collective-permute-start(bf16[328,128]{1,0:T(8,128)(2,1)S(1)} %get-tuple-element.27), channel_id=1, source_target_pairs={{0,10},{2,8},{4,14},{6,12},{8,2},{10,0},{12,6},{14,4},{1,11},{3,9}... | collective-permute-start | bytes 251912 | tf_op jit(solution)/shard_map/ppermute | solution.py:527
  7.0 7.4 %collective-permute-start.1 = (bf16[328,128]{1,0:T(8,128)(2,1)S(1)}, bf16[328,128]{1,0:T(8,128)(2,1)S(1)}, u32[]{:S(2)}, u32[]{:S(2)}) collective-permute-start(bf16[328,128]{1,0:T(8,128)(2,1)S(1)} %get-tuple-element.28), channel_id=1, source_target_pairs={{0,14},{2,12},{4,2},{6,0},{8,6},{10,4},{12,10},{14,8},{1,15},{3,13... | collective-permute-start | bytes 251912 | tf_op jit(solution)/shard_map/ppermute | solution.py:527
  8.4 9.6 %collective-permute-start.2 = (bf16[328,128]{1,0:T(8,128)(2,1)S(1)}, bf16[328,128]{1,0:T(8,128)(2,1)S(1)}, u32[]{:S(2)}, u32[]{:S(2)}) collective-permute-start(bf16[328,128]{1,0:T(8,128)(2,1)S(1)} %get-tuple-element.29), channel_id=1, source_target_pairs={{0,6},{2,4},{4,10},{6,8},{8,14},{10,12},{12,2},{14,0},{1,7},{3,5},... | collective-permute-start | bytes 251912 | tf_op jit(solution)/shard_map/ppermute | solution.py:527
  10.0 11.1 %collective-permute-start.4 = (bf16[328,128]{1,0:T(8,128)(2,1)S(1)}, bf16[328,128]{1,0:T(8,128)(2,1)S(1)}, u32[]{:S(2)}, u32[]{:S(2)}) collective-permute-start(bf16[328,128]{1,0:T(8,128)(2,1)S(1)} %get-tuple-element.31), channel_id=1, source_target_pairs={{0,8},{2,10},{4,12},{6,14},{8,0},{10,2},{12,4},{14,6},{1,9},{3,11}... | collective-permute-start | bytes 251912 | tf_op jit(solution)/shard_map/ppermute | solution.py:527
  10.3 10.7 %collective-permute-start.5 = (bf16[328,128]{1,0:T(8,128)(2,1)S(1)}, bf16[328,128]{1,0:T(8,128)(2,1)S(1)}, u32[]{:S(2)}, u32[]{:S(2)}) collective-permute-start(bf16[328,128]{1,0:T(8,128)(2,1)S(1)} %get-tuple-element.32), channel_id=1, source_target_pairs={{0,12},{2,14},{4,0},{6,2},{8,4},{10,6},{12,8},{14,10},{1,13},{3,15... | collective-permute-start | bytes 251912 | tf_op jit(solution)/shard_map/ppermute | solution.py:527
  13.9 7.1 %collective-permute-start.6 = (bf16[328,128]{1,0:T(8,128)(2,1)S(1)}, bf16[328,128]{1,0:T(8,128)(2,1)S(1)}, u32[]{:S(2)}, u32[]{:S(2)}) collective-permute-start(bf16[328,128]{1,0:T(8,128)(2,1)S(1)} %get-tuple-element.33), channel_id=1, source_target_pairs={{0,4},{2,6},{4,8},{6,10},{8,12},{10,14},{12,0},{14,2},{1,5},{3,7},... | collective-permute-start | bytes 251912 | tf_op jit(solution)/shard_map/ppermute | solution.py:527
  14.5 6.6 %collective-permute-start.3 = (bf16[328,128]{1,0:T(8,128)(2,1)S(1)}, bf16[328,128]{1,0:T(8,128)(2,1)S(1)}, u32[]{:S(2)}, u32[]{:S(2)}) collective-permute-start(bf16[328,128]{1,0:T(8,128)(2,1)S(1)} %get-tuple-element.30.refs_0_), channel_id=1, source_target_pairs={{0,2},{2,0},{4,6},{6,4},{8,10},{10,8},{12,14},{14,12},{1,3},{3,1},... | collective-permute-start | bytes 251912 | tf_op jit(solution)/shard_map/ppermute | solution.py:527
  16.1 0.8 %copy-start = (s32[8,8,32]{2,1,0:T(8,128)S(1)}, s32[8,8,32]{2,1,0:T(8,128)}, u32[]{:S(2)}) copy-start(s32[8,8,32]{2,1,0:T(8,128)} %listed.1) | copy-start | bytes 24580
  16.1 0.8 %copy-start.1 = (f32[16,4]{0,1:T(4,128)S(1)}, f32[16,4]{0,1:T(4,128)}, u32[]{:S(2)}) copy-start(f32[16,4]{0,1:T(4,128)} %param.17) | copy-start | bytes 772
  16.2 0.7 %copy-start.2 = (s32[2,8]{1,0:T(2,128)S(1)}, s32[2,8]{1,0:T(2,128)}, u32[]{:S(2)}) copy-start(s32[2,8]{1,0:T(2,128)} %choice.1) | copy-start | bytes 196
  21.9 3.1 %collective-permute-start.7 = (bf16[3,64,1024]{2,1,0:T(8,128)(2,1)S(1)}, bf16[3,64,1024]{2,1,0:T(8,128)(2,1)S(1)}, u32[]{:S(2)}, u32[]{:S(2)}) collective-permute-start(bf16[3,64,1024]{2,1,0:T(8,128)(2,1)S(1)} %get-tuple-element.34.refs_0_), channel_id=1, source_target_pairs={{0,1},{1,0},{2,3},{3,2},{4,5},{5,4},{6,7},{7,6},{8,9},{9,8},{10,11... | collective-permute-start | bytes 1179656 | tf_op jit(solution)/shard_map/ppermute | solution.py:545
  21.9 7.9 %collective-permute-start.8 = (bf16[328,128]{1,0:T(8,128)(2,1)S(1)}, bf16[328,128]{1,0:T(8,128)(2,1)S(1)}, u32[]{:S(2)}, u32[]{:S(2)}) collective-permute-start(bf16[328,128]{1,0:T(8,128)(2,1)S(1)} %collective-permute-done.refs_1_), channel_id=1, source_target_pairs={{0,2},{2,0},{1,3},{3,1},{4,6},{6,4},{5,7},{7,5},{8,10},{10,8},{9,1... | collective-permute-start | bytes 251912 | tf_op jit(solution)/shard_map/ppermute | solution.py:533
  23.0 6.8 %collective-permute-start.9 = (bf16[328,128]{1,0:T(8,128)(2,1)S(1)}, bf16[328,128]{1,0:T(8,128)(2,1)S(1)}, u32[]{:S(2)}, u32[]{:S(2)}) collective-permute-start(bf16[328,128]{1,0:T(8,128)(2,1)S(1)} %collective-permute-done.1.refs_2_), channel_id=1, source_target_pairs={{0,2},{2,0},{1,3},{3,1},{4,6},{6,4},{5,7},{7,5},{8,10},{10,8},{9,1... | collective-permute-start | bytes 251912 | tf_op jit(solution)/shard_map/ppermute | solution.py:533
  24.0 6.9 %collective-permute-start.10 = (bf16[328,128]{1,0:T(8,128)(2,1)S(1)}, bf16[328,128]{1,0:T(8,128)(2,1)S(1)}, u32[]{:S(2)}, u32[]{:S(2)}) collective-permute-start(bf16[328,128]{1,0:T(8,128)(2,1)S(1)} %collective-permute-done.2.refs_3_), channel_id=1, source_target_pairs={{0,2},{2,0},{1,3},{3,1},{4,6},{6,4},{5,7},{7,5},{8,10},{10,8},{9,1... | collective-permute-start | bytes 251912 | tf_op jit(solution)/shard_map/ppermute | solution.py:533
  25.2 7.0 %collective-permute-start.11 = (bf16[32,1024]{1,0:T(8,128)(2,1)S(1)}, bf16[32,1024]{1,0:T(8,128)(2,1)S(1)}, u32[]{:S(2)}, u32[]{:S(2)}) collective-permute-start(bf16[32,1024]{1,0:T(8,128)(2,1)S(1)} %get-tuple-element.37), channel_id=1, source_target_pairs={{0,2},{2,0},{1,3},{3,1},{4,6},{6,4},{5,7},{7,5},{8,10},{10,8},{9,1... | collective-permute-start | bytes 196616 | tf_op jit(solution)/shard_map/ppermute | solution.py:562
  26.3 5.1 %collective-permute-start.13 = (bf16[16,1024]{1,0:T(8,128)(2,1)S(1)}, bf16[16,1024]{1,0:T(8,128)(2,1)S(1)}, u32[]{:S(2)}, u32[]{:S(2)}) collective-permute-start(bf16[16,1024]{1,0:T(8,128)(2,1)S(1)} %get-tuple-element.38), channel_id=1, source_target_pairs={{0,12},{2,6},{1,15},{3,5},{4,0},{6,10},{5,3},{7,9},{8,4},{10,14},{... | collective-permute-start | bytes 98312 | tf_op jit(solution)/shard_map/ppermute | solution.py:573
  31.4 3.1 %collective-permute-start.14 = (bf16[16,1024]{1,0:T(8,128)(2,1)S(1)}, bf16[16,1024]{1,0:T(8,128)(2,1)S(1)}, u32[]{:S(2)}, u32[]{:S(2)}) collective-permute-start(bf16[16,1024]{1,0:T(8,128)(2,1)S(1)} %collective-permute-done.13.refs_2_), channel_id=1, source_target_pairs={{0,1},{1,0},{2,3},{3,2},{4,5},{5,4},{6,7},{7,6},{8,9},{9,8},{10,11... | collective-permute-start | bytes 98312 | tf_op jit(solution)/shard_map/ppermute | solution.py:575
  32.2 2.3 %collective-permute-start.12 = (bf16[32,1024]{1,0:T(8,128)(2,1)S(1)}, bf16[32,1024]{1,0:T(8,128)(2,1)S(1)}, u32[]{:S(2)}, u32[]{:S(2)}) collective-permute-start(bf16[32,1024]{1,0:T(8,128)(2,1)S(1)} %collective-permute-done.11.refs_0_), channel_id=1, source_target_pairs={{0,1},{1,0},{2,3},{3,2},{4,5},{5,4},{6,7},{7,6},{8,9},{9,8},{10,11... | collective-permute-start | bytes 196616 | tf_op jit(solution)/shard_map/ppermute | solution.py:563

commit v2 on v1

--- a/solution.py
+++ b/solution.py
@@ -233,21 +233,25 @@
     held = visits * visit_count
     visit, band = lax.axis_index("visit"), lax.axis_index("band")
     place(parcels, cap, part, image, lambda number: number)
-    mine = plane[pl.ds(pl.multiple_of(visit * part, part), part), :]
-    total = jnp.zeros(mine.shape, F32)
-    high = jnp.full(mine.shape, -jnp.inf, F32)
-    low = jnp.full(mine.shape, jnp.inf, F32)
-    for n in range(held):
-        own, local = divmod(n, visit_count)
-        number = ((own * bands + band) * visit_count + local + 1).astype(F32)
-        value = image[n].astype(F32)
-        bad = mine == number
-        total = total + jnp.where(bad, 0.0, value)
-        high = jnp.maximum(high, jnp.where(bad, -jnp.inf, value))
-        low = jnp.minimum(low, jnp.where(bad, jnp.inf, value))
-    partial[0] = total.astype(BF)
-    partial[1] = high.astype(BF)
-    partial[2] = low.astype(BF)
+    rows = pl.ds(pl.multiple_of(visit * part, part), part)
+    side = parcels[0].shape[1]
+    for start in range(0, image.shape[2], side):
+        cols = slice(start, start + side)
+        mine = plane[rows, cols]
+        total = jnp.zeros(mine.shape, F32)
+        high = jnp.full(mine.shape, -jnp.inf, F32)
+        low = jnp.full(mine.shape, jnp.inf, F32)
+        for n in range(held):
+            own, local = divmod(n, visit_count)
+            number = ((own * bands + band) * visit_count + local + 1).astype(F32)
+            value = image[n, :, cols].astype(F32)
+            bad = mine == number
+            total = total + jnp.where(bad, 0.0, value)
+            high = jnp.maximum(high, jnp.where(bad, -jnp.inf, value))
+            low = jnp.minimum(low, jnp.where(bad, jnp.inf, value))
+        partial[0, :, cols] = total.astype(BF)
+        partial[1, :, cols] = high.astype(BF)
+        partial[2, :, cols] = low.astype(BF)
     for j in range(visit_count):
         slab[j] = image[visit * visit_count + j]
 
@@ -273,29 +277,35 @@
     partials, (coadd, share, edge) = refs[:-3], refs[-3:]
     part, some = coadd.shape[0], share.shape[0]
     visit, band = lax.axis_index("visit"), lax.axis_index("band")
-    mine = plane[pl.ds(pl.multiple_of(visit * part, part), part), :]
-    total, high, low = (partials[0][n].astype(F32) for n in range(3))
-    for other in partials[1:]:
-        total = total + other[0].astype(F32)
-        high = jnp.maximum(high, other[1].astype(F32))
-        low = jnp.minimum(low, other[2].astype(F32))
-    scale = jnp.where(mine > 0.0, 1.0 / (visit_total - 3.0), 1.0 / (visit_total - 2.0))
-    coadd[...] = ((total - high - low) * scale).astype(BF)
+    rows = pl.ds(pl.multiple_of(visit * part, part), part)
+    width = coadd.shape[1]
+    step = math.gcd(128, width)
+    for first in range(0, width, step):
+        cols = slice(first, first + step)
+        total, high, low = (partials[0][n, :, cols].astype(F32) for n in range(3))
+        for other in partials[1:]:
+            total = total + other[0, :, cols].astype(F32)
+            high = jnp.maximum(high, other[1, :, cols].astype(F32))
+            low = jnp.minimum(low, other[2, :, cols].astype(F32))
+        scale = jnp.where(
+            plane[rows, cols] > 0.0, 1.0 / (visit_total - 3.0), 1.0 / (visit_total - 2.0)
+        )
+        coadd[:, cols] = ((total - high - low) * scale).astype(BF)
     share[...] = coadd[pl.ds(pl.multiple_of(band * some, some), some), :]
     start = pl.multiple_of(jnp.where(visit == 0, 0, part - margin), margin)
     edge[...] = coadd[pl.ds(start, margin), :]
 
 
-def shifted(image, margin, taps, side, first, until):
-    rows, width = image.shape
-    lane = iota((rows, side), 1)
-    blank = jnp.zeros((rows, side), BF)
+def shifted(image, rows, margin, taps, side, first, until):
+    width, height = image.shape[1], rows.stop - rows.start
+    lane = iota((height, side), 1)
+    blank = jnp.zeros((height, side), BF)
     shifts = []
     for dx in range(taps):
         shift = dx - margin
         low, high = (first - 1, until) if shift < 0 else (first, until + 1)
         turned = {
-            t: pltpu.roll(image[:, t * side : (t + 1) * side], -shift % side, 1)
+            t: pltpu.roll(image[rows, t * side : (t + 1) * side], -shift % side, 1)
             if 0 <= t < width // side
             else blank
             for t in range(low, high)
@@ -307,13 +317,13 @@
             elif shift > 0:
                 tiles.append(jnp.where(lane < side - shift, turned[t], turned[t + 1]))
             else:
-                tiles.append(image[:, t * side : (t + 1) * side])
+                tiles.append(image[rows, t * side : (t + 1) * side])
         shifts.append(jnp.concatenate(tiles, axis=1))
     return shifts
 
 
 def apply_rows(left, shifts, pick):
-    right = jnp.concatenate([pick(each) for each in shifts], axis=0)
+    right = jnp.concatenate([pick(dx, each) for dx, each in enumerate(shifts)], axis=0)
     return jnp.dot(left, right, preferred_element_type=F32)
 
 
@@ -332,19 +342,21 @@
         )
 
 
-def filter_ahead_body(margin, taps, side, per, bands, own, sums, image):
+def filter_ahead_body(margin, taps, side, per, low, bands, own, sums, edge):
     part, width = own.shape
-    block = 2 * margin
-    window = block + taps - 1
-    image[:margin] = jnp.zeros((margin, width), BF)
-    image[margin + part :] = jnp.zeros((margin, width), BF)
-    image[margin : margin + part] = own[...]
+    window = 2 * margin + taps - 1
     left = bands[:, : taps * window]
+    rows = slice(0, window - margin) if low else slice(part - window + margin, part)
+    outer = slice(0, margin) if low else slice(window - 2 * margin, window - margin)
+    blank = jnp.zeros((margin, per * side), BF)
     for t in range(0, width // side, per):
-        shifts = shifted(image, margin, taps, side, t, t + per)
-        for n in range(part // block):
-            rows = slice(n * block, n * block + window)
-            sums[n, :, t * side : (t + per) * side] = apply_rows(left, shifts, lambda x: x[rows])
+        cols = slice(t * side, (t + per) * side)
+        shifts = shifted(own, rows, margin, taps, side, t, t + per)
+        sums[:, cols] = apply_rows(
+            left, shifts, lambda dx, x: jnp.concatenate([blank, x] if low else [x, blank])
+        )
+        for dx, x in enumerate(shifts):
+            edge[dx, :, cols] = x[outer]
 
 
 def joined(pieces, halos, place_piece):
@@ -362,12 +374,13 @@
 
 
 def render_body(
-    margin, taps, tile_cols, per, bands, ends, mixes, plane, sums, own, slab, others, *refs
+    margin, taps, tile_cols, per, bands, ends, mixes, plane, low, high, head, tail, slab, others, *refs
 ):
-    part, width = own.shape
+    width = plane.shape[1]
     pieces, halos, (out, result, sems, image) = refs[:-6], refs[-6:-4], refs[-4:]
     block, step = 2 * margin, per * (width // tile_cols)
-    window, blocks = block + taps - 1, part // block
+    part = 2 * block
+    window = block + taps - 1
     visit_count, side = result.shape[0], width // tile_cols
     bases = bands.shape[0] // block
     visit, band = lax.axis_index("visit"), lax.axis_index("band")
@@ -375,21 +388,14 @@
     first = visit == 0
 
     def put(_, start, piece):
-        rows = pl.ds(pl.multiple_of(start + margin, margin), piece.shape[0])
+        rows = pl.ds(pl.multiple_of(start, margin), piece.shape[0])
         image[rows, :] = piece
 
     above, below = joined(pieces, halos, put)
-    image[:margin] = jnp.where(first, own[part - margin :, :], above)
-    image[margin + part : 2 * margin + part] = jnp.where(first, below, own[:margin, :])
-    image[2 * margin + part :] = jnp.where(first, above, below)
-    edge = slice(part + 2 * margin, part + 3 * margin)
-
-    def before(x):
-        return jnp.where(first, x[edge], x[part : part + margin])
-
-    def after(x):
-        return jnp.where(first, x[margin : 2 * margin], x[edge])
-
+    image[part : part + margin, :] = above
+    image[part + margin :, :] = below
+    over, under = slice(part, part + margin), slice(part + margin, part + 2 * margin)
+    top, bottom = slice(0, margin), slice(part - margin, part)
     numbers = [
         ((visit * band_count + band) * visit_count + j + 1).astype(F32)
         for j in range(visit_count)
@@ -413,18 +419,27 @@
     copies = []
     for c in range(width // step):
         cols = slice(c * step, (c + 1) * step)
-        shifts = shifted(image, margin, taps, side, c * per, (c + 1) * per)
-        for n in range(blocks):
-            rows = slice(n * block, n * block + window)
-            value = apply_rows(left, shifts, lambda x: x[rows])
-            finish((1 - visit) * part, n, c, others, value)
-        for n in range(blocks):
-            value = sums[n, :, cols]
-            if n == 0:
-                value += apply_rows(ends[0, :, : taps * margin], shifts, before)
-            if n == blocks - 1:
-                value += apply_rows(ends[1, :, : taps * margin], shifts, after)
-            finish(visit * part, n, c, slab, value)
+        shifts = shifted(image, slice(0, part + 2 * margin), margin, taps, side, c * per, (c + 1) * per)
+
+        def upper(dx, x):
+            before = jnp.where(first, tail[dx, :, cols], x[over])
+            return jnp.concatenate([before, x[: window - margin]])
+
+        def lower(dx, x):
+            after = jnp.where(first, x[under], head[dx, :, cols])
+            return jnp.concatenate([x[part - window + margin : part], after])
+
+        start = (1 - visit) * part
+        finish(start, 0, c, others, apply_rows(left, shifts, upper))
+        finish(start, 1, c, others, apply_rows(left, shifts, lower))
+        lack = apply_rows(
+            ends[0, :, : taps * margin], shifts, lambda dx, x: jnp.where(first, x[over], x[bottom])
+        )
+        finish(visit * part, 0, c, slab, low[:, cols] + lack)
+        lack = apply_rows(
+            ends[1, :, : taps * margin], shifts, lambda dx, x: jnp.where(first, x[top], x[under])
+        )
+        finish(visit * part, 1, c, slab, high[:, cols] + lack)
         copies.append(
             pltpu.make_async_copy(result.at[:, :, cols], out.at[:, :, cols], sems.at[c])
         )
@@ -448,10 +463,10 @@
     image[image.shape[0] - margin :] = below
     put(lax.axis_index("visit"), 0, own[...])
     for t in range(0, width // side, per):
-        shifts = shifted(image, margin, taps, side, t, t + per)
+        shifts = shifted(image, slice(0, image.shape[0]), margin, taps, side, t, t + per)
         for n in range(out.shape[0]):
             rows = slice(n * block, n * block + window)
-            value = apply_rows(bands[:, : taps * window], shifts, lambda x: x[rows])
+            value = apply_rows(bands[:, : taps * window], shifts, lambda dx, x: x[rows])
             out[n, :, t * side : (t + per) * side] = value.astype(BF)
 
 
@@ -583,30 +598,36 @@
     work = 2 * bases * side * width * taps * (block + taps - 1)
     per = tile_cols
     result = jax.ShapeDtypeStruct((visit_count, side, width), BF)
-    if visits == 2 and part % block == 0:
-        sums = kernel_call(
-            functools.partial(filter_ahead_body, margin, taps, side, per),
-            jax.ShapeDtypeStruct((part // block, bases * block, width), F32),
-            [VMEM] * 2,
-            [pltpu.VMEM((part + 2 * margin, width), BF)],
-            flops=work // 2,
-            data=4 * bases * part * width,
-            spare=24,
-        )(toeplitz, coadd)
+    if visits == 2 and part == 2 * block:
+        sums, edges = [], []
+        for low in (True, False):
+            one, edge = kernel_call(
+                functools.partial(filter_ahead_body, margin, taps, side, per, low),
+                [
+                    jax.ShapeDtypeStruct((bases * block, width), F32),
+                    jax.ShapeDtypeStruct((taps, margin, width), BF),
+                ],
+                [VMEM] * 2,
+                flops=work // 4,
+                data=4 * bases * part * width,
+                spare=16,
+            )(toeplitz, coadd)
+            sums.append(one)
+            edges.append(edge)
         return kernel_call(
             functools.partial(render_body, margin, taps, tile_cols, per),
             result,
-            [VMEM] * (8 + len(pieces) + 2),
+            [VMEM] * (10 + len(pieces) + 2),
             [
                 pltpu.VMEM(result.shape, BF),
                 pltpu.SemaphoreType.DMA((tile_cols // per,)),
-                pltpu.VMEM((part + 3 * margin, width), BF),
+                pltpu.VMEM((part + 2 * margin, width), BF),
             ],
             flops=work // 2,
             data=2 * bases * side * width,
             spare=24,
             out_specs=HBM,
-        )(toeplitz, ends, mixes, plane, sums, coadd, slab, *others, *pieces, *halos)
+        )(toeplitz, ends, mixes, plane, *sums, *edges, slab, *others, *pieces, *halos)
     filtered = kernel_call(
         functools.partial(filter_body, margin, taps, side, per),
         jax.ShapeDtypeStruct((side // block, bases * block, width), BF),

time: 39 us -> 41.5 us (1.064)
  waiting for transfers between devices: 5.31 us -> 8.82 us
  other arithmetic: 0.01 us -> 0.77 us
  local copies, waits for them, and re-layouts: 1.31 us -> 0.63 us
  starting transfers between devices: 21.2 us -> 20.7 us
    ppermute x3, waiting for transfers between devices: 1.18 us -> 4.65 us  [on_device(): lax.ppermute(arrived[k * visits + r], 'visit', [(v, (v - r) % visits) for...]
    ppermute x1, waiting for transfers between devices: 0.78 us -> 0.01 us  [on_device(): pieces.append(lax.ppermute(share, 'visit', turn(r)))]
    convert_element_type x1, other arithmetic: 0.01 us -> 0.77 us  [make_tables(): turned = jnp.transpose(kernels, (0, 2, 1)).astype(F32)]
    ppermute x7, starting transfers between devices: 13.5 us -> 12.7 us  [on_device(): arrived[n] = lax.ppermute(parcels[n], ('sky', 'visit'), pairs)]
    ppermute x7, waiting for transfers between devices: 3.1 us -> 3.83 us  [on_device(): arrived[n] = lax.ppermute(parcels[n], ('sky', 'visit'), pairs)]
    unnamed x11 -> x9, local copies, waits for them, and re-layouts: 1.02 us -> 0.34 us
    pallas_call x7 -> x8, Pallas kernels: 10.4 us -> 10.2 us  [call(): pl.pallas_call(body, out_shape=outs, in_specs=in_specs, out_specs=places,...]
  transfers between devices with their start and end apart: 15 -> 15, of which waited for: 4 -> 6; matrix products, arithmetic and copies ran while one was open for 2% -> 3% of each run, Pallas kernels for 10% -> 9%
where the time goes in v2:
time: 41.5 us; the launch traced here: 41.3 us
  starting transfers between devices  20.7 us (50%)
  Pallas kernels  10.2 us (25%)
  waiting for transfers between devices  8.82 us (21%)
  other arithmetic  0.77 us (2%)
  local copies, waits for them, and re-layouts  0.63 us (2%)
    ppermute x7, starting transfers between devices, on_device(): arrived[n] = lax.ppermute(parcels[n], ('sky', 'visit'), pairs)  12.7 us
    pallas_call x8, Pallas kernels, call(): pl.pallas_call(body, out_shape=outs, in_specs=in_specs, out_specs=places,...  10.2 us
    ppermute x3, waiting for transfers between devices, on_device(): lax.ppermute(arrived[k * visits + r], 'visit', [(v, (v - r) % visits) for...  4.65 us
    ppermute x7, waiting for transfers between devices, on_device(): arrived[n] = lax.ppermute(parcels[n], ('sky', 'visit'), pairs)  3.83 us
    ppermute x1, starting transfers between devices, on_device(): halos.append(lax.ppermute(edge, ('sky', 'visit', 'band'), pairs))  3.46 us
    ppermute x3, starting transfers between devices, on_device(): lax.ppermute(arrived[k * visits + r], 'visit', [(v, (v - r) % visits) for...  2.99 us
    ppermute x1, starting transfers between devices, on_device(): pieces.append(lax.ppermute(share, 'visit', turn(r)))  1.19 us
  transfers between devices with their start and end apart: 15, of which 6 were waited for; matrix products, arithmetic and copies ran while one was open for 3% of the time, Pallas kernels for 9%

profile of v2, /device:TPU:0, one launch (start us, length us, event | category | flops | bytes accessed | tf_op | source)
XLA Modules:
  0.0 41.3 jit_solution(725527992983831659)
XLA Ops:
  0.0 2.0 %shard_map.92 = (bf16[328,128]{1,0:T(8,128)(2,1)S(1)}, bf16[328,128]{1,0:T(8,128)(2,1)S(1)}, bf16[328,128]{1,0:T(8,128)(2,1)S(1)}, bf16[328,128]{1,0:T(8,128)(2,...) custom-call(s32[2,8]{1,0:T(2,128)} %refs_0_.1, ...), custom_call_target="tpu_custom_call" | custom-call | flops 134217728 | bytes 1048576 | tf_op jit(solution)/shard_map/pallas_call | solution.py:27
  2.0 5.1 %collective-permute-start = (bf16[328,128]{1,0:T(8,128)(2,1)S(1)}, bf16[328,128]{1,0:T(8,128)(2,1)S(1)}, u32[]{:S(2)}, u32[]{:S(2)}) collective-permute-start(bf16[328,128]{1,0:T(8,128)(2,1)S(1)} %get-tuple-element.31), channel_id=1, source_target_pairs={{0,10},{2,8},{4,14},{6,12},{8,2},{10,0},{12,6},{14,4},{1,11},{3,9}... | collective-permute-start | bytes 251912 | tf_op jit(solution)/shard_map/ppermute | solution.py:542
  7.0 1.3 %collective-permute-start.1 = (bf16[328,128]{1,0:T(8,128)(2,1)S(1)}, bf16[328,128]{1,0:T(8,128)(2,1)S(1)}, u32[]{:S(2)}, u32[]{:S(2)}) collective-permute-start(bf16[328,128]{1,0:T(8,128)(2,1)S(1)} %get-tuple-element.32), channel_id=1, source_target_pairs={{0,14},{2,12},{4,2},{6,0},{8,6},{10,4},{12,10},{14,8},{1,15},{3,13... | collective-permute-start | bytes 251912 | tf_op jit(solution)/shard_map/ppermute | solution.py:542
  8.4 1.6 %collective-permute-start.2 = (bf16[328,128]{1,0:T(8,128)(2,1)S(1)}, bf16[328,128]{1,0:T(8,128)(2,1)S(1)}, u32[]{:S(2)}, u32[]{:S(2)}) collective-permute-start(bf16[328,128]{1,0:T(8,128)(2,1)S(1)} %get-tuple-element.33), channel_id=1, source_target_pairs={{0,6},{2,4},{4,10},{6,8},{8,14},{10,12},{12,2},{14,0},{1,7},{3,5},... | collective-permute-start | bytes 251912 | tf_op jit(solution)/shard_map/ppermute | solution.py:542
  10.0 0.3 collective-permute-start.4
  10.3 3.6 %collective-permute-start.5 = (bf16[328,128]{1,0:T(8,128)(2,1)S(1)}, bf16[328,128]{1,0:T(8,128)(2,1)S(1)}, u32[]{:S(2)}, u32[]{:S(2)}) collective-permute-start(bf16[328,128]{1,0:T(8,128)(2,1)S(1)} %get-tuple-element.36), channel_id=1, source_target_pairs={{0,12},{2,14},{4,0},{6,2},{8,4},{10,6},{12,8},{14,10},{1,13},{3,15... | collective-permute-start | bytes 251912 | tf_op jit(solution)/shard_map/ppermute | solution.py:542
  13.9 0.8 %convert_bitcast_fusion = f32[4,33,33]{1,0,2:T(4,128)S(1)} fusion(bf16[4,33,33]{2,0,1:T(4,128)(2,1)} %param.15), kind=kLoop, calls=%fused_computation | loop fusion | flops 4356 | bytes 26136 | tf_op jit(solution)/shard_map/convert_element_type | solution.py:190
  14.7 0.0 collective-permute-done.refs_1_
  14.7 0.1 collective-permute-start.6
  14.8 0.0 collective-permute-done.1.refs_2_
  14.8 0.7 %collective-permute-start.3 = (bf16[328,128]{1,0:T(8,128)(2,1)S(1)}, bf16[328,128]{1,0:T(8,128)(2,1)S(1)}, u32[]{:S(2)}, u32[]{:S(2)}) collective-permute-start(bf16[328,128]{1,0:T(8,128)(2,1)S(1)} %get-tuple-element.34.refs_0_), channel_id=1, source_target_pairs={{0,2},{2,0},{4,6},{6,4},{8,10},{10,8},{12,14},{14,12},{1,3},{3,1},... | collective-permute-start | bytes 251912 | tf_op jit(solution)/shard_map/ppermute | solution.py:542
  15.5 0.1 copy.16
  15.7 0.1 reshape.9.taps
  15.7 0.1 copy.18
  15.9 0.1 reshape.11.tails
  16.0 0.1 copy.17
  16.1 0.1 reshape.10.heads
  16.2 0.0 copy-done.1
  16.2 0.0 copy-done.2
  16.2 0.0 copy-done
  16.2 1.1 %shard_map.91 = (f32[128,1024]{1,0:T(8,128)S(1)}, bf16[128,2176]{1,0:T(8,128)(2,1)S(1)}, f32[64,128]{1,0:T(8,128)S(1)}, bf16[2,128,640]{2,1,0:T(8,128)(2,1)S(1)}) custom-call(s32[2,8]{1,0:T(2,128)S(1)} %copy-done.2, f32[4,16]{1,0:T(4,128)S(1)} %bitcast.5, s32[8,8,32]{2,1,0:T(8,128)S(1)} %copy-done, f32[4,17,128]{2,1,0:T(8,128)S(1)} %reshape.9.taps, ...), custom_call_target="tpu_custom_call" | custom-call | flops 67108864 | bytes 524288 | tf_op jit(solution)/shard_map/pallas_call | solution.py:27
  17.3 0.0 collective-permute-done.2.refs_3_
  17.3 2.9 %collective-permute-done.4.refs_5_ = bf16[328,128]{1,0:T(8,128)(2,1)S(1)} collective-permute-done((bf16[328,128]{1,0:T(8,128)(2,1)S(1)}, bf16[328,128]{1,0:T(8,128)(2,1)S(1)}, u32[]{:S(2)}, u32[]{:S(2)}) %collective-permute-start.4) | collective-permute-done | bytes 84000 | tf_op jit(solution)/shard_map/ppermute | solution.py:542
  20.2 0.0 collective-permute-done.5.refs_6_
  20.2 1.0 %collective-permute-done.6.refs_7_ = bf16[328,128]{1,0:T(8,128)(2,1)S(1)} collective-permute-done((bf16[328,128]{1,0:T(8,128)(2,1)S(1)}, bf16[328,128]{1,0:T(8,128)(2,1)S(1)}, u32[]{:S(2)}, u32[]{:S(2)}) %collective-permute-start.6) | collective-permute-done | bytes 84000 | tf_op jit(solution)/shard_map/ppermute | solution.py:542
  21.1 0.0 collective-permute-done.3.refs_4_
  21.1 0.6 %shard_map.93 = (bf16[2,64,1024]{2,1,0:T(8,128)(2,1)S(1)}, bf16[3,64,1024]{2,1,0:T(8,128)(2,1)S(1)}) custom-call(f32[128,1024]{1,0:T(8,128)S(1)} %get-tuple-element.29.plane, bf16[328,128]{1,0:T(8,128)(2,1)S(1)} %get-tuple-element.30.refs_0_, bf16[328,128]{1,0:T(8,128)(2,1)S(1)} %collective-permute-done.refs_1_, ...), custom_call_target="tpu_custom_call" | custom-call | flops 2621440 | bytes 1048576 | tf_op jit(solution)/shard_map/pallas_call | solution.py:27
  21.7 0.1 collective-permute-start.7
  21.8 1.0 %collective-permute-start.8 = (bf16[328,128]{1,0:T(8,128)(2,1)S(1)}, bf16[328,128]{1,0:T(8,128)(2,1)S(1)}, u32[]{:S(2)}, u32[]{:S(2)}) collective-permute-start(bf16[328,128]{1,0:T(8,128)(2,1)S(1)} %collective-permute-done.refs_1_), channel_id=1, source_target_pairs={{0,2},{2,0},{1,3},{3,1},{4,6},{6,4},{5,7},{7,5},{8,10},{10,8},{9,1... | collective-permute-start | bytes 251912 | tf_op jit(solution)/shard_map/ppermute | solution.py:548
  22.7 1.1 %collective-permute-start.9 = (bf16[328,128]{1,0:T(8,128)(2,1)S(1)}, bf16[328,128]{1,0:T(8,128)(2,1)S(1)}, u32[]{:S(2)}, u32[]{:S(2)}) collective-permute-start(bf16[328,128]{1,0:T(8,128)(2,1)S(1)} %collective-permute-done.1.refs_2_), channel_id=1, source_target_pairs={{0,2},{2,0},{1,3},{3,1},{4,6},{6,4},{5,7},{7,5},{8,10},{10,8},{9,1... | collective-permute-start | bytes 251912 | tf_op jit(solution)/shard_map/ppermute | solution.py:548
  23.9 0.9 %collective-permute-start.10 = (bf16[328,128]{1,0:T(8,128)(2,1)S(1)}, bf16[328,128]{1,0:T(8,128)(2,1)S(1)}, u32[]{:S(2)}, u32[]{:S(2)}) collective-permute-start(bf16[328,128]{1,0:T(8,128)(2,1)S(1)} %collective-permute-done.2.refs_3_), channel_id=1, source_target_pairs={{0,2},{2,0},{1,3},{3,1},{4,6},{6,4},{5,7},{7,5},{8,10},{10,8},{9,1... | collective-permute-start | bytes 251912 | tf_op jit(solution)/shard_map/ppermute | solution.py:548
  24.8 0.0 collective-permute-done.7.refs_1_
  24.8 0.2 shard_map.94
  25.0 1.2 %collective-permute-start.11 = (bf16[32,1024]{1,0:T(8,128)(2,1)S(1)}, bf16[32,1024]{1,0:T(8,128)(2,1)S(1)}, u32[]{:S(2)}, u32[]{:S(2)}) collective-permute-start(bf16[32,1024]{1,0:T(8,128)(2,1)S(1)} %get-tuple-element.45), channel_id=1, source_target_pairs={{0,2},{2,0},{1,3},{3,1},{4,6},{6,4},{5,7},{7,5},{8,10},{10,8},{9,1... | collective-permute-start | bytes 196616 | tf_op jit(solution)/shard_map/ppermute | solution.py:577
  26.2 1.1 %collective-permute-done.8.refs_1_ = bf16[328,128]{1,0:T(8,128)(2,1)S(1)} collective-permute-done((bf16[328,128]{1,0:T(8,128)(2,1)S(1)}, bf16[328,128]{1,0:T(8,128)(2,1)S(1)}, u32[]{:S(2)}, u32[]{:S(2)}) %collective-permute-start.8) | collective-permute-done | bytes 84000 | tf_op jit(solution)/shard_map/ppermute | solution.py:548
  27.2 1.8 %collective-permute-done.9.refs_2_ = bf16[328,128]{1,0:T(8,128)(2,1)S(1)} collective-permute-done((bf16[328,128]{1,0:T(8,128)(2,1)S(1)}, bf16[328,128]{1,0:T(8,128)(2,1)S(1)}, u32[]{:S(2)}, u32[]{:S(2)}) %collective-permute-start.9) | collective-permute-done | bytes 84000 | tf_op jit(solution)/shard_map/ppermute | solution.py:548
  29.0 1.8 %collective-permute-done.10.refs_3_ = bf16[328,128]{1,0:T(8,128)(2,1)S(1)} collective-permute-done((bf16[328,128]{1,0:T(8,128)(2,1)S(1)}, bf16[328,128]{1,0:T(8,128)(2,1)S(1)}, u32[]{:S(2)}, u32[]{:S(2)}) %collective-permute-start.10) | collective-permute-done | bytes 84000 | tf_op jit(solution)/shard_map/ppermute | solution.py:548
  30.8 0.2 shard_map.97.others
  31.0 3.5 %collective-permute-start.13 = (bf16[16,1024]{1,0:T(8,128)(2,1)S(1)}, bf16[16,1024]{1,0:T(8,128)(2,1)S(1)}, u32[]{:S(2)}, u32[]{:S(2)}) collective-permute-start(bf16[16,1024]{1,0:T(8,128)(2,1)S(1)} %get-tuple-element.46), channel_id=1, source_target_pairs={{0,12},{2,6},{1,15},{3,5},{4,0},{6,10},{5,3},{7,9},{8,4},{10,14},{... | collective-permute-start | bytes 98312 | tf_op jit(solution)/shard_map/ppermute | solution.py:588
  34.4 0.0 collective-permute-done.11.refs_0_
  34.5 0.0 collective-permute-start.12
  34.5 1.3 %shard_map.96 = (f32[128,1024]{1,0:T(8,128)S(1)}, bf16[33,16,1024]{2,1,0:T(8,128)(2,1)S(1)}) custom-call(bf16[128,2176]{1,0:T(8,128)(2,1)S(1)} %get-tuple-element.26.bands, bf16[64,1024]{1,0:T(8,128)(2,1)S(1)} %get-tuple-element.39.own), custom_call_target="tpu_custom_call" | custom-call | flops 553648128 | bytes 1048576 | tf_op jit(solution)/shard_map/pallas_call | solution.py:27
  35.7 0.3 collective-permute-done.13.refs_2_
  36.0 0.2 collective-permute-start.14
  36.3 1.2 %shard_map.95 = (f32[128,1024]{1,0:T(8,128)S(1)}, bf16[33,16,1024]{2,1,0:T(8,128)(2,1)S(1)}) custom-call(bf16[128,2176]{1,0:T(8,128)(2,1)S(1)} %get-tuple-element.26.bands, bf16[64,1024]{1,0:T(8,128)(2,1)S(1)} %get-tuple-element.39.own), custom_call_target="tpu_custom_call" | custom-call | flops 553648128 | bytes 1048576 | tf_op jit(solution)/shard_map/pallas_call | solution.py:27
  37.5 0.0 collective-permute-done.14.refs_3_
  37.6 0.0 collective-permute-done.12.refs_1_
  37.6 3.7 %shard_map.98 = bf16[2,128,1024]{2,1,0:T(8,128)(2,1)} custom-call(bf16[128,2176]{1,0:T(8,128)(2,1)S(1)} %get-tuple-element.26.bands, bf16[2,128,640]{2,1,0:T(8,128)(2,1)S(1)} %get-tuple-element.27.ends, f32[64,128]{1,0:T(8,128)S(1)} %get-tuple-element.28.mixes, f32[128,1024]{1,0:T(8,128)S(1)} %get-tuple-element.29.plane, ...), custom_call_target="tpu_custom_call" | custom-call | flops 1107296256 | bytes 1048576 | tf_op jit(solution)/shard_map/pallas_call | solution.py:27
  (7 shorter events, 0.0 us)
Async XLA Ops:
  0.0 16.2 %copy-start.1 = (f32[16,4]{0,1:T(4,128)S(1)}, f32[16,4]{0,1:T(4,128)}, u32[]{:S(2)}) copy-start(f32[16,4]{0,1:T(4,128)} %param.17) | copy-start | bytes 772
  0.0 16.2 %copy-start.2 = (s32[2,8]{1,0:T(2,128)S(1)}, s32[2,8]{1,0:T(2,128)}, u32[]{:S(2)}) copy-start(s32[2,8]{1,0:T(2,128)} %choice.1) | copy-start | bytes 196
  0.0 16.2 %copy-start = (s32[8,8,32]{2,1,0:T(8,128)S(1)}, s32[8,8,32]{2,1,0:T(8,128)}, u32[]{:S(2)}) copy-start(s32[8,8,32]{2,1,0:T(8,128)} %listed.1) | copy-start | bytes 24580
  2.0 12.7 %collective-permute-start = (bf16[328,128]{1,0:T(8,128)(2,1)S(1)}, bf16[328,128]{1,0:T(8,128)(2,1)S(1)}, u32[]{:S(2)}, u32[]{:S(2)}) collective-permute-start(bf16[328,128]{1,0:T(8,128)(2,1)S(1)} %get-tuple-element.31), channel_id=1, source_target_pairs={{0,10},{2,8},{4,14},{6,12},{8,2},{10,0},{12,6},{14,4},{1,11},{3,9}... | collective-permute-start | bytes 251912 | tf_op jit(solution)/shard_map/ppermute | solution.py:542
  7.0 7.7 %collective-permute-start.1 = (bf16[328,128]{1,0:T(8,128)(2,1)S(1)}, bf16[328,128]{1,0:T(8,128)(2,1)S(1)}, u32[]{:S(2)}, u32[]{:S(2)}) collective-permute-start(bf16[328,128]{1,0:T(8,128)(2,1)S(1)} %get-tuple-element.32), channel_id=1, source_target_pairs={{0,14},{2,12},{4,2},{6,0},{8,6},{10,4},{12,10},{14,8},{1,15},{3,13... | collective-permute-start | bytes 251912 | tf_op jit(solution)/shard_map/ppermute | solution.py:542
  8.4 8.9 %collective-permute-start.2 = (bf16[328,128]{1,0:T(8,128)(2,1)S(1)}, bf16[328,128]{1,0:T(8,128)(2,1)S(1)}, u32[]{:S(2)}, u32[]{:S(2)}) collective-permute-start(bf16[328,128]{1,0:T(8,128)(2,1)S(1)} %get-tuple-element.33), channel_id=1, source_target_pairs={{0,6},{2,4},{4,10},{6,8},{8,14},{10,12},{12,2},{14,0},{1,7},{3,5},... | collective-permute-start | bytes 251912 | tf_op jit(solution)/shard_map/ppermute | solution.py:542
  10.0 10.2 %collective-permute-start.4 = (bf16[328,128]{1,0:T(8,128)(2,1)S(1)}, bf16[328,128]{1,0:T(8,128)(2,1)S(1)}, u32[]{:S(2)}, u32[]{:S(2)}) collective-permute-start(bf16[328,128]{1,0:T(8,128)(2,1)S(1)} %get-tuple-element.35), channel_id=1, source_target_pairs={{0,8},{2,10},{4,12},{6,14},{8,0},{10,2},{12,4},{14,6},{1,9},{3,11}... | collective-permute-start | bytes 251912 | tf_op jit(solution)/shard_map/ppermute | solution.py:542
  10.3 9.8 %collective-permute-start.5 = (bf16[328,128]{1,0:T(8,128)(2,1)S(1)}, bf16[328,128]{1,0:T(8,128)(2,1)S(1)}, u32[]{:S(2)}, u32[]{:S(2)}) collective-permute-start(bf16[328,128]{1,0:T(8,128)(2,1)S(1)} %get-tuple-element.36), channel_id=1, source_target_pairs={{0,12},{2,14},{4,0},{6,2},{8,4},{10,6},{12,8},{14,10},{1,13},{3,15... | collective-permute-start | bytes 251912 | tf_op jit(solution)/shard_map/ppermute | solution.py:542
  14.7 6.4 %collective-permute-start.6 = (bf16[328,128]{1,0:T(8,128)(2,1)S(1)}, bf16[328,128]{1,0:T(8,128)(2,1)S(1)}, u32[]{:S(2)}, u32[]{:S(2)}) collective-permute-start(bf16[328,128]{1,0:T(8,128)(2,1)S(1)} %get-tuple-element.37), channel_id=1, source_target_pairs={{0,4},{2,6},{4,8},{6,10},{8,12},{10,14},{12,0},{14,2},{1,5},{3,7},... | collective-permute-start | bytes 251912 | tf_op jit(solution)/shard_map/ppermute | solution.py:542
  14.8 6.3 %collective-permute-start.3 = (bf16[328,128]{1,0:T(8,128)(2,1)S(1)}, bf16[328,128]{1,0:T(8,128)(2,1)S(1)}, u32[]{:S(2)}, u32[]{:S(2)}) collective-permute-start(bf16[328,128]{1,0:T(8,128)(2,1)S(1)} %get-tuple-element.34.refs_0_), channel_id=1, source_target_pairs={{0,2},{2,0},{4,6},{6,4},{8,10},{10,8},{12,14},{14,12},{1,3},{3,1},... | collective-permute-start | bytes 251912 | tf_op jit(solution)/shard_map/ppermute | solution.py:542
  21.7 3.1 %collective-permute-start.7 = (bf16[3,64,1024]{2,1,0:T(8,128)(2,1)S(1)}, bf16[3,64,1024]{2,1,0:T(8,128)(2,1)S(1)}, u32[]{:S(2)}, u32[]{:S(2)}) collective-permute-start(bf16[3,64,1024]{2,1,0:T(8,128)(2,1)S(1)} %get-tuple-element.38.refs_0_), channel_id=1, source_target_pairs={{0,1},{1,0},{2,3},{3,2},{4,5},{5,4},{6,7},{7,6},{8,9},{9,8},{10,11... | collective-permute-start | bytes 1179656 | tf_op jit(solution)/shard_map/ppermute | solution.py:560
  21.8 5.4 %collective-permute-start.8 = (bf16[328,128]{1,0:T(8,128)(2,1)S(1)}, bf16[328,128]{1,0:T(8,128)(2,1)S(1)}, u32[]{:S(2)}, u32[]{:S(2)}) collective-permute-start(bf16[328,128]{1,0:T(8,128)(2,1)S(1)} %collective-permute-done.refs_1_), channel_id=1, source_target_pairs={{0,2},{2,0},{1,3},{3,1},{4,6},{6,4},{5,7},{7,5},{8,10},{10,8},{9,1... | collective-permute-start | bytes 251912 | tf_op jit(solution)/shard_map/ppermute | solution.py:548
  22.7 6.3 %collective-permute-start.9 = (bf16[328,128]{1,0:T(8,128)(2,1)S(1)}, bf16[328,128]{1,0:T(8,128)(2,1)S(1)}, u32[]{:S(2)}, u32[]{:S(2)}) collective-permute-start(bf16[328,128]{1,0:T(8,128)(2,1)S(1)} %collective-permute-done.1.refs_2_), channel_id=1, source_target_pairs={{0,2},{2,0},{1,3},{3,1},{4,6},{6,4},{5,7},{7,5},{8,10},{10,8},{9,1... | collective-permute-start | bytes 251912 | tf_op jit(solution)/shard_map/ppermute | solution.py:548
  23.9 6.9 %collective-permute-start.10 = (bf16[328,128]{1,0:T(8,128)(2,1)S(1)}, bf16[328,128]{1,0:T(8,128)(2,1)S(1)}, u32[]{:S(2)}, u32[]{:S(2)}) collective-permute-start(bf16[328,128]{1,0:T(8,128)(2,1)S(1)} %collective-permute-done.2.refs_3_), channel_id=1, source_target_pairs={{0,2},{2,0},{1,3},{3,1},{4,6},{6,4},{5,7},{7,5},{8,10},{10,8},{9,1... | collective-permute-start | bytes 251912 | tf_op jit(solution)/shard_map/ppermute | solution.py:548
  25.0 9.5 %collective-permute-start.11 = (bf16[32,1024]{1,0:T(8,128)(2,1)S(1)}, bf16[32,1024]{1,0:T(8,128)(2,1)S(1)}, u32[]{:S(2)}, u32[]{:S(2)}) collective-permute-start(bf16[32,1024]{1,0:T(8,128)(2,1)S(1)} %get-tuple-element.45), channel_id=1, source_target_pairs={{0,2},{2,0},{1,3},{3,1},{4,6},{6,4},{5,7},{7,5},{8,10},{10,8},{9,1... | collective-permute-start | bytes 196616 | tf_op jit(solution)/shard_map/ppermute | solution.py:577
  31.0 5.1 %collective-permute-start.13 = (bf16[16,1024]{1,0:T(8,128)(2,1)S(1)}, bf16[16,1024]{1,0:T(8,128)(2,1)S(1)}, u32[]{:S(2)}, u32[]{:S(2)}) collective-permute-start(bf16[16,1024]{1,0:T(8,128)(2,1)S(1)} %get-tuple-element.46), channel_id=1, source_target_pairs={{0,12},{2,6},{1,15},{3,5},{4,0},{6,10},{5,3},{7,9},{8,4},{10,14},{... | collective-permute-start | bytes 98312 | tf_op jit(solution)/shard_map/ppermute | solution.py:588
  34.5 3.1 %collective-permute-start.12 = (bf16[32,1024]{1,0:T(8,128)(2,1)S(1)}, bf16[32,1024]{1,0:T(8,128)(2,1)S(1)}, u32[]{:S(2)}, u32[]{:S(2)}) collective-permute-start(bf16[32,1024]{1,0:T(8,128)(2,1)S(1)} %collective-permute-done.11.refs_0_), channel_id=1, source_target_pairs={{0,1},{1,0},{2,3},{3,2},{4,5},{5,4},{6,7},{7,6},{8,9},{9,8},{10,11... | collective-permute-start | bytes 196616 | tf_op jit(solution)/shard_map/ppermute | solution.py:578
  36.0 1.5 %collective-permute-start.14 = (bf16[16,1024]{1,0:T(8,128)(2,1)S(1)}, bf16[16,1024]{1,0:T(8,128)(2,1)S(1)}, u32[]{:S(2)}, u32[]{:S(2)}) collective-permute-start(bf16[16,1024]{1,0:T(8,128)(2,1)S(1)} %collective-permute-done.13.refs_2_), channel_id=1, source_target_pairs={{0,1},{1,0},{2,3},{3,2},{4,5},{5,4},{6,7},{7,6},{8,9},{9,8},{10,11... | collective-permute-start | bytes 98312 | tf_op jit(solution)/shard_map/ppermute | solution.py:590

commit v3 on v2

--- a/solution.py
+++ b/solution.py
@@ -48,8 +48,8 @@
 
 
 def warp_body(patches, visits, cap, *refs):
-    sources, parcels, held = refs[:5], refs[5:-10], refs[-10:]
-    routes, offsets, entries, table, raw, small, large, seats, labels, weights = held
+    sources, parcels, held = refs[:5], refs[5:-9], refs[-9:]
+    routes, offsets, entries, table, raw, small, large, seats, labels = held
     copies = [
         pltpu.make_async_copy(source, target, small.at[n])
         for n, (source, target) in enumerate(zip(sources[:4], held[:4]))
@@ -91,17 +91,15 @@
         rolled = pltpu.roll(rows, 0, 1, stride=1, stride_axis=0)
         return jnp.where(near, rolled, 0.0).astype(BF)
 
-    for n in range(2 * tiles):
-        weights[n] = spread(n)
+    for load in loads:
+        load.wait()
     for k in range(patches):
         labels[k] = jnp.full((LABELS, side), -1.0, F32)
     count = [jnp.int32(0)] * patches
-    for load in loads:
-        load.wait()
     for i, v in itertools.product(range(tile_cols), range(visit_count)):
         n = v * tile_cols + i
-        halfway = jnp.dot(weights[2 * n], raw[v, i], preferred_element_type=F32).astype(BF)
-        warped = jnp.dot(halfway, weights[2 * n + 1], preferred_element_type=F32).astype(BF)
+        halfway = jnp.dot(spread(2 * n), raw[v, i], preferred_element_type=F32).astype(BF)
+        warped = jnp.dot(halfway, spread(2 * n + 1), preferred_element_type=F32).astype(BF)
         route = routes[v, i]
         owner = lax.div(route, tile_cols)
         slot = route - owner * tile_cols
@@ -137,7 +135,6 @@
             pltpu.SemaphoreType.DMA((math.gcd(4, tile_cols),)),
             pltpu.VMEM((patches * cap, side, side), BF),
             pltpu.VMEM((patches, LABELS, side), F32),
-            pltpu.VMEM((2 * visit_count * tile_cols, side, side), BF),
         ],
         flops=4 * visit_count * tile_cols * side**3,
         data=4 * raw.size,
@@ -274,9 +271,9 @@
 
 
 def coadd_body(visit_total, margin, plane, *refs):
-    partials, (coadd, share, edge) = refs[:-3], refs[-3:]
-    part, some = coadd.shape[0], share.shape[0]
-    visit, band = lax.axis_index("visit"), lax.axis_index("band")
+    partials, (coadd, edge) = refs[:-2], refs[-2:]
+    part = coadd.shape[0]
+    visit = lax.axis_index("visit")
     rows = pl.ds(pl.multiple_of(visit * part, part), part)
     width = coadd.shape[1]
     step = math.gcd(128, width)
@@ -291,12 +288,11 @@
             plane[rows, cols] > 0.0, 1.0 / (visit_total - 3.0), 1.0 / (visit_total - 2.0)
         )
         coadd[:, cols] = ((total - high - low) * scale).astype(BF)
-    share[...] = coadd[pl.ds(pl.multiple_of(band * some, some), some), :]
     start = pl.multiple_of(jnp.where(visit == 0, 0, part - margin), margin)
     edge[...] = coadd[pl.ds(start, margin), :]
 
 
-def shifted(image, rows, margin, taps, side, first, until):
+def shifted(image, rows, margin, taps, side, first, until, made):
     width, height = image.shape[1], rows.stop - rows.start
     lane = iota((height, side), 1)
     blank = jnp.zeros((height, side), BF)
@@ -304,18 +300,17 @@
     for dx in range(taps):
         shift = dx - margin
         low, high = (first - 1, until) if shift < 0 else (first, until + 1)
-        turned = {
-            t: pltpu.roll(image[rows, t * side : (t + 1) * side], -shift % side, 1)
-            if 0 <= t < width // side
-            else blank
-            for t in range(low, high)
-        } if shift else {}
+        for t in range(low, high) if shift else ():
+            if not 0 <= t < width // side:
+                made[t, dx] = blank
+            elif (t, dx) not in made:
+                made[t, dx] = pltpu.roll(image[rows, t * side : (t + 1) * side], -shift % side, 1)
         tiles = []
         for t in range(first, until):
             if shift < 0:
-                tiles.append(jnp.where(lane < -shift, turned[t - 1], turned[t]))
+                tiles.append(jnp.where(lane < -shift, made[t - 1, dx], made[t, dx]))
             elif shift > 0:
-                tiles.append(jnp.where(lane < side - shift, turned[t], turned[t + 1]))
+                tiles.append(jnp.where(lane < side - shift, made[t, dx], made[t + 1, dx]))
             else:
                 tiles.append(image[rows, t * side : (t + 1) * side])
         shifts.append(jnp.concatenate(tiles, axis=1))
@@ -349,9 +344,10 @@
     rows = slice(0, window - margin) if low else slice(part - window + margin, part)
     outer = slice(0, margin) if low else slice(window - 2 * margin, window - margin)
     blank = jnp.zeros((margin, per * side), BF)
+    made = {}
     for t in range(0, width // side, per):
         cols = slice(t * side, (t + per) * side)
-        shifts = shifted(own, rows, margin, taps, side, t, t + per)
+        shifts = shifted(own, rows, margin, taps, side, t, t + per, made)
         sums[:, cols] = apply_rows(
             left, shifts, lambda dx, x: jnp.concatenate([blank, x] if low else [x, blank])
         )
@@ -363,8 +359,7 @@
     sky, visit, band = (lax.axis_index(name) for name in ("sky", "visit", "band"))
     patches, visits = lax.axis_size("sky"), lax.axis_size("visit")
     for n, piece in enumerate(pieces):
-        some = piece.shape[0]
-        place_piece(lax.rem(visit + 1 + n // 2, visits), lax.rem(band + n, 2) * some, piece[...])
+        place_piece(lax.rem(visit + 1 + n, visits), piece[...])
     mine = lax.rem(visit, 2) == band
     below = jnp.where(mine, halos[0][...], halos[1][...])
     above = jnp.where(mine, halos[1][...], halos[0][...])
@@ -387,9 +382,8 @@
     band_count = lax.axis_size("band")
     first = visit == 0
 
-    def put(_, start, piece):
-        rows = pl.ds(pl.multiple_of(start, margin), piece.shape[0])
-        image[rows, :] = piece
+    def put(_, piece):
+        image[:part, :] = piece
 
     above, below = joined(pieces, halos, put)
     image[part : part + margin, :] = above
@@ -417,9 +411,10 @@
                 result[j, rows, cols] = jnp.where(bad == numbers[j], 0.0, pixels).astype(BF)
 
     copies = []
+    made = {}
     for c in range(width // step):
         cols = slice(c * step, (c + 1) * step)
-        shifts = shifted(image, slice(0, part + 2 * margin), margin, taps, side, c * per, (c + 1) * per)
+        shifts = shifted(image, slice(0, part + 2 * margin), margin, taps, side, c * per, (c + 1) * per, made)
 
         def upper(dx, x):
             before = jnp.where(first, tail[dx, :, cols], x[over])
@@ -454,16 +449,16 @@
     block = 2 * margin
     window = block + taps - 1
 
-    def put(turn, start, piece):
-        start = pl.multiple_of(turn * part + start + margin, margin)
-        image[pl.ds(start, piece.shape[0])] = piece
+    def put(turn, piece):
+        image[pl.ds(pl.multiple_of(turn * part + margin, margin), part), :] = piece
 
     above, below = joined(pieces, halos, put)
     image[:margin] = above
     image[image.shape[0] - margin :] = below
-    put(lax.axis_index("visit"), 0, own[...])
+    put(lax.axis_index("visit"), own[...])
+    made = {}
     for t in range(0, width // side, per):
-        shifts = shifted(image, slice(0, image.shape[0]), margin, taps, side, t, t + per)
+        shifts = shifted(image, slice(0, image.shape[0]), margin, taps, side, t, t + per, made)
         for n in range(out.shape[0]):
             rows = slice(n * block, n * block + window)
             value = apply_rows(bands[:, : taps * window], shifts, lambda dx, x: x[rows])
@@ -560,9 +555,9 @@
         lax.ppermute(partial, "band", [(b, (b + q) % bands) for b in range(bands)])
         for q in range(1, bands)
     ]
-    coadd, share, edge = kernel_call(
+    coadd, edge = kernel_call(
         functools.partial(coadd_body, visit_total, margin),
-        [jax.ShapeDtypeStruct((rows, width), BF) for rows in (part, part // bands, margin)],
+        [jax.ShapeDtypeStruct((rows, width), BF) for rows in (part, margin)],
         [VMEM] * (1 + bands),
         flops=8 * part * width,
         data=8 * part * width,
@@ -574,8 +569,7 @@
     swap = [(b, (b + 1) % bands) for b in range(bands)]
     pieces = []
     for r in range(1, visits):
-        pieces.append(lax.ppermute(share, "visit", turn(r)))
-        pieces.append(lax.ppermute(pieces[-1], "band", swap))
+        pieces.append(lax.ppermute(coadd, "visit", turn(r)))
     halos = []
     for first in range(0, visits, bands):
         pairs = []
@@ -596,7 +590,7 @@
         data=4 * visit_count * side * width,
     )(*own_others)
     work = 2 * bases * side * width * taps * (block + taps - 1)
-    per = tile_cols
+    per = math.gcd(4, tile_cols)
     result = jax.ShapeDtypeStruct((visit_count, side, width), BF)
     if visits == 2 and part == 2 * block:
         sums, edges = [], []

time: 41.5 us -> 40.8 us (0.983)
  Pallas kernels: 10.2 us -> 9.75 us
    ppermute x2 -> x1, starting transfers between devices: 1.2 us -> 1.2 us  [on_device(): pieces.append(lax.ppermute(coadd, 'visit', turn(r)))]
  transfers between devices with their start and end apart: 15 -> 14, of which waited for: 6 -> 6; matrix products, arithmetic and copies ran while one was open for 3% -> 3% of each run, Pallas kernels for 9% -> 10%
where the time goes in v3:
time: 40.8 us; the launch traced here: 40.6 us
  starting transfers between devices  20.4 us (50%)
  Pallas kernels  9.75 us (24%)
  waiting for transfers between devices  8.83 us (22%)
  other arithmetic  0.77 us (2%)
  local copies, waits for them, and re-layouts  0.63 us (2%)
    ppermute x7, starting transfers between devices, on_device(): arrived[n] = lax.ppermute(parcels[n], ('sky', 'visit'), pairs)  12.7 us
    pallas_call x8, Pallas kernels, call(): pl.pallas_call(body, out_shape=outs, in_specs=in_specs, out_specs=places,...  9.75 us
    ppermute x3, waiting for transfers between devices, on_device(): lax.ppermute(arrived[k * visits + r], 'visit', [(v, (v - r) % visits) for...  4.65 us
    ppermute x7, waiting for transfers between devices, on_device(): arrived[n] = lax.ppermute(parcels[n], ('sky', 'visit'), pairs)  3.85 us
    ppermute x1, starting transfers between devices, on_device(): halos.append(lax.ppermute(edge, ('sky', 'visit', 'band'), pairs))  3.45 us
    ppermute x3, starting transfers between devices, on_device(): lax.ppermute(arrived[k * visits + r], 'visit', [(v, (v - r) % visits) for...  2.99 us
    ppermute x1, starting transfers between devices, on_device(): pieces.append(lax.ppermute(coadd, 'visit', turn(r)))  1.2 us
  transfers between devices with their start and end apart: 14, of which 6 were waited for; matrix products, arithmetic and copies ran while one was open for 3% of the time, Pallas kernels for 10%

profile of v3, /device:TPU:0, one launch (start us, length us, event | category | flops | bytes accessed | tf_op | source)
XLA Modules:
  0.0 40.6 jit_solution(6406501712083831348)
XLA Ops:
  0.0 0.0 copy-start.1
  0.0 0.0 copy-start.2
  0.0 1.8 %shard_map.92 = (bf16[328,128]{1,0:T(8,128)(2,1)S(1)}, bf16[328,128]{1,0:T(8,128)(2,1)S(1)}, bf16[328,128]{1,0:T(8,128)(2,1)S(1)}, bf16[328,128]{1,0:T(8,128)(2,...) custom-call(s32[2,8]{1,0:T(2,128)} %refs_0_.1, ...), custom_call_target="tpu_custom_call" | custom-call | flops 134217728 | bytes 1048576 | tf_op jit(solution)/shard_map/pallas_call | solution.py:27
  1.9 5.1 %collective-permute-start = (bf16[328,128]{1,0:T(8,128)(2,1)S(1)}, bf16[328,128]{1,0:T(8,128)(2,1)S(1)}, u32[]{:S(2)}, u32[]{:S(2)}) collective-permute-start(bf16[328,128]{1,0:T(8,128)(2,1)S(1)} %get-tuple-element.30), channel_id=1, source_target_pairs={{0,10},{2,8},{4,14},{6,12},{8,2},{10,0},{12,6},{14,4},{1,11},{3,9}... | collective-permute-start | bytes 251912 | tf_op jit(solution)/shard_map/ppermute | solution.py:537
  6.9 1.3 %collective-permute-start.1 = (bf16[328,128]{1,0:T(8,128)(2,1)S(1)}, bf16[328,128]{1,0:T(8,128)(2,1)S(1)}, u32[]{:S(2)}, u32[]{:S(2)}) collective-permute-start(bf16[328,128]{1,0:T(8,128)(2,1)S(1)} %get-tuple-element.31), channel_id=1, source_target_pairs={{0,14},{2,12},{4,2},{6,0},{8,6},{10,4},{12,10},{14,8},{1,15},{3,13... | collective-permute-start | bytes 251912 | tf_op jit(solution)/shard_map/ppermute | solution.py:537
  8.2 1.6 %collective-permute-start.2 = (bf16[328,128]{1,0:T(8,128)(2,1)S(1)}, bf16[328,128]{1,0:T(8,128)(2,1)S(1)}, u32[]{:S(2)}, u32[]{:S(2)}) collective-permute-start(bf16[328,128]{1,0:T(8,128)(2,1)S(1)} %get-tuple-element.32), channel_id=1, source_target_pairs={{0,6},{2,4},{4,10},{6,8},{8,14},{10,12},{12,2},{14,0},{1,7},{3,5},... | collective-permute-start | bytes 251912 | tf_op jit(solution)/shard_map/ppermute | solution.py:537
  9.8 0.3 collective-permute-start.4
  10.2 3.6 %collective-permute-start.5 = (bf16[328,128]{1,0:T(8,128)(2,1)S(1)}, bf16[328,128]{1,0:T(8,128)(2,1)S(1)}, u32[]{:S(2)}, u32[]{:S(2)}) collective-permute-start(bf16[328,128]{1,0:T(8,128)(2,1)S(1)} %get-tuple-element.35), channel_id=1, source_target_pairs={{0,12},{2,14},{4,0},{6,2},{8,4},{10,6},{12,8},{14,10},{1,13},{3,15... | collective-permute-start | bytes 251912 | tf_op jit(solution)/shard_map/ppermute | solution.py:537
  13.8 0.8 %convert_bitcast_fusion = f32[4,33,33]{1,0,2:T(4,128)S(1)} fusion(bf16[4,33,33]{2,0,1:T(4,128)(2,1)} %param.15), kind=kLoop, calls=%fused_computation | loop fusion | flops 4356 | bytes 26136 | tf_op jit(solution)/shard_map/convert_element_type | solution.py:187
  14.6 0.0 collective-permute-done.refs_1_
  14.6 0.1 collective-permute-start.6
  14.6 0.0 collective-permute-done.1.refs_2_
  14.6 0.7 %collective-permute-start.3 = (bf16[328,128]{1,0:T(8,128)(2,1)S(1)}, bf16[328,128]{1,0:T(8,128)(2,1)S(1)}, u32[]{:S(2)}, u32[]{:S(2)}) collective-permute-start(bf16[328,128]{1,0:T(8,128)(2,1)S(1)} %get-tuple-element.33.refs_0_), channel_id=1, source_target_pairs={{0,2},{2,0},{4,6},{6,4},{8,10},{10,8},{12,14},{14,12},{1,3},{3,1},... | collective-permute-start | bytes 251912 | tf_op jit(solution)/shard_map/ppermute | solution.py:537
  15.4 0.1 copy.16
  15.5 0.1 reshape.9.taps
  15.6 0.1 copy.18
  15.7 0.1 reshape.11.tails
  15.8 0.1 copy.17
  15.9 0.1 reshape.10.heads
  16.0 0.0 copy-done.1
  16.0 0.0 copy-done.2
  16.1 0.0 copy-done
  16.1 1.1 %shard_map.91 = (f32[128,1024]{1,0:T(8,128)S(1)}, bf16[128,2176]{1,0:T(8,128)(2,1)S(1)}, f32[64,128]{1,0:T(8,128)S(1)}, bf16[2,128,640]{2,1,0:T(8,128)(2,1)S(1)}) custom-call(s32[2,8]{1,0:T(2,128)S(1)} %copy-done.2, f32[4,16]{1,0:T(4,128)S(1)} %bitcast.5, s32[8,8,32]{2,1,0:T(8,128)S(1)} %copy-done, f32[4,17,128]{2,1,0:T(8,128)S(1)} %reshape.9.taps, ...), custom_call_target="tpu_custom_call" | custom-call | flops 67108864 | bytes 524288 | tf_op jit(solution)/shard_map/pallas_call | solution.py:27
  17.1 0.0 collective-permute-done.2.refs_3_
  17.1 2.9 %collective-permute-done.4.refs_5_ = bf16[328,128]{1,0:T(8,128)(2,1)S(1)} collective-permute-done((bf16[328,128]{1,0:T(8,128)(2,1)S(1)}, bf16[328,128]{1,0:T(8,128)(2,1)S(1)}, u32[]{:S(2)}, u32[]{:S(2)}) %collective-permute-start.4) | collective-permute-done | bytes 84000 | tf_op jit(solution)/shard_map/ppermute | solution.py:537
  20.0 0.0 collective-permute-done.5.refs_6_
  20.0 1.0 %collective-permute-done.6.refs_7_ = bf16[328,128]{1,0:T(8,128)(2,1)S(1)} collective-permute-done((bf16[328,128]{1,0:T(8,128)(2,1)S(1)}, bf16[328,128]{1,0:T(8,128)(2,1)S(1)}, u32[]{:S(2)}, u32[]{:S(2)}) %collective-permute-start.6) | collective-permute-done | bytes 84000 | tf_op jit(solution)/shard_map/ppermute | solution.py:537
  21.0 0.0 collective-permute-done.3.refs_4_
  21.0 0.6 %shard_map.93 = (bf16[2,64,1024]{2,1,0:T(8,128)(2,1)S(1)}, bf16[3,64,1024]{2,1,0:T(8,128)(2,1)S(1)}) custom-call(f32[128,1024]{1,0:T(8,128)S(1)} %get-tuple-element.28.plane, bf16[328,128]{1,0:T(8,128)(2,1)S(1)} %get-tuple-element.29.refs_0_, bf16[328,128]{1,0:T(8,128)(2,1)S(1)} %collective-permute-done.refs_1_, ...), custom_call_target="tpu_custom_call" | custom-call | flops 2621440 | bytes 1048576 | tf_op jit(solution)/shard_map/pallas_call | solution.py:27
  21.6 0.1 collective-permute-start.7
  21.7 1.0 %collective-permute-start.8 = (bf16[328,128]{1,0:T(8,128)(2,1)S(1)}, bf16[328,128]{1,0:T(8,128)(2,1)S(1)}, u32[]{:S(2)}, u32[]{:S(2)}) collective-permute-start(bf16[328,128]{1,0:T(8,128)(2,1)S(1)} %collective-permute-done.refs_1_), channel_id=1, source_target_pairs={{0,2},{2,0},{1,3},{3,1},{4,6},{6,4},{5,7},{7,5},{8,10},{10,8},{9,1... | collective-permute-start | bytes 251912 | tf_op jit(solution)/shard_map/ppermute | solution.py:543
  22.6 1.1 %collective-permute-start.9 = (bf16[328,128]{1,0:T(8,128)(2,1)S(1)}, bf16[328,128]{1,0:T(8,128)(2,1)S(1)}, u32[]{:S(2)}, u32[]{:S(2)}) collective-permute-start(bf16[328,128]{1,0:T(8,128)(2,1)S(1)} %collective-permute-done.1.refs_2_), channel_id=1, source_target_pairs={{0,2},{2,0},{1,3},{3,1},{4,6},{6,4},{5,7},{7,5},{8,10},{10,8},{9,1... | collective-permute-start | bytes 251912 | tf_op jit(solution)/shard_map/ppermute | solution.py:543
  23.7 0.9 %collective-permute-start.10 = (bf16[328,128]{1,0:T(8,128)(2,1)S(1)}, bf16[328,128]{1,0:T(8,128)(2,1)S(1)}, u32[]{:S(2)}, u32[]{:S(2)}) collective-permute-start(bf16[328,128]{1,0:T(8,128)(2,1)S(1)} %collective-permute-done.2.refs_3_), channel_id=1, source_target_pairs={{0,2},{2,0},{1,3},{3,1},{4,6},{6,4},{5,7},{7,5},{8,10},{10,8},{9,1... | collective-permute-start | bytes 251912 | tf_op jit(solution)/shard_map/ppermute | solution.py:543
  24.6 0.0 collective-permute-done.7.refs_1_
  24.7 0.2 shard_map.94
  24.8 1.2 %collective-permute-start.11 = (bf16[64,1024]{1,0:T(8,128)(2,1)S(1)}, bf16[64,1024]{1,0:T(8,128)(2,1)S(1)}, u32[]{:S(2)}, u32[]{:S(2)}) collective-permute-start(bf16[64,1024]{1,0:T(8,128)(2,1)S(1)} %get-tuple-element.38.own), channel_id=1, source_target_pairs={{0,2},{2,0},{1,3},{3,1},{4,6},{6,4},{5,7},{7,5},{8,10},{10,8},{9,1... | collective-permute-start | bytes 393224 | tf_op jit(solution)/shard_map/ppermute | solution.py:572
  26.0 1.1 %collective-permute-done.8.refs_1_ = bf16[328,128]{1,0:T(8,128)(2,1)S(1)} collective-permute-done((bf16[328,128]{1,0:T(8,128)(2,1)S(1)}, bf16[328,128]{1,0:T(8,128)(2,1)S(1)}, u32[]{:S(2)}, u32[]{:S(2)}) %collective-permute-start.8) | collective-permute-done | bytes 84000 | tf_op jit(solution)/shard_map/ppermute | solution.py:543
  27.1 1.8 %collective-permute-done.9.refs_2_ = bf16[328,128]{1,0:T(8,128)(2,1)S(1)} collective-permute-done((bf16[328,128]{1,0:T(8,128)(2,1)S(1)}, bf16[328,128]{1,0:T(8,128)(2,1)S(1)}, u32[]{:S(2)}, u32[]{:S(2)}) %collective-permute-start.9) | collective-permute-done | bytes 84000 | tf_op jit(solution)/shard_map/ppermute | solution.py:543
  28.9 1.8 %collective-permute-done.10.refs_3_ = bf16[328,128]{1,0:T(8,128)(2,1)S(1)} collective-permute-done((bf16[328,128]{1,0:T(8,128)(2,1)S(1)}, bf16[328,128]{1,0:T(8,128)(2,1)S(1)}, u32[]{:S(2)}, u32[]{:S(2)}) %collective-permute-start.10) | collective-permute-done | bytes 84000 | tf_op jit(solution)/shard_map/ppermute | solution.py:543
  30.7 0.2 shard_map.97.others
  30.9 3.4 %collective-permute-start.12 = (bf16[16,1024]{1,0:T(8,128)(2,1)S(1)}, bf16[16,1024]{1,0:T(8,128)(2,1)S(1)}, u32[]{:S(2)}, u32[]{:S(2)}) collective-permute-start(bf16[16,1024]{1,0:T(8,128)(2,1)S(1)} %get-tuple-element.44), channel_id=1, source_target_pairs={{0,12},{2,6},{1,15},{3,5},{4,0},{6,10},{5,3},{7,9},{8,4},{10,14},{... | collective-permute-start | bytes 98312 | tf_op jit(solution)/shard_map/ppermute | solution.py:582
  34.3 1.3 %shard_map.96 = (f32[128,1024]{1,0:T(8,128)S(1)}, bf16[33,16,1024]{2,1,0:T(8,128)(2,1)S(1)}) custom-call(bf16[128,2176]{1,0:T(8,128)(2,1)S(1)} %get-tuple-element.25.bands, bf16[64,1024]{1,0:T(8,128)(2,1)S(1)} %get-tuple-element.38.own), custom_call_target="tpu_custom_call" | custom-call | flops 553648128 | bytes 1048576 | tf_op jit(solution)/shard_map/pallas_call | solution.py:27
  35.6 0.3 collective-permute-done.12.refs_1_
  35.9 0.0 collective-permute-start.13
  35.9 1.3 %shard_map.95 = (f32[128,1024]{1,0:T(8,128)S(1)}, bf16[33,16,1024]{2,1,0:T(8,128)(2,1)S(1)}) custom-call(bf16[128,2176]{1,0:T(8,128)(2,1)S(1)} %get-tuple-element.25.bands, bf16[64,1024]{1,0:T(8,128)(2,1)S(1)} %get-tuple-element.38.own), custom_call_target="tpu_custom_call" | custom-call | flops 553648128 | bytes 1048576 | tf_op jit(solution)/shard_map/pallas_call | solution.py:27
  37.2 0.0 collective-permute-done.13.refs_2_
  37.2 0.0 collective-permute-done.11.refs_0_
  37.2 3.4 %shard_map.98 = bf16[2,128,1024]{2,1,0:T(8,128)(2,1)} custom-call(bf16[128,2176]{1,0:T(8,128)(2,1)S(1)} %get-tuple-element.25.bands, bf16[2,128,640]{2,1,0:T(8,128)(2,1)S(1)} %get-tuple-element.26.ends, f32[64,128]{1,0:T(8,128)S(1)} %get-tuple-element.27.mixes, f32[128,1024]{1,0:T(8,128)S(1)} %get-tuple-element.28.plane, ...), custom_call_target="tpu_custom_call" | custom-call | flops 1107296256 | bytes 1048576 | tf_op jit(solution)/shard_map/pallas_call | solution.py:27
  (5 shorter events, 0.0 us)
Async XLA Ops:
  0.0 16.0 %copy-start.1 = (f32[16,4]{0,1:T(4,128)S(1)}, f32[16,4]{0,1:T(4,128)}, u32[]{:S(2)}) copy-start(f32[16,4]{0,1:T(4,128)} %param.17) | copy-start | bytes 772
  0.0 16.0 %copy-start.2 = (s32[2,8]{1,0:T(2,128)S(1)}, s32[2,8]{1,0:T(2,128)}, u32[]{:S(2)}) copy-start(s32[2,8]{1,0:T(2,128)} %choice.1) | copy-start | bytes 196
  0.0 16.1 %copy-start = (s32[8,8,32]{2,1,0:T(8,128)S(1)}, s32[8,8,32]{2,1,0:T(8,128)}, u32[]{:S(2)}) copy-start(s32[8,8,32]{2,1,0:T(8,128)} %listed.1) | copy-start | bytes 24580
  1.9 12.7 %collective-permute-start = (bf16[328,128]{1,0:T(8,128)(2,1)S(1)}, bf16[328,128]{1,0:T(8,128)(2,1)S(1)}, u32[]{:S(2)}, u32[]{:S(2)}) collective-permute-start(bf16[328,128]{1,0:T(8,128)(2,1)S(1)} %get-tuple-element.30), channel_id=1, source_target_pairs={{0,10},{2,8},{4,14},{6,12},{8,2},{10,0},{12,6},{14,4},{1,11},{3,9}... | collective-permute-start | bytes 251912 | tf_op jit(solution)/shard_map/ppermute | solution.py:537
  6.9 7.7 %collective-permute-start.1 = (bf16[328,128]{1,0:T(8,128)(2,1)S(1)}, bf16[328,128]{1,0:T(8,128)(2,1)S(1)}, u32[]{:S(2)}, u32[]{:S(2)}) collective-permute-start(bf16[328,128]{1,0:T(8,128)(2,1)S(1)} %get-tuple-element.31), channel_id=1, source_target_pairs={{0,14},{2,12},{4,2},{6,0},{8,6},{10,4},{12,10},{14,8},{1,15},{3,13... | collective-permute-start | bytes 251912 | tf_op jit(solution)/shard_map/ppermute | solution.py:537
  8.2 8.9 %collective-permute-start.2 = (bf16[328,128]{1,0:T(8,128)(2,1)S(1)}, bf16[328,128]{1,0:T(8,128)(2,1)S(1)}, u32[]{:S(2)}, u32[]{:S(2)}) collective-permute-start(bf16[328,128]{1,0:T(8,128)(2,1)S(1)} %get-tuple-element.32), channel_id=1, source_target_pairs={{0,6},{2,4},{4,10},{6,8},{8,14},{10,12},{12,2},{14,0},{1,7},{3,5},... | collective-permute-start | bytes 251912 | tf_op jit(solution)/shard_map/ppermute | solution.py:537
  9.8 10.2 %collective-permute-start.4 = (bf16[328,128]{1,0:T(8,128)(2,1)S(1)}, bf16[328,128]{1,0:T(8,128)(2,1)S(1)}, u32[]{:S(2)}, u32[]{:S(2)}) collective-permute-start(bf16[328,128]{1,0:T(8,128)(2,1)S(1)} %get-tuple-element.34), channel_id=1, source_target_pairs={{0,8},{2,10},{4,12},{6,14},{8,0},{10,2},{12,4},{14,6},{1,9},{3,11}... | collective-permute-start | bytes 251912 | tf_op jit(solution)/shard_map/ppermute | solution.py:537
  10.2 9.8 %collective-permute-start.5 = (bf16[328,128]{1,0:T(8,128)(2,1)S(1)}, bf16[328,128]{1,0:T(8,128)(2,1)S(1)}, u32[]{:S(2)}, u32[]{:S(2)}) collective-permute-start(bf16[328,128]{1,0:T(8,128)(2,1)S(1)} %get-tuple-element.35), channel_id=1, source_target_pairs={{0,12},{2,14},{4,0},{6,2},{8,4},{10,6},{12,8},{14,10},{1,13},{3,15... | collective-permute-start | bytes 251912 | tf_op jit(solution)/shard_map/ppermute | solution.py:537
  14.6 6.4 %collective-permute-start.6 = (bf16[328,128]{1,0:T(8,128)(2,1)S(1)}, bf16[328,128]{1,0:T(8,128)(2,1)S(1)}, u32[]{:S(2)}, u32[]{:S(2)}) collective-permute-start(bf16[328,128]{1,0:T(8,128)(2,1)S(1)} %get-tuple-element.36), channel_id=1, source_target_pairs={{0,4},{2,6},{4,8},{6,10},{8,12},{10,14},{12,0},{14,2},{1,5},{3,7},... | collective-permute-start | bytes 251912 | tf_op jit(solution)/shard_map/ppermute | solution.py:537
  14.6 6.3 %collective-permute-start.3 = (bf16[328,128]{1,0:T(8,128)(2,1)S(1)}, bf16[328,128]{1,0:T(8,128)(2,1)S(1)}, u32[]{:S(2)}, u32[]{:S(2)}) collective-permute-start(bf16[328,128]{1,0:T(8,128)(2,1)S(1)} %get-tuple-element.33.refs_0_), channel_id=1, source_target_pairs={{0,2},{2,0},{4,6},{6,4},{8,10},{10,8},{12,14},{14,12},{1,3},{3,1},... | collective-permute-start | bytes 251912 | tf_op jit(solution)/shard_map/ppermute | solution.py:537
  21.6 3.1 %collective-permute-start.7 = (bf16[3,64,1024]{2,1,0:T(8,128)(2,1)S(1)}, bf16[3,64,1024]{2,1,0:T(8,128)(2,1)S(1)}, u32[]{:S(2)}, u32[]{:S(2)}) collective-permute-start(bf16[3,64,1024]{2,1,0:T(8,128)(2,1)S(1)} %get-tuple-element.37.refs_0_), channel_id=1, source_target_pairs={{0,1},{1,0},{2,3},{3,2},{4,5},{5,4},{6,7},{7,6},{8,9},{9,8},{10,11... | collective-permute-start | bytes 1179656 | tf_op jit(solution)/shard_map/ppermute | solution.py:555
  21.7 5.4 %collective-permute-start.8 = (bf16[328,128]{1,0:T(8,128)(2,1)S(1)}, bf16[328,128]{1,0:T(8,128)(2,1)S(1)}, u32[]{:S(2)}, u32[]{:S(2)}) collective-permute-start(bf16[328,128]{1,0:T(8,128)(2,1)S(1)} %collective-permute-done.refs_1_), channel_id=1, source_target_pairs={{0,2},{2,0},{1,3},{3,1},{4,6},{6,4},{5,7},{7,5},{8,10},{10,8},{9,1... | collective-permute-start | bytes 251912 | tf_op jit(solution)/shard_map/ppermute | solution.py:543
  22.6 6.3 %collective-permute-start.9 = (bf16[328,128]{1,0:T(8,128)(2,1)S(1)}, bf16[328,128]{1,0:T(8,128)(2,1)S(1)}, u32[]{:S(2)}, u32[]{:S(2)}) collective-permute-start(bf16[328,128]{1,0:T(8,128)(2,1)S(1)} %collective-permute-done.1.refs_2_), channel_id=1, source_target_pairs={{0,2},{2,0},{1,3},{3,1},{4,6},{6,4},{5,7},{7,5},{8,10},{10,8},{9,1... | collective-permute-start | bytes 251912 | tf_op jit(solution)/shard_map/ppermute | solution.py:543
  23.7 6.9 %collective-permute-start.10 = (bf16[328,128]{1,0:T(8,128)(2,1)S(1)}, bf16[328,128]{1,0:T(8,128)(2,1)S(1)}, u32[]{:S(2)}, u32[]{:S(2)}) collective-permute-start(bf16[328,128]{1,0:T(8,128)(2,1)S(1)} %collective-permute-done.2.refs_3_), channel_id=1, source_target_pairs={{0,2},{2,0},{1,3},{3,1},{4,6},{6,4},{5,7},{7,5},{8,10},{10,8},{9,1... | collective-permute-start | bytes 251912 | tf_op jit(solution)/shard_map/ppermute | solution.py:543
  24.8 12.3 %collective-permute-start.11 = (bf16[64,1024]{1,0:T(8,128)(2,1)S(1)}, bf16[64,1024]{1,0:T(8,128)(2,1)S(1)}, u32[]{:S(2)}, u32[]{:S(2)}) collective-permute-start(bf16[64,1024]{1,0:T(8,128)(2,1)S(1)} %get-tuple-element.38.own), channel_id=1, source_target_pairs={{0,2},{2,0},{1,3},{3,1},{4,6},{6,4},{5,7},{7,5},{8,10},{10,8},{9,1... | collective-permute-start | bytes 393224 | tf_op jit(solution)/shard_map/ppermute | solution.py:572
  30.9 5.0 %collective-permute-start.12 = (bf16[16,1024]{1,0:T(8,128)(2,1)S(1)}, bf16[16,1024]{1,0:T(8,128)(2,1)S(1)}, u32[]{:S(2)}, u32[]{:S(2)}) collective-permute-start(bf16[16,1024]{1,0:T(8,128)(2,1)S(1)} %get-tuple-element.44), channel_id=1, source_target_pairs={{0,12},{2,6},{1,15},{3,5},{4,0},{6,10},{5,3},{7,9},{8,4},{10,14},{... | collective-permute-start | bytes 98312 | tf_op jit(solution)/shard_map/ppermute | solution.py:582
  35.9 1.3 %collective-permute-start.13 = (bf16[16,1024]{1,0:T(8,128)(2,1)S(1)}, bf16[16,1024]{1,0:T(8,128)(2,1)S(1)}, u32[]{:S(2)}, u32[]{:S(2)}) collective-permute-start(bf16[16,1024]{1,0:T(8,128)(2,1)S(1)} %collective-permute-done.12.refs_1_), channel_id=1, source_target_pairs={{0,1},{1,0},{2,3},{3,2},{4,5},{5,4},{6,7},{7,6},{8,9},{9,8},{10,11... | collective-permute-start | bytes 98312 | tf_op jit(solution)/shard_map/ppermute | solution.py:584

commit v4 on v3

--- a/solution.py
+++ b/solution.py
@@ -271,9 +271,9 @@
 
 
 def coadd_body(visit_total, margin, plane, *refs):
-    partials, (coadd, edge) = refs[:-2], refs[-2:]
-    part = coadd.shape[0]
-    visit = lax.axis_index("visit")
+    partials, (coadd, share, edge) = refs[:-3], refs[-3:]
+    part, some = coadd.shape[0], share.shape[0]
+    visit, band = lax.axis_index("visit"), lax.axis_index("band")
     rows = pl.ds(pl.multiple_of(visit * part, part), part)
     width = coadd.shape[1]
     step = math.gcd(128, width)
@@ -288,6 +288,7 @@
             plane[rows, cols] > 0.0, 1.0 / (visit_total - 3.0), 1.0 / (visit_total - 2.0)
         )
         coadd[:, cols] = ((total - high - low) * scale).astype(BF)
+    share[...] = coadd[pl.ds(pl.multiple_of(band * some, some), some), :]
     start = pl.multiple_of(jnp.where(visit == 0, 0, part - margin), margin)
     edge[...] = coadd[pl.ds(start, margin), :]
 
@@ -359,7 +360,8 @@
     sky, visit, band = (lax.axis_index(name) for name in ("sky", "visit", "band"))
     patches, visits = lax.axis_size("sky"), lax.axis_size("visit")
     for n, piece in enumerate(pieces):
-        place_piece(lax.rem(visit + 1 + n, visits), piece[...])
+        some = piece.shape[0]
+        place_piece(lax.rem(visit + 1 + n // 2, visits), lax.rem(band + n, 2) * some, piece[...])
     mine = lax.rem(visit, 2) == band
     below = jnp.where(mine, halos[0][...], halos[1][...])
     above = jnp.where(mine, halos[1][...], halos[0][...])
@@ -382,8 +384,9 @@
     band_count = lax.axis_size("band")
     first = visit == 0
 
-    def put(_, piece):
-        image[:part, :] = piece
+    def put(_, start, piece):
+        rows = pl.ds(pl.multiple_of(start, margin), piece.shape[0])
+        image[rows, :] = piece
 
     above, below = joined(pieces, halos, put)
     image[part : part + margin, :] = above
@@ -449,13 +452,14 @@
     block = 2 * margin
     window = block + taps - 1
 
-    def put(turn, piece):
-        image[pl.ds(pl.multiple_of(turn * part + margin, margin), part), :] = piece
+    def put(turn, start, piece):
+        start = pl.multiple_of(turn * part + start + margin, margin)
+        image[pl.ds(start, piece.shape[0])] = piece
 
     above, below = joined(pieces, halos, put)
     image[:margin] = above
     image[image.shape[0] - margin :] = below
-    put(lax.axis_index("visit"), own[...])
+    put(lax.axis_index("visit"), 0, own[...])
     made = {}
     for t in range(0, width // side, per):
         shifts = shifted(image, slice(0, image.shape[0]), margin, taps, side, t, t + per, made)
@@ -555,9 +559,9 @@
         lax.ppermute(partial, "band", [(b, (b + q) % bands) for b in range(bands)])
         for q in range(1, bands)
     ]
-    coadd, edge = kernel_call(
+    coadd, share, edge = kernel_call(
         functools.partial(coadd_body, visit_total, margin),
-        [jax.ShapeDtypeStruct((rows, width), BF) for rows in (part, margin)],
+        [jax.ShapeDtypeStruct((rows, width), BF) for rows in (part, part // bands, margin)],
         [VMEM] * (1 + bands),
         flops=8 * part * width,
         data=8 * part * width,
@@ -569,7 +573,8 @@
     swap = [(b, (b + 1) % bands) for b in range(bands)]
     pieces = []
     for r in range(1, visits):
-        pieces.append(lax.ppermute(coadd, "visit", turn(r)))
+        pieces.append(lax.ppermute(share, "visit", turn(r)))
+        pieces.append(lax.ppermute(pieces[-1], "band", swap))
     halos = []
     for first in range(0, visits, bands):
         pairs = []

time: 40.8 us -> 41.1 us (level)
    ppermute x1 -> x2, starting transfers between devices: 1.2 us -> 1.2 us  [the longest x1 1.19 us: on_device(): pieces.append(lax.ppermute(share, 'visit', turn(r)))]
  transfers between devices with their start and end apart: 14 -> 15, of which waited for: 6 -> 6; matrix products, arithmetic and copies ran while one was open for 3% -> 3% of each run, Pallas kernels for 10% -> 10%
where the time goes in v4:
time: 41.1 us; the launch traced here: 40.9 us
  starting transfers between devices  20.7 us (50%)
  Pallas kernels  9.77 us (24%)
  waiting for transfers between devices  8.83 us (21%)
  other arithmetic  0.77 us (2%)
  local copies, waits for them, and re-layouts  0.63 us (2%)
    ppermute x7, starting transfers between devices, on_device(): arrived[n] = lax.ppermute(parcels[n], ('sky', 'visit'), pairs)  12.7 us
    pallas_call x8, Pallas kernels, call(): pl.pallas_call(body, out_shape=outs, in_specs=in_specs, out_specs=places,...  9.77 us
    ppermute x3, waiting for transfers between devices, on_device(): lax.ppermute(arrived[k * visits + r], 'visit', [(v, (v - r) % visits) for...  4.65 us
    ppermute x7, waiting for transfers between devices, on_device(): arrived[n] = lax.ppermute(parcels[n], ('sky', 'visit'), pairs)  3.85 us
    ppermute x1, starting transfers between devices, on_device(): halos.append(lax.ppermute(edge, ('sky', 'visit', 'band'), pairs))  3.45 us
    ppermute x3, starting transfers between devices, on_device(): lax.ppermute(arrived[k * visits + r], 'visit', [(v, (v - r) % visits) for...  2.99 us
    ppermute x1, starting transfers between devices, on_device(): pieces.append(lax.ppermute(share, 'visit', turn(r)))  1.19 us
  transfers between devices with their start and end apart: 15, of which 6 were waited for; matrix products, arithmetic and copies ran while one was open for 3% of the time, Pallas kernels for 10%

profile of v4, /device:TPU:0, one launch (start us, length us, event | category | flops | bytes accessed | tf_op | source)
XLA Modules:
  0.0 40.9 jit_solution(1943704060955508369)
XLA Ops:
  0.0 1.8 %shard_map.92 = (bf16[328,128]{1,0:T(8,128)(2,1)S(1)}, bf16[328,128]{1,0:T(8,128)(2,1)S(1)}, bf16[328,128]{1,0:T(8,128)(2,1)S(1)}, bf16[328,128]{1,0:T(8,128)(2,...) custom-call(s32[2,8]{1,0:T(2,128)} %refs_0_.1, ...), custom_call_target="tpu_custom_call" | custom-call | flops 134217728 | bytes 1048576 | tf_op jit(solution)/shard_map/pallas_call | solution.py:27
  1.9 5.1 %collective-permute-start = (bf16[328,128]{1,0:T(8,128)(2,1)S(1)}, bf16[328,128]{1,0:T(8,128)(2,1)S(1)}, u32[]{:S(2)}, u32[]{:S(2)}) collective-permute-start(bf16[328,128]{1,0:T(8,128)(2,1)S(1)} %get-tuple-element.31), channel_id=1, source_target_pairs={{0,10},{2,8},{4,14},{6,12},{8,2},{10,0},{12,6},{14,4},{1,11},{3,9}... | collective-permute-start | bytes 251912 | tf_op jit(solution)/shard_map/ppermute | solution.py:541
  6.9 1.3 %collective-permute-start.1 = (bf16[328,128]{1,0:T(8,128)(2,1)S(1)}, bf16[328,128]{1,0:T(8,128)(2,1)S(1)}, u32[]{:S(2)}, u32[]{:S(2)}) collective-permute-start(bf16[328,128]{1,0:T(8,128)(2,1)S(1)} %get-tuple-element.32), channel_id=1, source_target_pairs={{0,14},{2,12},{4,2},{6,0},{8,6},{10,4},{12,10},{14,8},{1,15},{3,13... | collective-permute-start | bytes 251912 | tf_op jit(solution)/shard_map/ppermute | solution.py:541
  8.2 1.6 %collective-permute-start.2 = (bf16[328,128]{1,0:T(8,128)(2,1)S(1)}, bf16[328,128]{1,0:T(8,128)(2,1)S(1)}, u32[]{:S(2)}, u32[]{:S(2)}) collective-permute-start(bf16[328,128]{1,0:T(8,128)(2,1)S(1)} %get-tuple-element.33), channel_id=1, source_target_pairs={{0,6},{2,4},{4,10},{6,8},{8,14},{10,12},{12,2},{14,0},{1,7},{3,5},... | collective-permute-start | bytes 251912 | tf_op jit(solution)/shard_map/ppermute | solution.py:541
  9.8 0.3 collective-permute-start.4
  10.2 3.6 %collective-permute-start.5 = (bf16[328,128]{1,0:T(8,128)(2,1)S(1)}, bf16[328,128]{1,0:T(8,128)(2,1)S(1)}, u32[]{:S(2)}, u32[]{:S(2)}) collective-permute-start(bf16[328,128]{1,0:T(8,128)(2,1)S(1)} %get-tuple-element.36), channel_id=1, source_target_pairs={{0,12},{2,14},{4,0},{6,2},{8,4},{10,6},{12,8},{14,10},{1,13},{3,15... | collective-permute-start | bytes 251912 | tf_op jit(solution)/shard_map/ppermute | solution.py:541
  13.8 0.8 %convert_bitcast_fusion = f32[4,33,33]{1,0,2:T(4,128)S(1)} fusion(bf16[4,33,33]{2,0,1:T(4,128)(2,1)} %param.15), kind=kLoop, calls=%fused_computation | loop fusion | flops 4356 | bytes 26136 | tf_op jit(solution)/shard_map/convert_element_type | solution.py:187
  14.6 0.0 collective-permute-done.refs_1_
  14.6 0.1 collective-permute-start.6
  14.6 0.0 collective-permute-done.1.refs_2_
  14.6 0.7 %collective-permute-start.3 = (bf16[328,128]{1,0:T(8,128)(2,1)S(1)}, bf16[328,128]{1,0:T(8,128)(2,1)S(1)}, u32[]{:S(2)}, u32[]{:S(2)}) collective-permute-start(bf16[328,128]{1,0:T(8,128)(2,1)S(1)} %get-tuple-element.34.refs_0_), channel_id=1, source_target_pairs={{0,2},{2,0},{4,6},{6,4},{8,10},{10,8},{12,14},{14,12},{1,3},{3,1},... | collective-permute-start | bytes 251912 | tf_op jit(solution)/shard_map/ppermute | solution.py:541
  15.4 0.1 copy.16
  15.5 0.1 reshape.9.taps
  15.6 0.1 copy.18
  15.7 0.1 reshape.11.tails
  15.8 0.1 copy.17
  15.9 0.1 reshape.10.heads
  16.0 0.0 copy-done.1
  16.0 0.0 copy-done.2
  16.1 0.0 copy-done
  16.1 1.1 %shard_map.91 = (f32[128,1024]{1,0:T(8,128)S(1)}, bf16[128,2176]{1,0:T(8,128)(2,1)S(1)}, f32[64,128]{1,0:T(8,128)S(1)}, bf16[2,128,640]{2,1,0:T(8,128)(2,1)S(1)}) custom-call(s32[2,8]{1,0:T(2,128)S(1)} %copy-done.2, f32[4,16]{1,0:T(4,128)S(1)} %bitcast.5, s32[8,8,32]{2,1,0:T(8,128)S(1)} %copy-done, f32[4,17,128]{2,1,0:T(8,128)S(1)} %reshape.9.taps, ...), custom_call_target="tpu_custom_call" | custom-call | flops 67108864 | bytes 524288 | tf_op jit(solution)/shard_map/pallas_call | solution.py:27
  17.1 0.0 collective-permute-done.2.refs_3_
  17.1 2.9 %collective-permute-done.4.refs_5_ = bf16[328,128]{1,0:T(8,128)(2,1)S(1)} collective-permute-done((bf16[328,128]{1,0:T(8,128)(2,1)S(1)}, bf16[328,128]{1,0:T(8,128)(2,1)S(1)}, u32[]{:S(2)}, u32[]{:S(2)}) %collective-permute-start.4) | collective-permute-done | bytes 84000 | tf_op jit(solution)/shard_map/ppermute | solution.py:541
  20.0 0.0 collective-permute-done.5.refs_6_
  20.0 1.0 %collective-permute-done.6.refs_7_ = bf16[328,128]{1,0:T(8,128)(2,1)S(1)} collective-permute-done((bf16[328,128]{1,0:T(8,128)(2,1)S(1)}, bf16[328,128]{1,0:T(8,128)(2,1)S(1)}, u32[]{:S(2)}, u32[]{:S(2)}) %collective-permute-start.6) | collective-permute-done | bytes 84000 | tf_op jit(solution)/shard_map/ppermute | solution.py:541
  21.0 0.0 collective-permute-done.3.refs_4_
  21.0 0.6 %shard_map.93 = (bf16[2,64,1024]{2,1,0:T(8,128)(2,1)S(1)}, bf16[3,64,1024]{2,1,0:T(8,128)(2,1)S(1)}) custom-call(f32[128,1024]{1,0:T(8,128)S(1)} %get-tuple-element.29.plane, bf16[328,128]{1,0:T(8,128)(2,1)S(1)} %get-tuple-element.30.refs_0_, bf16[328,128]{1,0:T(8,128)(2,1)S(1)} %collective-permute-done.refs_1_, ...), custom_call_target="tpu_custom_call" | custom-call | flops 2621440 | bytes 1048576 | tf_op jit(solution)/shard_map/pallas_call | solution.py:27
  21.6 0.1 collective-permute-start.7
  21.7 1.0 %collective-permute-start.8 = (bf16[328,128]{1,0:T(8,128)(2,1)S(1)}, bf16[328,128]{1,0:T(8,128)(2,1)S(1)}, u32[]{:S(2)}, u32[]{:S(2)}) collective-permute-start(bf16[328,128]{1,0:T(8,128)(2,1)S(1)} %collective-permute-done.refs_1_), channel_id=1, source_target_pairs={{0,2},{2,0},{1,3},{3,1},{4,6},{6,4},{5,7},{7,5},{8,10},{10,8},{9,1... | collective-permute-start | bytes 251912 | tf_op jit(solution)/shard_map/ppermute | solution.py:547
  22.6 1.1 %collective-permute-start.9 = (bf16[328,128]{1,0:T(8,128)(2,1)S(1)}, bf16[328,128]{1,0:T(8,128)(2,1)S(1)}, u32[]{:S(2)}, u32[]{:S(2)}) collective-permute-start(bf16[328,128]{1,0:T(8,128)(2,1)S(1)} %collective-permute-done.1.refs_2_), channel_id=1, source_target_pairs={{0,2},{2,0},{1,3},{3,1},{4,6},{6,4},{5,7},{7,5},{8,10},{10,8},{9,1... | collective-permute-start | bytes 251912 | tf_op jit(solution)/shard_map/ppermute | solution.py:547
  23.7 0.9 %collective-permute-start.10 = (bf16[328,128]{1,0:T(8,128)(2,1)S(1)}, bf16[328,128]{1,0:T(8,128)(2,1)S(1)}, u32[]{:S(2)}, u32[]{:S(2)}) collective-permute-start(bf16[328,128]{1,0:T(8,128)(2,1)S(1)} %collective-permute-done.2.refs_3_), channel_id=1, source_target_pairs={{0,2},{2,0},{1,3},{3,1},{4,6},{6,4},{5,7},{7,5},{8,10},{10,8},{9,1... | collective-permute-start | bytes 251912 | tf_op jit(solution)/shard_map/ppermute | solution.py:547
  24.6 0.0 collective-permute-done.7.refs_1_
  24.7 0.2 shard_map.94
  24.8 1.2 %collective-permute-start.11 = (bf16[32,1024]{1,0:T(8,128)(2,1)S(1)}, bf16[32,1024]{1,0:T(8,128)(2,1)S(1)}, u32[]{:S(2)}, u32[]{:S(2)}) collective-permute-start(bf16[32,1024]{1,0:T(8,128)(2,1)S(1)} %get-tuple-element.45), channel_id=1, source_target_pairs={{0,2},{2,0},{1,3},{3,1},{4,6},{6,4},{5,7},{7,5},{8,10},{10,8},{9,1... | collective-permute-start | bytes 196616 | tf_op jit(solution)/shard_map/ppermute | solution.py:576
  26.0 1.1 %collective-permute-done.8.refs_1_ = bf16[328,128]{1,0:T(8,128)(2,1)S(1)} collective-permute-done((bf16[328,128]{1,0:T(8,128)(2,1)S(1)}, bf16[328,128]{1,0:T(8,128)(2,1)S(1)}, u32[]{:S(2)}, u32[]{:S(2)}) %collective-permute-start.8) | collective-permute-done | bytes 84000 | tf_op jit(solution)/shard_map/ppermute | solution.py:547
  27.1 1.8 %collective-permute-done.9.refs_2_ = bf16[328,128]{1,0:T(8,128)(2,1)S(1)} collective-permute-done((bf16[328,128]{1,0:T(8,128)(2,1)S(1)}, bf16[328,128]{1,0:T(8,128)(2,1)S(1)}, u32[]{:S(2)}, u32[]{:S(2)}) %collective-permute-start.9) | collective-permute-done | bytes 84000 | tf_op jit(solution)/shard_map/ppermute | solution.py:547
  28.9 1.8 %collective-permute-done.10.refs_3_ = bf16[328,128]{1,0:T(8,128)(2,1)S(1)} collective-permute-done((bf16[328,128]{1,0:T(8,128)(2,1)S(1)}, bf16[328,128]{1,0:T(8,128)(2,1)S(1)}, u32[]{:S(2)}, u32[]{:S(2)}) %collective-permute-start.10) | collective-permute-done | bytes 84000 | tf_op jit(solution)/shard_map/ppermute | solution.py:547
  30.7 0.2 shard_map.97.others
  30.9 3.4 %collective-permute-start.13 = (bf16[16,1024]{1,0:T(8,128)(2,1)S(1)}, bf16[16,1024]{1,0:T(8,128)(2,1)S(1)}, u32[]{:S(2)}, u32[]{:S(2)}) collective-permute-start(bf16[16,1024]{1,0:T(8,128)(2,1)S(1)} %get-tuple-element.46), channel_id=1, source_target_pairs={{0,12},{2,6},{1,15},{3,5},{4,0},{6,10},{5,3},{7,9},{8,4},{10,14},{... | collective-permute-start | bytes 98312 | tf_op jit(solution)/shard_map/ppermute | solution.py:587
  34.3 0.0 collective-permute-done.11.refs_0_
  34.3 0.0 collective-permute-start.12
  34.3 1.3 %shard_map.96 = (f32[128,1024]{1,0:T(8,128)S(1)}, bf16[33,16,1024]{2,1,0:T(8,128)(2,1)S(1)}) custom-call(bf16[128,2176]{1,0:T(8,128)(2,1)S(1)} %get-tuple-element.26.bands, bf16[64,1024]{1,0:T(8,128)(2,1)S(1)} %get-tuple-element.39.own), custom_call_target="tpu_custom_call" | custom-call | flops 553648128 | bytes 1048576 | tf_op jit(solution)/shard_map/pallas_call | solution.py:27
  35.6 0.3 collective-permute-done.13.refs_2_
  35.9 0.3 collective-permute-start.14
  36.2 1.3 %shard_map.95 = (f32[128,1024]{1,0:T(8,128)S(1)}, bf16[33,16,1024]{2,1,0:T(8,128)(2,1)S(1)}) custom-call(bf16[128,2176]{1,0:T(8,128)(2,1)S(1)} %get-tuple-element.26.bands, bf16[64,1024]{1,0:T(8,128)(2,1)S(1)} %get-tuple-element.39.own), custom_call_target="tpu_custom_call" | custom-call | flops 553648128 | bytes 1048576 | tf_op jit(solution)/shard_map/pallas_call | solution.py:27
  37.4 0.0 collective-permute-done.14.refs_3_
  37.4 0.0 collective-permute-done.12.refs_1_
  37.4 3.4 %shard_map.98 = bf16[2,128,1024]{2,1,0:T(8,128)(2,1)} custom-call(bf16[128,2176]{1,0:T(8,128)(2,1)S(1)} %get-tuple-element.26.bands, bf16[2,128,640]{2,1,0:T(8,128)(2,1)S(1)} %get-tuple-element.27.ends, f32[64,128]{1,0:T(8,128)S(1)} %get-tuple-element.28.mixes, f32[128,1024]{1,0:T(8,128)S(1)} %get-tuple-element.29.plane, ...), custom_call_target="tpu_custom_call" | custom-call | flops 1107296256 | bytes 1048576 | tf_op jit(solution)/shard_map/pallas_call | solution.py:27
  (7 shorter events, 0.0 us)
Async XLA Ops:
  0.0 16.0 %copy-start.1 = (f32[16,4]{0,1:T(4,128)S(1)}, f32[16,4]{0,1:T(4,128)}, u32[]{:S(2)}) copy-start(f32[16,4]{0,1:T(4,128)} %param.17) | copy-start | bytes 772
  0.0 16.0 %copy-start.2 = (s32[2,8]{1,0:T(2,128)S(1)}, s32[2,8]{1,0:T(2,128)}, u32[]{:S(2)}) copy-start(s32[2,8]{1,0:T(2,128)} %choice.1) | copy-start | bytes 196
  0.0 16.1 %copy-start = (s32[8,8,32]{2,1,0:T(8,128)S(1)}, s32[8,8,32]{2,1,0:T(8,128)}, u32[]{:S(2)}) copy-start(s32[8,8,32]{2,1,0:T(8,128)} %listed.1) | copy-start | bytes 24580
  1.9 12.7 %collective-permute-start = (bf16[328,128]{1,0:T(8,128)(2,1)S(1)}, bf16[328,128]{1,0:T(8,128)(2,1)S(1)}, u32[]{:S(2)}, u32[]{:S(2)}) collective-permute-start(bf16[328,128]{1,0:T(8,128)(2,1)S(1)} %get-tuple-element.31), channel_id=1, source_target_pairs={{0,10},{2,8},{4,14},{6,12},{8,2},{10,0},{12,6},{14,4},{1,11},{3,9}... | collective-permute-start | bytes 251912 | tf_op jit(solution)/shard_map/ppermute | solution.py:541
  6.9 7.7 %collective-permute-start.1 = (bf16[328,128]{1,0:T(8,128)(2,1)S(1)}, bf16[328,128]{1,0:T(8,128)(2,1)S(1)}, u32[]{:S(2)}, u32[]{:S(2)}) collective-permute-start(bf16[328,128]{1,0:T(8,128)(2,1)S(1)} %get-tuple-element.32), channel_id=1, source_target_pairs={{0,14},{2,12},{4,2},{6,0},{8,6},{10,4},{12,10},{14,8},{1,15},{3,13... | collective-permute-start | bytes 251912 | tf_op jit(solution)/shard_map/ppermute | solution.py:541
  8.2 8.9 %collective-permute-start.2 = (bf16[328,128]{1,0:T(8,128)(2,1)S(1)}, bf16[328,128]{1,0:T(8,128)(2,1)S(1)}, u32[]{:S(2)}, u32[]{:S(2)}) collective-permute-start(bf16[328,128]{1,0:T(8,128)(2,1)S(1)} %get-tuple-element.33), channel_id=1, source_target_pairs={{0,6},{2,4},{4,10},{6,8},{8,14},{10,12},{12,2},{14,0},{1,7},{3,5},... | collective-permute-start | bytes 251912 | tf_op jit(solution)/shard_map/ppermute | solution.py:541
  9.8 10.2 %collective-permute-start.4 = (bf16[328,128]{1,0:T(8,128)(2,1)S(1)}, bf16[328,128]{1,0:T(8,128)(2,1)S(1)}, u32[]{:S(2)}, u32[]{:S(2)}) collective-permute-start(bf16[328,128]{1,0:T(8,128)(2,1)S(1)} %get-tuple-element.35), channel_id=1, source_target_pairs={{0,8},{2,10},{4,12},{6,14},{8,0},{10,2},{12,4},{14,6},{1,9},{3,11}... | collective-permute-start | bytes 251912 | tf_op jit(solution)/shard_map/ppermute | solution.py:541
  10.2 9.8 %collective-permute-start.5 = (bf16[328,128]{1,0:T(8,128)(2,1)S(1)}, bf16[328,128]{1,0:T(8,128)(2,1)S(1)}, u32[]{:S(2)}, u32[]{:S(2)}) collective-permute-start(bf16[328,128]{1,0:T(8,128)(2,1)S(1)} %get-tuple-element.36), channel_id=1, source_target_pairs={{0,12},{2,14},{4,0},{6,2},{8,4},{10,6},{12,8},{14,10},{1,13},{3,15... | collective-permute-start | bytes 251912 | tf_op jit(solution)/shard_map/ppermute | solution.py:541
  14.6 6.4 %collective-permute-start.6 = (bf16[328,128]{1,0:T(8,128)(2,1)S(1)}, bf16[328,128]{1,0:T(8,128)(2,1)S(1)}, u32[]{:S(2)}, u32[]{:S(2)}) collective-permute-start(bf16[328,128]{1,0:T(8,128)(2,1)S(1)} %get-tuple-element.37), channel_id=1, source_target_pairs={{0,4},{2,6},{4,8},{6,10},{8,12},{10,14},{12,0},{14,2},{1,5},{3,7},... | collective-permute-start | bytes 251912 | tf_op jit(solution)/shard_map/ppermute | solution.py:541
  14.6 6.3 %collective-permute-start.3 = (bf16[328,128]{1,0:T(8,128)(2,1)S(1)}, bf16[328,128]{1,0:T(8,128)(2,1)S(1)}, u32[]{:S(2)}, u32[]{:S(2)}) collective-permute-start(bf16[328,128]{1,0:T(8,128)(2,1)S(1)} %get-tuple-element.34.refs_0_), channel_id=1, source_target_pairs={{0,2},{2,0},{4,6},{6,4},{8,10},{10,8},{12,14},{14,12},{1,3},{3,1},... | collective-permute-start | bytes 251912 | tf_op jit(solution)/shard_map/ppermute | solution.py:541
  21.6 3.1 %collective-permute-start.7 = (bf16[3,64,1024]{2,1,0:T(8,128)(2,1)S(1)}, bf16[3,64,1024]{2,1,0:T(8,128)(2,1)S(1)}, u32[]{:S(2)}, u32[]{:S(2)}) collective-permute-start(bf16[3,64,1024]{2,1,0:T(8,128)(2,1)S(1)} %get-tuple-element.38.refs_0_), channel_id=1, source_target_pairs={{0,1},{1,0},{2,3},{3,2},{4,5},{5,4},{6,7},{7,6},{8,9},{9,8},{10,11... | collective-permute-start | bytes 1179656 | tf_op jit(solution)/shard_map/ppermute | solution.py:559
  21.7 5.4 %collective-permute-start.8 = (bf16[328,128]{1,0:T(8,128)(2,1)S(1)}, bf16[328,128]{1,0:T(8,128)(2,1)S(1)}, u32[]{:S(2)}, u32[]{:S(2)}) collective-permute-start(bf16[328,128]{1,0:T(8,128)(2,1)S(1)} %collective-permute-done.refs_1_), channel_id=1, source_target_pairs={{0,2},{2,0},{1,3},{3,1},{4,6},{6,4},{5,7},{7,5},{8,10},{10,8},{9,1... | collective-permute-start | bytes 251912 | tf_op jit(solution)/shard_map/ppermute | solution.py:547
  22.6 6.3 %collective-permute-start.9 = (bf16[328,128]{1,0:T(8,128)(2,1)S(1)}, bf16[328,128]{1,0:T(8,128)(2,1)S(1)}, u32[]{:S(2)}, u32[]{:S(2)}) collective-permute-start(bf16[328,128]{1,0:T(8,128)(2,1)S(1)} %collective-permute-done.1.refs_2_), channel_id=1, source_target_pairs={{0,2},{2,0},{1,3},{3,1},{4,6},{6,4},{5,7},{7,5},{8,10},{10,8},{9,1... | collective-permute-start | bytes 251912 | tf_op jit(solution)/shard_map/ppermute | solution.py:547
  23.7 6.9 %collective-permute-start.10 = (bf16[328,128]{1,0:T(8,128)(2,1)S(1)}, bf16[328,128]{1,0:T(8,128)(2,1)S(1)}, u32[]{:S(2)}, u32[]{:S(2)}) collective-permute-start(bf16[328,128]{1,0:T(8,128)(2,1)S(1)} %collective-permute-done.2.refs_3_), channel_id=1, source_target_pairs={{0,2},{2,0},{1,3},{3,1},{4,6},{6,4},{5,7},{7,5},{8,10},{10,8},{9,1... | collective-permute-start | bytes 251912 | tf_op jit(solution)/shard_map/ppermute | solution.py:547
  24.8 9.5 %collective-permute-start.11 = (bf16[32,1024]{1,0:T(8,128)(2,1)S(1)}, bf16[32,1024]{1,0:T(8,128)(2,1)S(1)}, u32[]{:S(2)}, u32[]{:S(2)}) collective-permute-start(bf16[32,1024]{1,0:T(8,128)(2,1)S(1)} %get-tuple-element.45), channel_id=1, source_target_pairs={{0,2},{2,0},{1,3},{3,1},{4,6},{6,4},{5,7},{7,5},{8,10},{10,8},{9,1... | collective-permute-start | bytes 196616 | tf_op jit(solution)/shard_map/ppermute | solution.py:576
  30.9 5.0 %collective-permute-start.13 = (bf16[16,1024]{1,0:T(8,128)(2,1)S(1)}, bf16[16,1024]{1,0:T(8,128)(2,1)S(1)}, u32[]{:S(2)}, u32[]{:S(2)}) collective-permute-start(bf16[16,1024]{1,0:T(8,128)(2,1)S(1)} %get-tuple-element.46), channel_id=1, source_target_pairs={{0,12},{2,6},{1,15},{3,5},{4,0},{6,10},{5,3},{7,9},{8,4},{10,14},{... | collective-permute-start | bytes 98312 | tf_op jit(solution)/shard_map/ppermute | solution.py:587
  34.3 3.1 %collective-permute-start.12 = (bf16[32,1024]{1,0:T(8,128)(2,1)S(1)}, bf16[32,1024]{1,0:T(8,128)(2,1)S(1)}, u32[]{:S(2)}, u32[]{:S(2)}) collective-permute-start(bf16[32,1024]{1,0:T(8,128)(2,1)S(1)} %collective-permute-done.11.refs_0_), channel_id=1, source_target_pairs={{0,1},{1,0},{2,3},{3,2},{4,5},{5,4},{6,7},{7,6},{8,9},{9,8},{10,11... | collective-permute-start | bytes 196616 | tf_op jit(solution)/shard_map/ppermute | solution.py:577
  35.9 1.5 %collective-permute-start.14 = (bf16[16,1024]{1,0:T(8,128)(2,1)S(1)}, bf16[16,1024]{1,0:T(8,128)(2,1)S(1)}, u32[]{:S(2)}, u32[]{:S(2)}) collective-permute-start(bf16[16,1024]{1,0:T(8,128)(2,1)S(1)} %collective-permute-done.13.refs_2_), channel_id=1, source_target_pairs={{0,1},{1,0},{2,3},{3,2},{4,5},{5,4},{6,7},{7,6},{8,9},{9,8},{10,11... | collective-permute-start | bytes 98312 | tf_op jit(solution)/shard_map/ppermute | solution.py:589
